TPU v7x, 32 devices: a whole 2x2x4 slice. The times are simulated.
32 devices in a mesh: seq: 8 (over z, x), head: 4 (over y, core).
Axes of the slice: x: 2, y: 2, z: 4, core: 2. Of those that a mesh axis runs over, the one named last changes fastest.
Arguments:
- queries: bfloat16 [1024, 4096], P('seq', 'head'), may hold values from -6 to 6
- keys: bfloat16 [1024, 4096], P('seq', 'head'), may hold values from -6 to 6
- values: bfloat16 [1024, 4096], P('seq', 'head'), may hold values from -3 to 3
- decay_codes: int32 [1024, 32], P('seq', 'head'), may hold values from 0 to 2048
- out_weight: bfloat16 [4096, 3072], P('head'), may hold values from -0.09375 to 0.09375
- out_grad: bfloat16 [1024, 3072], P('seq', 'head'), may hold values from -6 to 6
Outputs:
- mixed: bfloat16 [1024, 3072], P('seq', 'head')
- query_gradient: bfloat16 [1024, 4096], P('seq', 'head')
- key_grad: bfloat16 [1024, 4096], P('seq', 'head')
- value_gradient: bfloat16 [1024, 4096], P('seq', 'head')
All inputs are finite; a program needn't handle non-finite values.
Results may differ from a plain program's by a relative error of at most 0.014.
Values may be sent and summed in bfloat16 or wider, within the bound.
No kernel may reach another device: no remote copies, remote signals or barrier semaphores. Data moves between devices by JAX's collectives and lax.ppermute only.
A program may use at most 128 MiB of HBM per device.

v0:
```python
import jax
import jax.numpy as jnp
from jax import lax
from jax.sharding import PartitionSpec as P


def prefix(value, axis, join, neutral):
    count, mine = (lax.axis_size(axis), lax.axis_index(axis))
    pieces = jax.tree.map(lambda part: lax.all_gather(part, axis), value)
    subtotal = jax.tree.map(
        lambda part, zero: jnp.full_like(part, 0) + jnp.asarray(zero, part.dtype), value, neutral
    )

    def prefix_step(position, subtotal):
        longer = join(subtotal, jax.tree.map(lambda part: part[position], pieces))
        return jax.tree.map(lambda new, old: jnp.where(position < mine, new, old), longer, subtotal)

    return lax.fori_loop(0, count - 1, prefix_step, subtotal)


def entering(array, axis, combine, identity):
    devices, place = (lax.axis_size(axis), lax.axis_index(axis))
    everything = jax.tree.map(
        lambda part, kind: lax.all_gather(part.astype(kind), axis),
        array,
        (jnp.bfloat16, jnp.bfloat16),
    )
    start = jax.tree.map(
        lambda part, zero: jnp.broadcast_to(jnp.asarray(zero, part.dtype), part.shape),
        array,
        identity,
    )

    def entering_step(k, before):
        at = devices - 1 - k
        reached = at > place
        new = combine(
            before, jax.tree.map(lambda part, own: part[at].astype(own.dtype), everything, array)
        )
        return jax.tree.map(lambda a, b: jnp.where(reached, a, b), new, before)

    return lax.fori_loop(0, devices, entering_step, start)


def block_mask(cum_log):
    block_len = cum_log.shape[0]
    log_gap = cum_log.T[:, :, None] - cum_log.T[:, None, :]
    lower_part = (jnp.arange(block_len)[:, None] >= jnp.arange(block_len)[None, :])[None]
    return jnp.where(lower_part, jnp.exp(jnp.where(lower_part, log_gap, 0.0)), 0.0)


def combine(earlier, later):
    return (earlier[0] * later[0], later[0][:, None, None] * earlier[1] + later[1])


def local(queries, keys, values, decay_codes, out_weight, out_grad):
    tok_rows = queries.shape[0]
    head_count = decay_codes.shape[1]
    head_width = queries.shape[1] // head_count
    att_scale = 1.0 / head_width
    grad_flat = lax.dot_general(
        lax.all_gather(out_grad, "head", axis=1, tiled=True),
        out_weight,
        (((1,), (1,)), ((), ())),
        preferred_element_type=jnp.float32,
    ).astype(jnp.bfloat16)

    def to_heads(array):
        return array.reshape(tok_rows, head_count, head_width)

    query_h = to_heads(queries)
    key_h = to_heads(keys)
    value_h = to_heads(values)
    grad_h = to_heads(grad_flat)
    cum_log = jnp.cumsum(jnp.log(1.0 - decay_codes.astype(jnp.float32) / 4096.0), axis=0)
    decay_mask = block_mask(cum_log)
    rise_decay = jnp.exp(cum_log)[:, :, None]
    fall_decay = jnp.exp(cum_log[-1][None, :] - cum_log)[:, :, None]
    total_decay = jnp.exp(cum_log[-1])
    k_fall = (fall_decay * key_h.astype(jnp.float32)).astype(jnp.bfloat16)
    summary_fwd = jnp.einsum("thd,the->hde", k_fall, value_h, preferred_element_type=jnp.float32)
    q_rise = (att_scale * rise_decay * query_h.astype(jnp.float32)).astype(jnp.bfloat16)
    summary_bwd = jnp.einsum("shd,she->hde", q_rise, grad_h, preferred_element_type=jnp.float32)
    identity = (
        jnp.ones((head_count,), jnp.float32),
        jnp.zeros((head_count, head_width, head_width), jnp.float32),
    )
    passed_fwd, state_in = prefix((total_decay, summary_fwd), "seq", combine, identity)
    passed_bwd, carry_in = entering((total_decay, summary_bwd), "seq", combine, identity)
    scores = jnp.einsum("she,the->hst", query_h, key_h, preferred_element_type=jnp.float32)
    attn = (att_scale * scores * decay_mask).astype(jnp.bfloat16)
    pscores = jnp.einsum("she,the->hst", grad_h, value_h, preferred_element_type=jnp.float32)
    pmat = (att_scale * pscores * decay_mask).astype(jnp.bfloat16)
    g_rise = (att_scale * rise_decay * grad_h.astype(jnp.float32)).astype(jnp.bfloat16)
    v_fall = (fall_decay * value_h.astype(jnp.float32)).astype(jnp.bfloat16)
    local_out = jnp.einsum("hst,the->she", attn, value_h, preferred_element_type=jnp.float32)
    local_qgrad = jnp.einsum("hst,thd->shd", pmat, key_h, preferred_element_type=jnp.float32)
    local_kgrad = jnp.einsum("hst,shd->thd", pmat, query_h, preferred_element_type=jnp.float32)
    local_vgrad = jnp.einsum("hst,she->the", attn, grad_h, preferred_element_type=jnp.float32)
    state_b = state_in.astype(jnp.bfloat16)
    carry_b = carry_in.astype(jnp.bfloat16)
    attn_out = local_out + jnp.einsum(
        "shd,hde->she", q_rise, state_b, preferred_element_type=jnp.float32
    )
    query_gradient = local_qgrad + jnp.einsum(
        "she,hde->shd", g_rise, state_b, preferred_element_type=jnp.float32
    )
    key_grad = local_kgrad + jnp.einsum(
        "the,hde->thd", v_fall, carry_b, preferred_element_type=jnp.float32
    )
    value_gradient = local_vgrad + jnp.einsum(
        "thd,hde->the", k_fall, carry_b, preferred_element_type=jnp.float32
    )
    attn_flat = attn_out.astype(jnp.bfloat16).reshape(tok_rows, -1)
    partial_out = jnp.dot(attn_flat, out_weight, preferred_element_type=jnp.float32)
    mixed = lax.psum_scatter(
        partial_out.astype(jnp.bfloat16), "head", scatter_dimension=1, tiled=True
    )
    flat_width = queries.shape[1]
    return (
        mixed,
        query_gradient.astype(jnp.bfloat16).reshape(tok_rows, flat_width),
        key_grad.astype(jnp.bfloat16).reshape(tok_rows, flat_width),
        value_gradient.astype(jnp.bfloat16).reshape(tok_rows, flat_width),
    )


def solution(mesh):
    placed = (
        P("seq", "head"),
        P("seq", "head"),
        P("seq", "head"),
        P("seq", "head"),
        P("head", None),
        P("seq", "head"),
    )
    return jax.shard_map(
        local,
        mesh=mesh,
        in_specs=placed,
        out_specs=(P("seq", "head"), P("seq", "head"), P("seq", "head"), P("seq", "head")),
        check_vma=False,
    )
```

profile of v0, /device:TPU:0, one launch (start us, length us, event | category | flops | bytes accessed | tf_op | source)
XLA Modules:
  0.0 168.2 jit_solution(11531859500850806780)
XLA Ops:
  8.3 2.2 %fusion.16 = f32[8,128,128]{2,1,0:T(8,128)} fusion(f32[128,8]{0,1:T(8,128)S(1)} %copy.70, bf16[128,1024]{1,0:T(8,128)(2,1)S(1)} %copy-done, bf16[128,1024]{1,0:T(8,128)(2,1)} %param.11), kind=kOutput, calls=%fused_computation.37 | convolution fusion | flops 33947648 | bytes 1052672 | tf_op jit(solution)/shard_map/thd,the->hde/dot_general | solution.py:81
  10.7 1.1 copy.97
  11.8 10.3 %all_gather.26 = bf16[128,3072]{1,0:T(8,128)(2,1)S(1)} all-gather(bf16[128,768]{1,0:T(8,128)(2,1)} %param.15), channel_id=1, replica_groups=mesh['seq'=8,'head'=4] {'head'}, dimensions={1}, use_global_device_ids=true | all-gather | bytes 983040 | tf_op jit(solution)/shard_map/all_gather | solution.py:62
  22.1 5.1 %convolution_convert_fusion.2 = bf16[128,1024]{1,0:T(8,128)(2,1)S(1)} fusion(bf16[128,3072]{1,0:T(8,128)(2,1)S(1)} %all_gather.26, bf16[1024,3072]{1,0:T(8,128)(2,1)} %param.14), kind=kOutput, calls=%fused_computation.24 | convolution fusion | flops 805437440 | bytes 7340032 | tf_op jit(solution)/shard_map/dot_general | solution.py:61
  27.4 1.0 convolution_convert_fusion.1
  28.6 1.1 fusion.7
  30.0 21.2 %all-gather.2 = f32[8,1,8]{2,1,0:T(1,128)S(1)} all-gather(f32[1,1,8]{2,1,0:T(1,128)S(1)} %get-tuple-element.302), channel_id=1, replica_groups=mesh['seq'=8,'head'=4] {'seq'}, dimensions={0}, use_global_device_ids=true | all-gather | bytes 288 | tf_op jit(solution)/shard_map/all_gather | solution.py:9
  51.4 17.2 %all-gather.3 = bf16[8,1,8]{2,1,0:T(2,128)(2,1)S(1)} all-gather(bf16[1,1,8]{2,1,0:T(2,128)(2,1)S(1)} %get-tuple-element.300), channel_id=1, replica_groups=mesh['seq'=8,'head'=4] {'seq'}, dimensions={0}, use_global_device_ids=true | all-gather | bytes 144 | tf_op jit(solution)/shard_map/all_gather | solution.py:24
  68.5 1.2 fusion.35
  69.7 16.6 %all-gather.7.cloned.1.call-done = f32[64,128,128]{2,1,0:T(8,128)} async-done(((f32[8,128,128]{2,1,0:T(8,128)}), f32[64,128,128]{2,1,0:T(8,128)}) %all-gather.7.cloned.1.call-update) | async-done | bytes 4194320 | tf_op jit(solution)/shard_map/all_gather | solution.py:9
  86.3 8.5 %while.30 = (s32[]{:T(128)}, f32[8,128,128]{2,1,0:T(8,128)S(1)}, s32[]{:T(128)}, f32[8,8]{1,0:T(8,128)S(1)}, f32[8,8,128,128]{3,2,1,0:T(8,128)}, /*index=5*/s32[]{:T(128)}, s32[]{:T(128)}) while((s32[]{:T(128)}, f32[8,128,128]{2,1,0:T(8,128)S(1)}, s32[]{:T(128)}, f32[8,8]{1,0:T(8,128)S(1)}, f32[8,8,128,128]{3,2,1,0:T(8,128)}, ...), condition=%wide.region_2.3_spmd.clone, body=%wide.region_1.2_spmd.clone.sunk | while | flops 524292 | bytes 1573073 | solution.py:18
  86.4 1.2 fusion.59
  87.6 1.2 fusion.59
  88.8 1.2 fusion.59
  90.0 1.2 fusion.59
  91.2 1.2 fusion.59
  92.4 1.2 fusion.59
  93.6 1.2 fusion.59
  95.1 1.3 fusion.12
  96.4 4.7 %convolution_convert_fusion = bf16[128,3072]{1,0:T(8,128)(2,1)} fusion(bf16[128,1024]{0,1:T(8,128)(2,1)S(1)} %bitcast.131, bf16[1024,3072]{1,0:T(8,128)(2,1)} %param.14), kind=kOutput, calls=%fused_computation.6 | convolution fusion | flops 805699584 | bytes 7340032 | tf_op jit(solution)/shard_map/dot_general | solution.py:115
  101.2 35.6 %all-gather.9.cloned.1.call-done = bf16[64,128,128]{2,1,0:T(8,128)(2,1)} async-done(((bf16[8,128,128]{2,1,0:T(8,128)(2,1)}), bf16[64,128,128]{2,1,0:T(8,128)(2,1)}) %all-gather.9.cloned.1.call-update) | async-done | bytes 2097168 | tf_op jit(solution)/shard_map/all_gather | solution.py:24
  136.7 9.1 %while.31 = (s32[]{:T(128)}, f32[8,128,128]{2,1,0:T(8,128)S(1)}, s32[]{:T(128)}, bf16[8,8]{1,0:T(8,128)(2,1)S(1)}, bf16[8,8,128,128]{3,2,1,0:T(8,128)(2,1)}, /*index=5*/s32[]{:T(128)}, s32[]{:T(128)}, s32[]{:T(128)}, s32[]{:T(128)}) while((s32[]{:T(128)}, f32[8,128,128]{2,1,0:T(8,128)S(1)}, s32[]{:T(128)}, ...), condition=%wide.region_5.6_spmd.clone, body=%wide.region_4.5_spmd.clone.sunk | while | flops 655376 | bytes 1310975 | solution.py:42
  136.7 1.1 fusion.60
  137.9 1.1 fusion.60
  139.0 1.1 fusion.60
  140.1 1.1 fusion.60
  141.3 1.1 fusion.60
  142.4 1.1 fusion.60
  143.6 1.1 fusion.60
  144.7 1.1 fusion.60
  146.2 0.9 copy.89
  149.8 11.9 %reduce-scatter.2.cloned.1.call-done = bf16[128,768]{1,0:T(8,128)(2,1)} async-done(((bf16[128,3072]{1,0:T(8,128)(2,1)}), bf16[128,768]{1,0:T(8,128)(2,1)}) %reduce-scatter.2.cloned.1.call-update) | async-done | bytes 196624 | tf_op jit(solution)/shard_map/reduce_scatter | solution.py:116
  (47 shorter events, 5.5 us)
Async XLA Ops:
  7.2 1.2 copy-start
  7.2 79.2 %all-gather.7.cloned.1.call-start = ((), (), s32[]{:S(2)}) async-start(), calls=%async_computation.2 | async-start | bytes 4718592 | tf_op jit(solution)/shard_map/all_gather | solution.py:9
  8.1 20.5 %copy-start.1 = (bf16[128,1024]{1,0:T(8,128)(2,1)S(1)}, bf16[128,1024]{1,0:T(8,128)(2,1)}, u32[]{:S(2)}) copy-start(bf16[128,1024]{1,0:T(8,128)(2,1)} %param.11) | copy-start | bytes 786436
  10.6 126.1 %all-gather.9.cloned.1.call-start = ((), (), s32[]{:S(2)}) async-start(), calls=%async_computation.3 | async-start | bytes 2359296 | tf_op jit(solution)/shard_map/all_gather | solution.py:24
  28.4 133.2 %reduce-scatter.2.cloned.1.call-start = ((), (), s32[]{:S(2)}) async-start(), calls=%async_computation.1 | async-start | bytes 983040 | tf_op jit(solution)/shard_map/reduce_scatter | solution.py:116
Sparse Core Ops, SparseCore 0:
  10.7 75.5 all-gather.6
  89.0 47.6 all-gather.8
  139.8 21.7 reduce-scatter.1
where the time goes:
time: 169 us; the launch traced here: 168 us
  waiting for transfers between devices  64.1 us (38%)
  blocking collectives  48.7 us (29%)
  matrix products  18.7 us (11%)
  other arithmetic  18 us (11%)
  between operations  13.9 us (8%)
  local copies, waits for them, and re-layouts  4.15 us (2%)
    all_gather x1, waiting for transfers between devices, entering(): lax.all_gather(part.astype(kind), axis)  35.6 us
    all_gather x1, blocking collectives, prefix(): pieces = jax.tree.map(lambda part: lax.all_gather(part, axis), value)  21.2 us
    all_gather x1, blocking collectives, entering(): lax.all_gather(part.astype(kind), axis)  17.2 us
    all_gather x1, waiting for transfers between devices, prefix(): pieces = jax.tree.map(lambda part: lax.all_gather(part, axis), value)  16.6 us
    reduce_scatter x1, waiting for transfers between devices, local(): lax.psum_scatter(partial_out.astype(jnp.bfloat16), 'head', scatter_dimens...  11.9 us
    all_gather x1, blocking collectives, local(): lax.all_gather(out_grad, 'head', axis=1, tiled=True)  10.3 us
    select_n x8, other arithmetic, entering_step(): return jax.tree.map(lambda a, b: jnp.where(reached, a, b), new, before)  8.77 us
    select_n x7, other arithmetic, prefix_step(): jnp.where(position < mine, new, old)  8.22 us
  transfers between devices with their start and end apart: 3, of which 3 were waited for; matrix products, arithmetic and copies ran while one was open for 22% of the time, Pallas kernels for 0%

commit v1 on v0

v1 whole, which is shorter than its diff:
```python
import functools

import jax
import jax.numpy as jnp
from jax import lax
from jax.experimental import pallas as pl
from jax.experimental.pallas import tpu as pltpu
from jax.sharding import PartitionSpec as P

F32 = jnp.float32
BF16 = jnp.bfloat16
VMEM = pl.BlockSpec(memory_space=pltpu.VMEM)
SMEM = pl.BlockSpec(memory_space=pltpu.SMEM)
HBM = pl.BlockSpec(memory_space=pl.ANY)


def dot(a, b, ca, cb):
    return lax.dot_general(a, b, (((ca,), (cb,)), ((), ())), preferred_element_type=F32)


def aligned(index, size):
    return pl.ds(pl.multiple_of(index * size, size), size)


def call(kernel, outs, specs, args, scratch=(), limit=16, flops=0, nbytes=0):
    return pl.pallas_call(
        kernel,
        out_shape=outs,
        in_specs=specs,
        out_specs=[VMEM] * len(outs),
        scratch_shapes=list(scratch),
        compiler_params=pltpu.CompilerParams(vmem_limit_bytes=limit << 20),
        cost_estimate=pl.CostEstimate(flops=flops, bytes_accessed=nbytes, transcendentals=0),
    )(*args)


def shape(dims, dtype):
    return jax.ShapeDtypeStruct(dims, dtype)


def running_log(codes, axis):
    total = jnp.log(1.0 - codes.astype(F32) / 4096.0)
    place = lax.broadcasted_iota(jnp.int32, total.shape, axis)
    step = 1
    while step < total.shape[axis]:
        total = total + jnp.where(place >= step, pltpu.roll(total, step, axis), 0.0)
        step *= 2
    return total


class Plan:
    def __init__(self, tok, heads, width, seq):
        self.tok, self.heads, self.width, self.seq = tok, heads, width, seq
        self.group = next(g for g in (4, 2, 1) if heads % g == 0 and seq % g == 0)
        self.groups = seq // self.group
        self.quarter = heads // self.group
        self.half_tail = 8 * pl.cdiv(self.quarter, 8)
        self.tail = 2 * self.half_tail
        self.body = self.quarter * width
        self.rows = self.body + self.tail


def tail_rows(plan, totals):
    place = lax.broadcasted_iota(jnp.int32, (plan.tail, plan.width), 0)
    rows = jnp.zeros((plan.tail, plan.width), F32)
    for i, total in enumerate(totals):
        high = total.astype(BF16).astype(F32)
        rows = jnp.where(place == i, high, rows)
        rows = jnp.where(place == plan.half_tail + i, total - high, rows)
    return rows


def read_tail(plan, ref, base, i):
    at = base + plan.body + i
    return ref[at : at + 1, :] + ref[at + plan.half_tail : at + plan.half_tail + 1, :]


def put_summaries(plan, rank, left, right, cum, outs, scratch):
    width = plan.width
    last = jnp.exp(cum[plan.tok - 1 : plan.tok, :])
    for q in range(plan.group):
        base = q * plan.rows
        totals = []
        for i in range(plan.quarter):
            h = q * plan.quarter + i
            scratch[base + i * width : base + (i + 1) * width, :] = dot(left(h), right(h), 0, 0)
            totals.append(jnp.broadcast_to(last[:, h : h + 1], (1, width)))
        scratch[base + plan.body : base + plan.rows, :] = tail_rows(plan, totals)
    outs[0][...] = scratch[aligned(rank, plan.rows), :]
    for j in range(1, plan.group):
        outs[j][...] = scratch[aligned(rank ^ j, plan.rows), :].astype(BF16)


def summary_shapes(plan):
    rows = (plan.rows, plan.width)
    return [shape(rows, F32)] + [shape(rows, BF16)] * (plan.group - 1)


def summary_scratch(plan):
    return pltpu.VMEM((plan.group * plan.rows, plan.width), F32)


def forward_summary_kernel(plan, rank_ref, codes_ref, k_ref, v_ref, *rest):
    outs, scratch = rest[: plan.group], rest[plan.group]
    cum = running_log(codes_ref[...], 0)
    fall = jnp.exp(cum[plan.tok - 1 : plan.tok, :] - cum)

    def cols(h):
        return slice(h * plan.width, (h + 1) * plan.width)

    def left(h):
        return (fall[:, h : h + 1] * k_ref[:, cols(h)].astype(F32)).astype(BF16)

    put_summaries(plan, rank_ref[0], left, lambda h: v_ref[:, cols(h)], cum, outs, scratch)


def combine_kernel(plan, rank_ref, *rest):
    group, width = plan.group, plan.width
    ins, (pre_ref, total_ref, scratch) = rest[:group], rest[group:]
    rank = rank_ref[0]
    for j in range(group):
        scratch[aligned(rank ^ j, plan.rows), :] = ins[j][...].astype(F32)
    decays = []
    for i in range(plan.quarter):
        held = jnp.zeros((width, width), F32)
        decay = jnp.ones((1, width), F32)
        per_member = []
        for m in range(group):
            base = m * plan.rows
            at = slice(base + i * width, base + (i + 1) * width)
            pre_ref[at, :] = held
            per_member.append(decay)
            total = read_tail(plan, scratch, base, i)
            held = total * held + scratch[at, :]
            decay = decay * total
        decays.append(per_member + [decay])
        total_ref[i * width : (i + 1) * width, :] = held.astype(BF16)
    for m in range(group):
        base = m * plan.rows + plan.body
        pre_ref[base : base + plan.tail, :] = tail_rows(plan, [d[m] for d in decays])
    total_ref[plan.body : plan.rows, :] = tail_rows(plan, [d[group] for d in decays]).astype(BF16)


def spread_kernel(plan, rank_ref, enters_ref, entry_ref, pre_ref, *rest):
    group, width = plan.group, plan.width
    outs, scratch = rest[:group], rest[group]
    rank = rank_ref[0]
    enters = enters_ref[0] > 0
    for i in range(plan.quarter):
        at = slice(i * width, (i + 1) * width)
        entry = jnp.where(enters, entry_ref[at, :].astype(F32), 0.0)
        for m in range(group):
            base = m * plan.rows
            state = read_tail(plan, pre_ref, base, i) * entry
            state = state + pre_ref[base + i * width : base + (i + 1) * width, :]
            to = m * plan.body + i * width
            scratch[to : to + width, :] = state.astype(BF16)
    for j in range(group):
        outs[j][...] = scratch[aligned(rank ^ j, plan.body), :]


def swap(value, axis, offset):
    count = lax.axis_size(axis)
    return lax.ppermute(value, axis, [(i, i ^ offset) for i in range(count)])


def join(plan, earlier, later):
    earlier, later = earlier.astype(F32), later.astype(F32)
    bodies, totals = [], []
    for i in range(plan.quarter):
        at = slice(i * plan.width, (i + 1) * plan.width)
        mine = read_tail(plan, later, 0, i)
        bodies.append(mine * earlier[at] + later[at])
        totals.append(mine * read_tail(plan, earlier, 0, i))
    return jnp.concatenate(bodies + [tail_rows(plan, totals)]).astype(BF16)


def group_entry(plan, total, way, turn):
    count, span = plan.seq, plan.group

    def shift(value, by):
        hop = way * by * span
        return lax.ppermute(value, "seq", [(i, (i + hop) % count) for i in range(count)])

    entry = shift(total, 1)
    by = 1
    while by < plan.groups - 1:
        entry = jnp.where(turn > by, join(plan, shift(entry, by), entry), entry)
        by *= 2
    return entry


def scan_states(plan, summaries, way):
    place = lax.axis_index("seq")
    turn = place if way > 0 else plan.seq - 1 - place
    rank = (turn % plan.group).reshape(1)
    turn = turn // plan.group
    got = [summaries[0]] + [swap(summaries[j], "seq", j) for j in range(1, plan.group)]
    rows, body = (plan.rows, plan.width), (plan.body, plan.width)
    pre, total = call(
        functools.partial(combine_kernel, plan),
        [shape((plan.group * plan.rows, plan.width), F32), shape(rows, BF16)],
        [SMEM] + [VMEM] * plan.group,
        [rank] + got,
        [pltpu.VMEM((plan.group * plan.rows, plan.width), F32)],
    )
    entry = group_entry(plan, total, way, turn)
    states = call(
        functools.partial(spread_kernel, plan),
        [shape(body, BF16)] * plan.group,
        [SMEM, SMEM, VMEM, VMEM],
        [rank, (turn > 0).astype(jnp.int32).reshape(1), entry, pre],
        [pltpu.VMEM((plan.group * plan.body, plan.width), BF16)],
    )
    return [states[0]] + [swap(states[j], "seq", j) for j in range(1, plan.group)]


def gather_states(plan, rank, ins, scratch):
    for j in range(plan.group):
        scratch[aligned(rank ^ j, plan.body), :] = ins[j][...]


def mask_of(plan, cum, cum_t, h):
    size = (plan.tok, plan.tok)
    lower = lax.broadcasted_iota(jnp.int32, size, 0) >= lax.broadcasted_iota(jnp.int32, size, 1)
    gap = cum[:, h : h + 1] - cum_t[h : h + 1, :]
    return jnp.where(lower, jnp.exp(jnp.where(lower, gap, 0.0)), 0.0)


def forward_local_kernel(plan, codes_ref, codes_t_ref, q_ref, k_ref, v_ref, attn_ref, out_ref, rise_ref):
    scale = 1.0 / plan.width
    cum, cum_t = running_log(codes_ref[...], 0), running_log(codes_t_ref[...], 1)
    rise = scale * jnp.exp(cum)
    for h in range(plan.heads):
        at = slice(h * plan.width, (h + 1) * plan.width)
        rows = slice(h * plan.tok, (h + 1) * plan.tok)
        q = q_ref[:, at]
        scores = dot(q, k_ref[:, at], 1, 1)
        attn = (scale * scores * mask_of(plan, cum, cum_t, h)).astype(BF16)
        attn_ref[rows, :] = attn
        out_ref[:, at] = dot(attn, v_ref[:, at], 1, 0)
        rise_ref[:, at] = (rise[:, h : h + 1] * q.astype(F32)).astype(BF16)


def weight_copies(index_ref, weight_ref, buffers, sems, count, width):
    copies = []
    for s in range(count):
        at = pl.ds(pl.multiple_of(index_ref[s] * width, 128), width)
        copies.append(pltpu.make_async_copy(weight_ref.at[:, at], buffers.at[s], sems.at[s]))
        copies[-1].start()
    return copies


def grad_kernel(plan, count, last, rank_ref, index_ref, weight_ref, *rest):
    shards, rest = rest[:count], rest[count:]
    if last:
        before_ref, codes_ref, q_ref, grad_ref = rest[:4]
        outs = rest[4 : 4 + plan.group]
        scratch, buffers, sems = rest[4 + plan.group :]
    else:
        (sum_ref, buffers, sems), before_ref = rest, None
    width = shards[0].shape[1]
    copies = weight_copies(index_ref, weight_ref, buffers, sems, count, width)
    total = None if before_ref is None else before_ref[...]
    for s in range(count):
        copies[s].wait()
        part = dot(shards[s][...], buffers[s], 1, 1)
        total = part if total is None else total + part
    if not last:
        sum_ref[...] = total
        return
    grad_ref[...] = total.astype(BF16)
    cum = running_log(codes_ref[...], 0)
    rise = (1.0 / plan.width) * jnp.exp(cum)

    def cols(h):
        return slice(h * plan.width, (h + 1) * plan.width)

    def left(h):
        return (rise[:, h : h + 1] * q_ref[:, cols(h)].astype(F32)).astype(BF16)

    put_summaries(plan, rank_ref[0], left, lambda h: grad_ref[:, cols(h)], cum, outs, scratch)


def backward_local_kernel(
    plan, codes_ref, codes_t_ref, q_ref, k_ref, v_ref, grad_ref, attn_ref, lq_ref, lk_ref, lv_ref
):
    scale = 1.0 / plan.width
    cum, cum_t = running_log(codes_ref[...], 0), running_log(codes_t_ref[...], 1)
    for h in range(plan.heads):
        at = slice(h * plan.width, (h + 1) * plan.width)
        rows = slice(h * plan.tok, (h + 1) * plan.tok)
        grad = grad_ref[:, at]
        scores = dot(grad, v_ref[:, at], 1, 1)
        pmat = (scale * scores * mask_of(plan, cum, cum_t, h)).astype(BF16)
        lq_ref[:, at] = dot(pmat, k_ref[:, at], 1, 0)
        lk_ref[:, at] = dot(pmat, q_ref[:, at], 0, 0)
        lv_ref[:, at] = dot(attn_ref[rows, :], grad, 0, 0)


def mix_first_kernel(plan, count, rank_ref, index_ref, weight_ref, local_ref, rise_ref, *rest):
    ins, rest = rest[: plan.group], rest[plan.group :]
    flat_ref, outs = rest[0], rest[1 : 1 + count]
    states, buffers, sems = rest[1 + count :]
    copies = weight_copies(index_ref, weight_ref, buffers, sems, count, outs[0].shape[1])
    gather_states(plan, rank_ref[0], ins, states)
    for h in range(plan.heads):
        at = slice(h * plan.width, (h + 1) * plan.width)
        cross = dot(rise_ref[:, at], states[at, :], 1, 0)
        flat_ref[:, at] = (local_ref[:, at] + cross).astype(BF16)
    for s in range(count):
        copies[s].wait()
        outs[s][...] = dot(flat_ref[...], buffers[s], 1, 0).astype(outs[s].dtype)


def mix_second_kernel(plan, count, index_ref, weight_ref, flat_ref, *rest):
    outs, (buffers, sems) = rest[:count], rest[count:]
    copies = weight_copies(index_ref, weight_ref, buffers, sems, count, outs[0].shape[1])
    for s in range(count):
        copies[s].wait()
        outs[s][...] = dot(flat_ref[...], buffers[s], 1, 0).astype(outs[s].dtype)


def query_grad_kernel(plan, rank_ref, codes_ref, local_ref, grad_ref, *rest):
    ins, (out_ref, states) = rest[: plan.group], rest[plan.group :]
    gather_states(plan, rank_ref[0], ins, states)
    rise = (1.0 / plan.width) * jnp.exp(running_log(codes_ref[...], 0))
    for h in range(plan.heads):
        at = slice(h * plan.width, (h + 1) * plan.width)
        g_rise = (rise[:, h : h + 1] * grad_ref[:, at].astype(F32)).astype(BF16)
        out_ref[:, at] = (local_ref[:, at] + dot(g_rise, states[at, :], 1, 1)).astype(BF16)


def key_value_grad_kernel(plan, rank_ref, codes_ref, k_ref, v_ref, lk_ref, lv_ref, *rest):
    ins, (kg_ref, vg_ref, states) = rest[: plan.group], rest[plan.group :]
    gather_states(plan, rank_ref[0], ins, states)
    cum = running_log(codes_ref[...], 0)
    fall = jnp.exp(cum[plan.tok - 1 : plan.tok, :] - cum)
    for h in range(plan.heads):
        at = slice(h * plan.width, (h + 1) * plan.width)
        carry = states[at, :]
        v_fall = (fall[:, h : h + 1] * v_ref[:, at].astype(F32)).astype(BF16)
        k_fall = (fall[:, h : h + 1] * k_ref[:, at].astype(F32)).astype(BF16)
        kg_ref[:, at] = (lk_ref[:, at] + dot(v_fall, carry, 1, 1)).astype(BF16)
        vg_ref[:, at] = (lv_ref[:, at] + dot(k_fall, carry, 1, 0)).astype(BF16)


def local(queries, keys, values, decay_codes, out_weight, out_grad):
    tok, flat = queries.shape
    heads = decay_codes.shape[1]
    plan = Plan(tok, heads, flat // heads, lax.axis_size("seq"))
    across, feat = lax.axis_size("head"), out_grad.shape[1]
    place, mine = lax.axis_index("seq"), lax.axis_index("head")
    rank = (place % plan.group).reshape(1)
    rank_back = ((plan.seq - 1 - place) % plan.group).reshape(1)
    codes_t = decay_codes.T
    deep = out_weight.shape[0]

    def order(offsets):
        return jnp.stack([mine ^ o for o in offsets]).astype(jnp.int32)

    def buffers(count):
        return [pltpu.VMEM((count, deep, feat), BF16), pltpu.SemaphoreType.DMA((count,))]

    shards = {0: out_grad}
    hop = across // 2
    while hop:
        shards.update({o ^ hop: swap(part, "head", hop) for o, part in list(shards.items())})
        hop //= 2
    half = across // 2

    summaries = call(
        functools.partial(forward_summary_kernel, plan),
        summary_shapes(plan),
        [SMEM, VMEM, VMEM, VMEM],
        [rank, decay_codes, keys, values],
        [summary_scratch(plan)],
        flops=2 * tok * flat * plan.width,
        nbytes=4 * tok * flat,
    )
    states = scan_states(plan, summaries, 1)

    wide = (tok, flat)
    near, far = list(range(half)), list(range(half, across))
    (part,) = call(
        functools.partial(grad_kernel, plan, half, False),
        [shape(wide, F32)],
        [SMEM, SMEM, HBM] + [VMEM] * half,
        [rank, order(near), out_weight] + [shards[o] for o in near],
        buffers(half),
        flops=2 * tok * flat * feat * half,
        nbytes=2 * flat * feat * half,
    )
    grad, *summaries_back = call(
        functools.partial(grad_kernel, plan, half, True),
        [shape(wide, BF16)] + summary_shapes(plan),
        [SMEM, SMEM, HBM] + [VMEM] * (half + 3),
        [rank_back, order(far), out_weight] + [shards[o] for o in far] + [part, decay_codes, queries],
        [summary_scratch(plan)] + buffers(half),
        flops=2 * tok * flat * feat * half,
        nbytes=2 * flat * feat * half,
    )
    carries = scan_states(plan, summaries_back, -1)

    attn, local_out, q_rise = call(
        functools.partial(forward_local_kernel, plan),
        [shape((heads * tok, tok), BF16), shape(wide, F32), shape(wide, BF16)],
        [VMEM] * 5,
        [decay_codes, codes_t, queries, keys, values],
        flops=4 * tok * flat * plan.width,
        nbytes=14 * tok * flat,
    )
    local_q, local_k, local_v = call(
        functools.partial(backward_local_kernel, plan),
        [shape(wide, F32)] * 3,
        [VMEM] * 7,
        [decay_codes, codes_t, queries, keys, values, grad, attn],
        flops=8 * tok * flat * plan.width,
        nbytes=22 * tok * flat,
    )

    held = pltpu.VMEM((flat, plan.width), BF16)
    far = far[::-1]
    attn_out, *sent = call(
        functools.partial(mix_first_kernel, plan, half),
        [shape(wide, BF16)] + [shape((tok, feat), BF16)] * half,
        [SMEM, SMEM, HBM, VMEM, VMEM] + [VMEM] * plan.group,
        [rank, order(far), out_weight, local_out, q_rise] + states,
        [held] + buffers(half),
        flops=2 * tok * flat * feat * half,
        nbytes=2 * flat * feat * half,
    )
    near = near[::-1]
    kept = call(
        functools.partial(mix_second_kernel, plan, half),
        [shape((tok, feat), F32 if o == 0 else BF16) for o in near],
        [SMEM, HBM, VMEM],
        [order(near), out_weight, attn_out],
        buffers(half),
        flops=2 * tok * flat * feat * half,
        nbytes=2 * flat * feat * half,
    )

    def halve(parts, hop):
        moved = {o: swap(part, "head", hop) for o, part in parts.items() if o & hop}
        return {
            o: (part.astype(F32) + moved[o | hop].astype(F32)).astype(F32 if o == 0 else BF16)
            for o, part in parts.items()
            if not o & hop
        }

    far_parts, near_parts = dict(zip(far, sent)), dict(zip(near, kept))
    hop = 1
    while hop < half:
        far_parts, near_parts = halve(far_parts, hop), halve(near_parts, hop)
        hop *= 2
    mixed = halve({**far_parts, **near_parts}, half)[0].astype(BF16)

    (query_grad,) = call(
        functools.partial(query_grad_kernel, plan),
        [shape(wide, BF16)],
        [SMEM] + [VMEM] * (3 + plan.group),
        [rank, decay_codes, local_q, grad] + states,
        [held],
        flops=2 * tok * flat * plan.width,
        nbytes=10 * tok * flat,
    )
    key_grad, value_grad = call(
        functools.partial(key_value_grad_kernel, plan),
        [shape(wide, BF16)] * 2,
        [SMEM] + [VMEM] * (5 + plan.group),
        [rank_back, decay_codes, keys, values, local_k, local_v] + carries,
        [held],
        flops=4 * tok * flat * plan.width,
        nbytes=18 * tok * flat,
    )
    return mixed, query_grad, key_grad, value_grad


def solution(mesh):
    whole = P("seq", "head")
    return jax.shard_map(
        local,
        mesh=mesh,
        in_specs=(whole, whole, whole, whole, P("head", None), whole),
        out_specs=(whole,) * 4,
        check_vma=False,
    )
```

time: 169 us -> 69.5 us (0.41)
  waiting for transfers between devices: 64.1 us -> 15.1 us
  blocking collectives: 48.7 us -> 0 us
  starting transfers between devices: 0.12 us -> 24.3 us
  matrix products: 18.7 us -> 0 us
  other arithmetic: 18 us -> 1.11 us
  Pallas kernels: 0 us -> 15.9 us
  between operations: 13.9 us -> 0.84 us
  local copies, waits for them, and re-layouts: 4.15 us -> 11.9 us
    all_gather x2 -> x0, waiting for transfers between devices: 52.2 us -> none  [the longest x1 35.6 us: entering(): lax.all_gather(part.astype(kind), axis)]
    all_gather x3 -> x0, blocking collectives: 48.7 us -> none  [the longest x1 21.2 us: prefix(): pieces = jax.tree.map(lambda part: lax.all_gather(part, axis), value)]
    ppermute x0 -> x20, starting transfers between devices: none -> 24.3 us  [the longest x18 18.4 us: swap(): return lax.ppermute(value, axis, [(i, i ^ offset) for i in range(count)])]
    dot_general x14 -> x0, matrix products: 18.7 us -> none  [the longest x1 5.05 us: local(): lax.dot_general(lax.all_gather(out_grad, 'head', axis=1, tiled=True), out...]
    select_n x15 -> x0, other arithmetic: 17 us -> none  [the longest x8 8.77 us: entering_step(): return jax.tree.map(lambda a, b: jnp.where(reached, a, b), new, before)]
    pallas_call x0 -> x13, Pallas kernels: none -> 15.9 us  [call(): pl.pallas_call(kernel, out_shape=outs, in_specs=specs, out_specs=[VMEM] *...]
    ppermute x0 -> x20, waiting for transfers between devices: none -> 15.1 us  [the longest x18 10.7 us: swap(): return lax.ppermute(value, axis, [(i, i ^ offset) for i in range(count)])]
    reduce_scatter x1 -> x0, waiting for transfers between devices: 11.9 us -> none  [local(): lax.psum_scatter(partial_out.astype(jnp.bfloat16), 'head', scatter_dimens...]
  transfers between devices with their start and end apart: 3 -> 20, of which waited for: 3 -> 10; matrix products, arithmetic and copies ran while one was open for 22% -> 2% of each run, Pallas kernels for 0% -> 20%
where the time goes in v1:
time: 69.5 us; the launch traced here: 69.1 us
  starting transfers between devices  24.3 us (35%)
  Pallas kernels  15.9 us (23%)
  waiting for transfers between devices  15.1 us (22%)
  local copies, waits for them, and re-layouts  11.9 us (17%)
  other arithmetic  1.11 us (2%)
  between operations  0.84 us (1%)
    ppermute x18, starting transfers between devices, swap(): return lax.ppermute(value, axis, [(i, i ^ offset) for i in range(count)])  18.4 us
    pallas_call x13, Pallas kernels, call(): pl.pallas_call(kernel, out_shape=outs, in_specs=specs, out_specs=[VMEM] *...  15.9 us
    unnamed x29, local copies, waits for them, and re-layouts  11.9 us
    ppermute x18, waiting for transfers between devices, swap(): return lax.ppermute(value, axis, [(i, i ^ offset) for i in range(count)])  10.7 us
    ppermute x2, starting transfers between devices, shift(): lax.ppermute(value, 'seq', [(i, (i + hop) % count) for i in range(count)])  5.85 us
    ppermute x2, waiting for transfers between devices, shift(): lax.ppermute(value, 'seq', [(i, (i + hop) % count) for i in range(count)])  4.32 us
  transfers between devices with their start and end apart: 20, of which 10 were waited for; matrix products, arithmetic and copies ran while one was open for 2% of the time, Pallas kernels for 20%

profile of v1, /device:TPU:0, one launch (start us, length us, event | category | flops | bytes accessed | tf_op | source)
XLA Modules:
  0.0 69.1 jit_solution(5366653688265163161)
XLA Ops:
  1.4 0.9 %copy-done.3 = bf16[128,1024]{1,0:T(8,128)(2,1)S(1)} copy-done((bf16[128,1024]{1,0:T(8,128)(2,1)S(1)}, bf16[128,1024]{1,0:T(8,128)(2,1)}, u32[]{:S(2)}) %copy-start.3) | copy-done | bytes 262168
  2.4 0.9 %copy-done.6 = bf16[128,1024]{1,0:T(8,128)(2,1)S(1)} copy-done((bf16[128,1024]{1,0:T(8,128)(2,1)S(1)}, bf16[128,1024]{1,0:T(8,128)(2,1)}, u32[]{:S(2)}) %copy-start.6) | copy-done | bytes 262168
  3.9 3.0 %collective-permute-start = (bf16[272,128]{1,0:T(8,128)(2,1)S(1)}, bf16[272,128]{1,0:T(8,128)(2,1)S(1)}, u32[]{:S(2)}, u32[]{:S(2)}) collective-permute-start(bf16[272,128]{1,0:T(8,128)(2,1)S(1)} %get-tuple-element.41), channel_id=1, source_target_pairs={{0,4},{4,0},{8,12},{12,8},{16,20},{20,16},{24,28},{28,24},{1,5},{5... | collective-permute-start | bytes 208904 | tf_op jit(solution)/shard_map/ppermute | solution.py:164
  7.0 1.6 %collective-permute-start.1 = (bf16[272,128]{1,0:T(8,128)(2,1)S(1)}, bf16[272,128]{1,0:T(8,128)(2,1)S(1)}, u32[]{:S(2)}, u32[]{:S(2)}) collective-permute-start(bf16[272,128]{1,0:T(8,128)(2,1)S(1)} %get-tuple-element.42), channel_id=1, source_target_pairs={{0,8},{4,12},{8,0},{12,4},{16,24},{20,28},{24,16},{28,20},{1,9},{5... | collective-permute-start | bytes 208904 | tf_op jit(solution)/shard_map/ppermute | solution.py:164
  8.5 1.9 %collective-permute-start.10 = (bf16[128,768]{1,0:T(8,128)(2,1)}, bf16[128,768]{1,0:T(8,128)(2,1)S(1)}, u32[]{:S(2)}, u32[]{:S(2)}) collective-permute-start(bf16[128,768]{1,0:T(8,128)(2,1)} %rest_0_.1), channel_id=1, source_target_pairs={{0,2},{1,3},{2,0},{3,1},{4,6},{5,7},{6,4},{7,5},{8,10},{9,11},{10,... | collective-permute-start | bytes 589832 | tf_op jit(solution)/shard_map/ppermute | solution.py:164
  10.5 0.9 %copy-done.4 = bf16[128,1024]{1,0:T(8,128)(2,1)S(1)} copy-done((bf16[128,1024]{1,0:T(8,128)(2,1)S(1)}, bf16[128,1024]{1,0:T(8,128)(2,1)}, u32[]{:S(2)}) %copy-start.4) | copy-done | bytes 262168
  11.4 0.9 %copy-done.7 = bf16[128,1024]{1,0:T(8,128)(2,1)S(1)} copy-done((bf16[128,1024]{1,0:T(8,128)(2,1)S(1)}, bf16[128,1024]{1,0:T(8,128)(2,1)}, u32[]{:S(2)}) %copy-start.7) | copy-done | bytes 262168
  12.4 0.9 %copy-done.9 = bf16[128,1024]{1,0:T(8,128)(2,1)S(1)} copy-done((bf16[128,1024]{1,0:T(8,128)(2,1)S(1)}, bf16[128,1024]{1,0:T(8,128)(2,1)}, u32[]{:S(2)}) %copy-start.9) | copy-done | bytes 262168
  14.0 1.7 %shard_map.93 = (bf16[1024,128]{1,0:T(8,128)(2,1)S(1)}, f32[128,1024]{1,0:T(8,128)S(1)}, bf16[128,1024]{1,0:T(8,128)(2,1)S(1)}) custom-call(s32[128,8]{1,0:T(8,128)S(1)} %copy.10.codes_ref.rest_3_, s32[8,128]{1,0:T(8,128)S(1)} %bitcast.9, bf16[128,1024]{1,0:T(8,128)(2,1)S(1)} %copy-done.9, bf16[128,1024]{1,0:T(8,128)(2,1)S(1)} %copy-done.4, ...), custom_call_target="tpu_custom_call" | custom-call | flops 67108864 | bytes 1835008 | tf_op jit(solution)/shard_map/pallas_call | solution.py:26
  15.9 2.7 %collective-permute-start.3 = (bf16[272,128]{1,0:T(8,128)(2,1)S(1)}, bf16[272,128]{1,0:T(8,128)(2,1)S(1)}, u32[]{:S(2)}, u32[]{:S(2)}) collective-permute-start(bf16[272,128]{1,0:T(8,128)(2,1)S(1)} %get-tuple-element.44), channel_id=1, source_target_pairs={{0,16},{4,20},{8,24},{12,28},{16,0},{20,4},{24,8},{28,12},{1,17},{... | collective-permute-start | bytes 208904 | tf_op jit(solution)/shard_map/ppermute | solution.py:183
  18.6 4.3 %collective-permute-done.3.entry_ref = bf16[272,128]{1,0:T(8,128)(2,1)S(1)} collective-permute-done((bf16[272,128]{1,0:T(8,128)(2,1)S(1)}, bf16[272,128]{1,0:T(8,128)(2,1)S(1)}, u32[]{:S(2)}, u32[]{:S(2)}) %collective-permute-start.3) | collective-permute-done | bytes 69664 | tf_op jit(solution)/shard_map/ppermute | solution.py:183
  23.0 1.6 %collective-permute-start.4 = (bf16[256,128]{1,0:T(8,128)(2,1)S(1)}, bf16[256,128]{1,0:T(8,128)(2,1)S(1)}, u32[]{:S(2)}, u32[]{:S(2)}) collective-permute-start(bf16[256,128]{1,0:T(8,128)(2,1)S(1)} %get-tuple-element.47), channel_id=1, source_target_pairs={{0,4},{4,0},{8,12},{12,8},{16,20},{20,16},{24,28},{28,24},{1,5},{5... | collective-permute-start | bytes 196616 | tf_op jit(solution)/shard_map/ppermute | solution.py:164
  25.3 1.3 %collective-permute-start.6 = (bf16[256,128]{1,0:T(8,128)(2,1)S(1)}, bf16[256,128]{1,0:T(8,128)(2,1)S(1)}, u32[]{:S(2)}, u32[]{:S(2)}) collective-permute-start(bf16[256,128]{1,0:T(8,128)(2,1)S(1)} %get-tuple-element.49), channel_id=1, source_target_pairs={{0,12},{4,8},{8,4},{12,0},{16,28},{20,24},{24,20},{28,16},{1,13},{... | collective-permute-start | bytes 196616 | tf_op jit(solution)/shard_map/ppermute | solution.py:164
  27.4 1.5 %collective-permute-done.5.rest_2_ = bf16[256,128]{1,0:T(8,128)(2,1)S(1)} collective-permute-done((bf16[256,128]{1,0:T(8,128)(2,1)S(1)}, bf16[256,128]{1,0:T(8,128)(2,1)S(1)}, u32[]{:S(2)}, u32[]{:S(2)}) %collective-permute-start.5) | collective-permute-done | bytes 65568 | tf_op jit(solution)/shard_map/ppermute | solution.py:164
  28.8 1.6 %collective-permute-done.6.rest_3_ = bf16[256,128]{1,0:T(8,128)(2,1)S(1)} collective-permute-done((bf16[256,128]{1,0:T(8,128)(2,1)S(1)}, bf16[256,128]{1,0:T(8,128)(2,1)S(1)}, u32[]{:S(2)}, u32[]{:S(2)}) %collective-permute-start.6) | collective-permute-done | bytes 65568 | tf_op jit(solution)/shard_map/ppermute | solution.py:164
  30.4 2.8 %copy-done = bf16[1024,3072]{1,0:T(8,128)(2,1)S(1)} copy-done((bf16[1024,3072]{1,0:T(8,128)(2,1)S(1)}, bf16[1024,3072]{1,0:T(8,128)(2,1)}, u32[]{:S(2)}) %copy-start) | copy-done | bytes 6291480
  33.2 2.1 %shard_map.97 = (bf16[128,1024]{1,0:T(8,128)(2,1)S(1)}, bf16[128,768]{1,0:T(8,128)(2,1)S(1)}, bf16[128,768]{1,0:T(8,128)(2,1)S(1)}) custom-call(s32[1]{0:T(128)} %bitcast.2.rank_ref, s32[2]{0:T(128)S(1)} %pad_add_fusion.1.index_ref, bf16[1024,3072]{1,0:T(8,128)(2,1)S(1)} %copy-done, f32[128,1024]{1,0:T(8,128)S(1)} %get-tuple-element.38.local_ref, ...), custom_call_target="tpu_custom_call" | custom-call | flops 402653184 | bytes 3145728 | tf_op jit(solution)/shard_map/pallas_call | solution.py:26
  36.1 2.8 %copy-done.1 = bf16[1024,3072]{1,0:T(8,128)(2,1)S(1)} copy-done((bf16[1024,3072]{1,0:T(8,128)(2,1)S(1)}, bf16[1024,3072]{1,0:T(8,128)(2,1)}, u32[]{:S(2)}) %copy-start.1) | copy-done | bytes 6291480
  38.9 1.9 %shard_map.98 = (bf16[128,768]{1,0:T(8,128)(2,1)S(1)}, f32[128,768]{1,0:T(8,128)S(1)}) custom-call(s32[2]{0:T(128)S(1)} %pad_add_fusion.index_ref, bf16[1024,3072]{1,0:T(8,128)(2,1)S(1)} %copy-done.1, bf16[128,1024]{1,0:T(8,128)(2,1)S(1)} %get-tuple-element.50.flat_ref), custom_call_target="tpu_custom_call" | custom-call | flops 402653184 | bytes 3145728 | tf_op jit(solution)/shard_map/pallas_call | solution.py:26
  41.7 2.2 %shard_map.99.rest_2_ = f32[128,1024]{1,0:T(8,128)S(1)} custom-call(s32[1]{0:T(128)} %bitcast.2.rank_ref, s32[2]{0:T(128)S(1)} %pad_add_fusion.3.index_ref, bf16[1024,3072]{1,0:T(8,128)(2,1)S(1)} %copy-done.2, bf16[128,768]{1,0:T(8,128)(2,1)S(1)} %copy-done.11, bf16[128,768]{1,0:T(8,128)(2,1)S(1)} %collective-permute-done.12.rest_1_), custom_call_target="tpu_custom_call" | custom-call | flops 402653184 | bytes 3145728 | tf_op jit(solution)/shard_map/pallas_call | solution.py:26
  43.9 2.4 %shard_map.100 = (bf16[128,1024]{1,0:T(8,128)(2,1)S(1)}, f32[272,128]{1,0:T(8,128)S(1)}, bf16[272,128]{1,0:T(8,128)(2,1)S(1)}, bf16[272,128]{1,0:T(8,128)(2,1)S(1)}, bf16[272,128]{1,0:T(8,128)(2,1)S(1)}) custom-call(s32[1]{0:T(128)} %bitcast.7.rank_ref, s32[2]{0:T(128)S(1)} %pad_add_fusion.2.index_ref, bf16[1024,3072]{1,0:T(8,128)(2,1)S(1)} %copy-done.2, ...), custom_call_target="tpu_custom_call" | custom-call | flops 402653184 | bytes 3145728 | tf_op jit(solution)/shard_map/pallas_call | solution.py:26
  47.0 1.3 %collective-permute-start.14 = (bf16[272,128]{1,0:T(8,128)(2,1)S(1)}, bf16[272,128]{1,0:T(8,128)(2,1)S(1)}, u32[]{:S(2)}, u32[]{:S(2)}) collective-permute-start(bf16[272,128]{1,0:T(8,128)(2,1)S(1)} %get-tuple-element.62), channel_id=1, source_target_pairs={{0,8},{4,12},{8,0},{12,4},{16,24},{20,28},{24,16},{28,20},{1,9},{5... | collective-permute-start | bytes 208904 | tf_op jit(solution)/shard_map/ppermute | solution.py:164
  48.3 1.6 %collective-permute-start.15 = (bf16[272,128]{1,0:T(8,128)(2,1)S(1)}, bf16[272,128]{1,0:T(8,128)(2,1)S(1)}, u32[]{:S(2)}, u32[]{:S(2)}) collective-permute-start(bf16[272,128]{1,0:T(8,128)(2,1)S(1)} %get-tuple-element.63), channel_id=1, source_target_pairs={{0,12},{4,8},{8,4},{12,0},{16,28},{20,24},{24,20},{28,16},{1,13},{... | collective-permute-start | bytes 208904 | tf_op jit(solution)/shard_map/ppermute | solution.py:164
  51.3 2.2 %collective-permute-done.15.rest_3_ = bf16[272,128]{1,0:T(8,128)(2,1)S(1)} collective-permute-done((bf16[272,128]{1,0:T(8,128)(2,1)S(1)}, bf16[272,128]{1,0:T(8,128)(2,1)S(1)}, u32[]{:S(2)}, u32[]{:S(2)}) %collective-permute-start.15) | collective-permute-done | bytes 69664 | tf_op jit(solution)/shard_map/ppermute | solution.py:164
  53.6 3.2 %collective-permute-start.16 = (bf16[272,128]{1,0:T(8,128)(2,1)S(1)}, bf16[272,128]{1,0:T(8,128)(2,1)S(1)}, u32[]{:S(2)}, u32[]{:S(2)}) collective-permute-start(bf16[272,128]{1,0:T(8,128)(2,1)S(1)} %get-tuple-element.64), channel_id=1, source_target_pairs={{0,16},{4,20},{8,24},{12,28},{16,0},{20,4},{24,8},{28,12},{1,17},{... | collective-permute-start | bytes 208904 | tf_op jit(solution)/shard_map/ppermute | solution.py:183
  56.8 2.2 %shard_map.101 = (f32[128,1024]{1,0:T(8,128)S(1)}, f32[128,1024]{1,0:T(8,128)S(1)}, f32[128,1024]{1,0:T(8,128)S(1)}) custom-call(s32[128,8]{1,0:T(8,128)S(1)} %copy.10.codes_ref.rest_3_, s32[8,128]{1,0:T(8,128)S(1)} %bitcast.10, bf16[128,1024]{1,0:T(8,128)(2,1)S(1)} %copy-done.10, bf16[128,1024]{1,0:T(8,128)(2,1)S(1)} %copy-done.5, ...), custom_call_target="tpu_custom_call" | custom-call | flops 134217728 | bytes 2883584 | tf_op jit(solution)/shard_map/pallas_call | solution.py:26
  59.0 1.1 %shard_map.102 = bf16[128,1024]{1,0:T(8,128)(2,1)} custom-call(s32[1]{0:T(128)} %bitcast.2.rank_ref, s32[128,8]{1,0:T(8,128)S(1)} %copy.10.codes_ref.rest_3_, f32[128,1024]{1,0:T(8,128)S(1)} %get-tuple-element.57.local_ref, bf16[128,1024]{1,0:T(8,128)(2,1)S(1)} %get-tuple-element.55.grad_ref, bf16[256,128]{1,0:T(8,128)(2,1)S(1)} %get-tuple-element.46.rest_0_, ...), custom_call_target="tpu_custom_call" | custom-call | flops 33554432 | bytes 1310720 | tf_op jit(solution)/shard_map/pallas_call | solution.py:26
  60.2 1.0 %collective-permute-start.17 = (bf16[256,128]{1,0:T(8,128)(2,1)S(1)}, bf16[256,128]{1,0:T(8,128)(2,1)S(1)}, u32[]{:S(2)}, u32[]{:S(2)}) collective-permute-start(bf16[256,128]{1,0:T(8,128)(2,1)S(1)} %get-tuple-element.67), channel_id=1, source_target_pairs={{0,4},{4,0},{8,12},{12,8},{16,20},{20,16},{24,28},{28,24},{1,5},{5... | collective-permute-start | bytes 196616 | tf_op jit(solution)/shard_map/ppermute | solution.py:164
  61.2 1.4 %collective-permute-start.18 = (bf16[256,128]{1,0:T(8,128)(2,1)S(1)}, bf16[256,128]{1,0:T(8,128)(2,1)S(1)}, u32[]{:S(2)}, u32[]{:S(2)}) collective-permute-start(bf16[256,128]{1,0:T(8,128)(2,1)S(1)} %get-tuple-element.68), channel_id=1, source_target_pairs={{0,8},{4,12},{8,0},{12,4},{16,24},{20,28},{24,16},{28,20},{1,9},{5... | collective-permute-start | bytes 196616 | tf_op jit(solution)/shard_map/ppermute | solution.py:164
  62.7 1.1 %collective-permute-start.19 = (bf16[256,128]{1,0:T(8,128)(2,1)S(1)}, bf16[256,128]{1,0:T(8,128)(2,1)S(1)}, u32[]{:S(2)}, u32[]{:S(2)}) collective-permute-start(bf16[256,128]{1,0:T(8,128)(2,1)S(1)} %get-tuple-element.69), channel_id=1, source_target_pairs={{0,12},{4,8},{8,4},{12,0},{16,28},{20,24},{24,20},{28,16},{1,13},{... | collective-permute-start | bytes 196616 | tf_op jit(solution)/shard_map/ppermute | solution.py:164
  65.5 2.3 %collective-permute-done.19.rest_3_ = bf16[256,128]{1,0:T(8,128)(2,1)S(1)} collective-permute-done((bf16[256,128]{1,0:T(8,128)(2,1)S(1)}, bf16[256,128]{1,0:T(8,128)(2,1)S(1)}, u32[]{:S(2)}, u32[]{:S(2)}) %collective-permute-start.19) | collective-permute-done | bytes 65568 | tf_op jit(solution)/shard_map/ppermute | solution.py:164
  67.8 1.2 %shard_map.105 = (bf16[128,1024]{1,0:T(8,128)(2,1)}, bf16[128,1024]{1,0:T(8,128)(2,1)}) custom-call(s32[1]{0:T(128)} %bitcast.7.rank_ref, s32[128,8]{1,0:T(8,128)S(1)} %copy.10.codes_ref.rest_3_, bf16[128,1024]{1,0:T(8,128)(2,1)S(1)} %copy-done.5, bf16[128,1024]{1,0:T(8,128)(2,1)S(1)} %copy-done.8, f32[128,1024]{1,0:T(8,128)S(1)} %get-tuple-element.58.lk_ref, ...), custom_call_target="tpu_custom_call" | custom-call | flops 67108864 | bytes 2359296 | tf_op jit(solution)/shard_map/pallas_call | solution.py:26
  (56 shorter events, 9.4 us)
Async XLA Ops:
  1.4 1.0 %copy-start.3 = (bf16[128,1024]{1,0:T(8,128)(2,1)S(1)}, bf16[128,1024]{1,0:T(8,128)(2,1)}, u32[]{:S(2)}) copy-start(bf16[128,1024]{1,0:T(8,128)(2,1)} %k_ref.7) | copy-start | bytes 786436
  2.4 0.9 %copy-start.6 = (bf16[128,1024]{1,0:T(8,128)(2,1)S(1)}, bf16[128,1024]{1,0:T(8,128)(2,1)}, u32[]{:S(2)}) copy-start(bf16[128,1024]{1,0:T(8,128)(2,1)} %v_ref.7) | copy-start | bytes 786436
  3.9 11.8 %collective-permute-start = (bf16[272,128]{1,0:T(8,128)(2,1)S(1)}, bf16[272,128]{1,0:T(8,128)(2,1)S(1)}, u32[]{:S(2)}, u32[]{:S(2)}) collective-permute-start(bf16[272,128]{1,0:T(8,128)(2,1)S(1)} %get-tuple-element.41), channel_id=1, source_target_pairs={{0,4},{4,0},{8,12},{12,8},{16,20},{20,16},{24,28},{28,24},{1,5},{5... | collective-permute-start | bytes 208904 | tf_op jit(solution)/shard_map/ppermute | solution.py:164
  7.0 8.8 %collective-permute-start.1 = (bf16[272,128]{1,0:T(8,128)(2,1)S(1)}, bf16[272,128]{1,0:T(8,128)(2,1)S(1)}, u32[]{:S(2)}, u32[]{:S(2)}) collective-permute-start(bf16[272,128]{1,0:T(8,128)(2,1)S(1)} %get-tuple-element.42), channel_id=1, source_target_pairs={{0,8},{4,12},{8,0},{12,4},{16,24},{20,28},{24,16},{28,20},{1,9},{5... | collective-permute-start | bytes 208904 | tf_op jit(solution)/shard_map/ppermute | solution.py:164
  8.5 7.2 %collective-permute-start.2 = (bf16[272,128]{1,0:T(8,128)(2,1)S(1)}, bf16[272,128]{1,0:T(8,128)(2,1)S(1)}, u32[]{:S(2)}, u32[]{:S(2)}) collective-permute-start(bf16[272,128]{1,0:T(8,128)(2,1)S(1)} %get-tuple-element.43), channel_id=1, source_target_pairs={{0,12},{4,8},{8,4},{12,0},{16,28},{20,24},{24,20},{28,16},{1,13},{... | collective-permute-start | bytes 208904 | tf_op jit(solution)/shard_map/ppermute | solution.py:164
  8.5 27.1 %collective-permute-start.10 = (bf16[128,768]{1,0:T(8,128)(2,1)}, bf16[128,768]{1,0:T(8,128)(2,1)S(1)}, u32[]{:S(2)}, u32[]{:S(2)}) collective-permute-start(bf16[128,768]{1,0:T(8,128)(2,1)} %rest_0_.1), channel_id=1, source_target_pairs={{0,2},{1,3},{2,0},{3,1},{4,6},{5,7},{6,4},{7,5},{8,10},{9,11},{10,... | collective-permute-start | bytes 589832 | tf_op jit(solution)/shard_map/ppermute | solution.py:164
  10.5 31.1 %collective-permute-start.12 = (bf16[128,768]{1,0:T(8,128)(2,1)}, bf16[128,768]{1,0:T(8,128)(2,1)S(1)}, u32[]{:S(2)}, u32[]{:S(2)}) collective-permute-start(bf16[128,768]{1,0:T(8,128)(2,1)} %rest_0_.1), channel_id=1, source_target_pairs={{0,1},{1,0},{2,3},{3,2},{4,5},{5,4},{6,7},{7,6},{8,9},{9,8},{10,11... | collective-permute-start | bytes 589832 | tf_op jit(solution)/shard_map/ppermute | solution.py:164
  10.5 1.0 %copy-start.4 = (bf16[128,1024]{1,0:T(8,128)(2,1)S(1)}, bf16[128,1024]{1,0:T(8,128)(2,1)}, u32[]{:S(2)}) copy-start(bf16[128,1024]{1,0:T(8,128)(2,1)} %k_ref.7) | copy-start | bytes 786436
  11.4 0.9 %copy-start.7 = (bf16[128,1024]{1,0:T(8,128)(2,1)S(1)}, bf16[128,1024]{1,0:T(8,128)(2,1)}, u32[]{:S(2)}) copy-start(bf16[128,1024]{1,0:T(8,128)(2,1)} %v_ref.7) | copy-start | bytes 786436
  15.9 7.0 %collective-permute-start.3 = (bf16[272,128]{1,0:T(8,128)(2,1)S(1)}, bf16[272,128]{1,0:T(8,128)(2,1)S(1)}, u32[]{:S(2)}, u32[]{:S(2)}) collective-permute-start(bf16[272,128]{1,0:T(8,128)(2,1)S(1)} %get-tuple-element.44), channel_id=1, source_target_pairs={{0,16},{4,20},{8,24},{12,28},{16,0},{20,4},{24,8},{28,12},{1,17},{... | collective-permute-start | bytes 208904 | tf_op jit(solution)/shard_map/ppermute | solution.py:183
  23.0 4.3 %collective-permute-start.4 = (bf16[256,128]{1,0:T(8,128)(2,1)S(1)}, bf16[256,128]{1,0:T(8,128)(2,1)S(1)}, u32[]{:S(2)}, u32[]{:S(2)}) collective-permute-start(bf16[256,128]{1,0:T(8,128)(2,1)S(1)} %get-tuple-element.47), channel_id=1, source_target_pairs={{0,4},{4,0},{8,12},{12,8},{16,20},{20,16},{24,28},{28,24},{1,5},{5... | collective-permute-start | bytes 196616 | tf_op jit(solution)/shard_map/ppermute | solution.py:164
  24.6 4.3 %collective-permute-start.5 = (bf16[256,128]{1,0:T(8,128)(2,1)S(1)}, bf16[256,128]{1,0:T(8,128)(2,1)S(1)}, u32[]{:S(2)}, u32[]{:S(2)}) collective-permute-start(bf16[256,128]{1,0:T(8,128)(2,1)S(1)} %get-tuple-element.48), channel_id=1, source_target_pairs={{0,8},{4,12},{8,0},{12,4},{16,24},{20,28},{24,16},{28,20},{1,9},{5... | collective-permute-start | bytes 196616 | tf_op jit(solution)/shard_map/ppermute | solution.py:164
  25.3 5.2 %collective-permute-start.6 = (bf16[256,128]{1,0:T(8,128)(2,1)S(1)}, bf16[256,128]{1,0:T(8,128)(2,1)S(1)}, u32[]{:S(2)}, u32[]{:S(2)}) collective-permute-start(bf16[256,128]{1,0:T(8,128)(2,1)S(1)} %get-tuple-element.49), channel_id=1, source_target_pairs={{0,12},{4,8},{8,4},{12,0},{16,28},{20,24},{24,20},{28,16},{1,13},{... | collective-permute-start | bytes 196616 | tf_op jit(solution)/shard_map/ppermute | solution.py:164
  30.4 2.8 %copy-start = (bf16[1024,3072]{1,0:T(8,128)(2,1)S(1)}, bf16[1024,3072]{1,0:T(8,128)(2,1)}, u32[]{:S(2)}) copy-start(bf16[1024,3072]{1,0:T(8,128)(2,1)} %weight_ref.7) | copy-start | bytes 18874372
  33.2 8.3 %copy-start.11 = (bf16[128,768]{1,0:T(8,128)(2,1)S(1)}, bf16[128,768]{1,0:T(8,128)(2,1)}, u32[]{:S(2)}) copy-start(bf16[128,768]{1,0:T(8,128)(2,1)} %rest_0_.1) | copy-start | bytes 589828
  35.4 5.5 %collective-permute-start.8 = (bf16[128,768]{1,0:T(8,128)(2,1)S(1)}, bf16[128,768]{1,0:T(8,128)(2,1)S(1)}, u32[]{:S(2)}, u32[]{:S(2)}) collective-permute-start(bf16[128,768]{1,0:T(8,128)(2,1)S(1)} %get-tuple-element.54), channel_id=1, source_target_pairs={{0,1},{1,0},{2,3},{3,2},{4,5},{5,4},{6,7},{7,6},{8,9},{9,8},{10,11... | collective-permute-start | bytes 589832 | tf_op jit(solution)/shard_map/ppermute | solution.py:164
  35.6 8.3 %collective-permute-start.11 = (bf16[128,768]{1,0:T(8,128)(2,1)S(1)}, bf16[128,768]{1,0:T(8,128)(2,1)S(1)}, u32[]{:S(2)}, u32[]{:S(2)}) collective-permute-start(bf16[128,768]{1,0:T(8,128)(2,1)S(1)} %collective-permute-done.10.rest_0_), channel_id=1, source_target_pairs={{0,1},{1,0},{2,3},{3,2},{4,5},{5,4},{6,7},{7,6},{8,9},{9,8},{10,11... | collective-permute-start | bytes 589832 | tf_op jit(solution)/shard_map/ppermute | solution.py:164
  36.1 2.8 %copy-start.1 = (bf16[1024,3072]{1,0:T(8,128)(2,1)S(1)}, bf16[1024,3072]{1,0:T(8,128)(2,1)}, u32[]{:S(2)}) copy-start(bf16[1024,3072]{1,0:T(8,128)(2,1)} %weight_ref.7) | copy-start | bytes 18874372
  38.9 2.8 %copy-start.2 = (bf16[1024,3072]{1,0:T(8,128)(2,1)S(1)}, bf16[1024,3072]{1,0:T(8,128)(2,1)}, u32[]{:S(2)}) copy-start(bf16[1024,3072]{1,0:T(8,128)(2,1)} %weight_ref.7) | copy-start | bytes 18874372
  38.9 5.0 %copy-start.10 = (bf16[128,1024]{1,0:T(8,128)(2,1)S(1)}, bf16[128,1024]{1,0:T(8,128)(2,1)}, u32[]{:S(2)}) copy-start(bf16[128,1024]{1,0:T(8,128)(2,1)} %q_ref.3) | copy-start | bytes 786436
  40.8 23.0 %collective-permute-start.7 = (bf16[128,768]{1,0:T(8,128)(2,1)S(1)}, bf16[128,768]{1,0:T(8,128)(2,1)S(1)}, u32[]{:S(2)}, u32[]{:S(2)}) collective-permute-start(bf16[128,768]{1,0:T(8,128)(2,1)S(1)} %get-tuple-element.52), channel_id=1, source_target_pairs={{0,1},{1,0},{2,3},{3,2},{4,5},{5,4},{6,7},{7,6},{8,9},{9,8},{10,11... | collective-permute-start | bytes 589832 | tf_op jit(solution)/shard_map/ppermute | solution.py:164
  40.9 15.9 %copy-start.5 = (bf16[128,1024]{1,0:T(8,128)(2,1)S(1)}, bf16[128,1024]{1,0:T(8,128)(2,1)}, u32[]{:S(2)}) copy-start(bf16[128,1024]{1,0:T(8,128)(2,1)} %k_ref.7) | copy-start | bytes 786436
  40.9 15.9 %copy-start.8 = (bf16[128,1024]{1,0:T(8,128)(2,1)S(1)}, bf16[128,1024]{1,0:T(8,128)(2,1)}, u32[]{:S(2)}) copy-start(bf16[128,1024]{1,0:T(8,128)(2,1)} %v_ref.7) | copy-start | bytes 786436
  41.0 15.9 %copy-start.13 = (s32[128,8]{0,1:T(8,128)S(1)}, s32[128,8]{0,1:T(8,128)}, u32[]{:S(2)}) copy-start(s32[128,8]{0,1:T(8,128)} %param.9) | copy-start | bytes 12292
  41.0 22.8 %collective-permute-start.9 = (bf16[128,768]{1,0:T(8,128)(2,1)S(1)}, bf16[128,768]{1,0:T(8,128)(2,1)S(1)}, u32[]{:S(2)}, u32[]{:S(2)}) collective-permute-start(bf16[128,768]{1,0:T(8,128)(2,1)S(1)} %add_convert_fusion.1), channel_id=1, source_target_pairs={{0,2},{1,3},{2,0},{3,1},{4,6},{5,7},{6,4},{7,5},{8,10},{9,11},{10,... | collective-permute-start | bytes 589832 | tf_op jit(solution)/shard_map/ppermute | solution.py:164
  46.3 4.4 %collective-permute-start.13 = (bf16[272,128]{1,0:T(8,128)(2,1)S(1)}, bf16[272,128]{1,0:T(8,128)(2,1)S(1)}, u32[]{:S(2)}, u32[]{:S(2)}) collective-permute-start(bf16[272,128]{1,0:T(8,128)(2,1)S(1)} %get-tuple-element.61), channel_id=1, source_target_pairs={{0,4},{4,0},{8,12},{12,8},{16,20},{20,16},{24,28},{28,24},{1,5},{5... | collective-permute-start | bytes 208904 | tf_op jit(solution)/shard_map/ppermute | solution.py:164
  47.0 4.3 %collective-permute-start.14 = (bf16[272,128]{1,0:T(8,128)(2,1)S(1)}, bf16[272,128]{1,0:T(8,128)(2,1)S(1)}, u32[]{:S(2)}, u32[]{:S(2)}) collective-permute-start(bf16[272,128]{1,0:T(8,128)(2,1)S(1)} %get-tuple-element.62), channel_id=1, source_target_pairs={{0,8},{4,12},{8,0},{12,4},{16,24},{20,28},{24,16},{28,20},{1,9},{5... | collective-permute-start | bytes 208904 | tf_op jit(solution)/shard_map/ppermute | solution.py:164
  48.3 5.2 %collective-permute-start.15 = (bf16[272,128]{1,0:T(8,128)(2,1)S(1)}, bf16[272,128]{1,0:T(8,128)(2,1)S(1)}, u32[]{:S(2)}, u32[]{:S(2)}) collective-permute-start(bf16[272,128]{1,0:T(8,128)(2,1)S(1)} %get-tuple-element.63), channel_id=1, source_target_pairs={{0,12},{4,8},{8,4},{12,0},{16,28},{20,24},{24,20},{28,16},{1,13},{... | collective-permute-start | bytes 208904 | tf_op jit(solution)/shard_map/ppermute | solution.py:164
  53.6 6.5 %collective-permute-start.16 = (bf16[272,128]{1,0:T(8,128)(2,1)S(1)}, bf16[272,128]{1,0:T(8,128)(2,1)S(1)}, u32[]{:S(2)}, u32[]{:S(2)}) collective-permute-start(bf16[272,128]{1,0:T(8,128)(2,1)S(1)} %get-tuple-element.64), channel_id=1, source_target_pairs={{0,16},{4,20},{8,24},{12,28},{16,0},{20,4},{24,8},{28,12},{1,17},{... | collective-permute-start | bytes 208904 | tf_op jit(solution)/shard_map/ppermute | solution.py:183
  60.2 5.0 %collective-permute-start.17 = (bf16[256,128]{1,0:T(8,128)(2,1)S(1)}, bf16[256,128]{1,0:T(8,128)(2,1)S(1)}, u32[]{:S(2)}, u32[]{:S(2)}) collective-permute-start(bf16[256,128]{1,0:T(8,128)(2,1)S(1)} %get-tuple-element.67), channel_id=1, source_target_pairs={{0,4},{4,0},{8,12},{12,8},{16,20},{20,16},{24,28},{28,24},{1,5},{5... | collective-permute-start | bytes 196616 | tf_op jit(solution)/shard_map/ppermute | solution.py:164
  61.2 4.3 %collective-permute-start.18 = (bf16[256,128]{1,0:T(8,128)(2,1)S(1)}, bf16[256,128]{1,0:T(8,128)(2,1)S(1)}, u32[]{:S(2)}, u32[]{:S(2)}) collective-permute-start(bf16[256,128]{1,0:T(8,128)(2,1)S(1)} %get-tuple-element.68), channel_id=1, source_target_pairs={{0,8},{4,12},{8,0},{12,4},{16,24},{20,28},{24,16},{28,20},{1,9},{5... | collective-permute-start | bytes 196616 | tf_op jit(solution)/shard_map/ppermute | solution.py:164
  62.7 5.2 %collective-permute-start.19 = (bf16[256,128]{1,0:T(8,128)(2,1)S(1)}, bf16[256,128]{1,0:T(8,128)(2,1)S(1)}, u32[]{:S(2)}, u32[]{:S(2)}) collective-permute-start(bf16[256,128]{1,0:T(8,128)(2,1)S(1)} %get-tuple-element.69), channel_id=1, source_target_pairs={{0,12},{4,8},{8,4},{12,0},{16,28},{20,24},{24,20},{28,16},{1,13},{... | collective-permute-start | bytes 196616 | tf_op jit(solution)/shard_map/ppermute | solution.py:164
  (2 other events, 1.6 us)

commit v2 on v1

v2 whole, which is shorter than its diff:
```python
import functools

import jax
import jax.numpy as jnp
from jax import lax
from jax.experimental import pallas as pl
from jax.experimental.pallas import tpu as pltpu
from jax.sharding import PartitionSpec as P


F32 = jnp.float32
BF16 = jnp.bfloat16
VMEM = pl.BlockSpec(memory_space=pltpu.VMEM)
SMEM = pl.BlockSpec(memory_space=pltpu.SMEM)
HBM = pl.BlockSpec(memory_space=pltpu.HBM)


def dot(a, b, ca, cb):
    return lax.dot_general(a, b, (((ca,), (cb,)), ((), ())), preferred_element_type=F32)


def aligned(index, size):
    return pl.ds(pl.multiple_of(index * size, size), size)


def call(kernel, outs, specs, args, scratch=(), limit=16, flops=0, nbytes=0):
    return pl.pallas_call(
        kernel,
        out_shape=outs,
        in_specs=specs,
        out_specs=[VMEM] * len(outs),
        scratch_shapes=list(scratch),
        compiler_params=pltpu.CompilerParams(vmem_limit_bytes=limit << 20),
        cost_estimate=pl.CostEstimate(flops=flops, bytes_accessed=nbytes, transcendentals=0),
    )(*args)


def in_hbm(array):
    return pltpu.with_memory_space_constraint(array, pltpu.HBM)


def shape(dims, dtype):
    return jax.ShapeDtypeStruct(dims, dtype)


def running_log(codes_ref):
    total = jnp.log(1.0 - codes_ref[...].astype(F32) / 4096.0)
    place = lax.broadcasted_iota(jnp.int32, total.shape, 1)
    step = 1
    while step < total.shape[1]:
        total = total + jnp.where(place >= step, pltpu.roll(total, step, 1), 0.0)
        step *= 2
    return total


def running_pair(codes_ref):
    cum_t = running_log(codes_ref)
    return cum_t.T, cum_t


def positions(plan, way):
    place = lax.axis_index("seq")
    turn = place if way > 0 else plan.seq - 1 - place
    return lax.rem(turn, plan.group), lax.div(turn, plan.group)


class Plan:
    def __init__(self, tok, heads, width, seq):
        self.tok, self.heads, self.width, self.seq = tok, heads, width, seq
        self.group = next(g for g in (4, 2, 1) if heads % g == 0 and seq % g == 0)
        self.groups = seq // self.group
        self.quarter = heads // self.group
        self.half_tail = 8 * pl.cdiv(self.quarter, 8)
        self.tail = 2 * self.half_tail
        self.body = self.quarter * width
        self.rows = self.body + self.tail


def tail_rows(plan, totals):
    place = lax.broadcasted_iota(jnp.int32, (plan.tail, plan.width), 0)
    rows = jnp.zeros((plan.tail, plan.width), F32)
    for i, total in enumerate(totals):
        high = total.astype(BF16).astype(F32)
        rows = jnp.where(place == i, high, rows)
        rows = jnp.where(place == plan.half_tail + i, total - high, rows)
    return rows


def read_tail(plan, ref, base, i):
    at = base + plan.body + i
    return ref[at : at + 1, :] + ref[at + plan.half_tail : at + plan.half_tail + 1, :]


def put_summaries(plan, rank, left, right, cum, outs, scratch, arrive=None):
    width = plan.width
    last = jnp.exp(cum[plan.tok - 1 : plan.tok, :])
    for q in range(plan.group):
        base = q * plan.rows
        totals = []
        if arrive is not None:
            arrive(q)
        for i in range(plan.quarter):
            h = q * plan.quarter + i
            scratch[base + i * width : base + (i + 1) * width, :] = dot(left(h), right(h), 0, 0)
            totals.append(jnp.broadcast_to(last[:, h : h + 1], (1, width)))
        scratch[base + plan.body : base + plan.rows, :] = tail_rows(plan, totals)
    outs[0][...] = scratch[aligned(rank, plan.rows), :]
    for j in range(1, plan.group):
        outs[j][...] = scratch[aligned(rank ^ j, plan.rows), :].astype(BF16)


def summary_shapes(plan):
    rows = (plan.rows, plan.width)
    return [shape(rows, F32)] + [shape(rows, BF16)] * (plan.group - 1)


def summary_scratch(plan):
    return pltpu.VMEM((plan.group * plan.rows, plan.width), F32)


def forward_summary_kernel(plan, *refs):
    codes, keys, values, queries = refs[:4]
    outs, rest = refs[4 : 4 + plan.group], refs[4 + plan.group :]
    codes_ref, k_ref, v_ref, q_ref, scratch, sems = rest
    wide = plan.quarter * plan.width
    loads = [pltpu.make_async_copy(codes, codes_ref, sems.at[0])]
    for q in range(plan.group):
        at = slice(q * wide, (q + 1) * wide)
        loads.append(pltpu.make_async_copy(keys.at[:, at], k_ref.at[:, at], sems.at[2 * q + 1]))
        loads.append(pltpu.make_async_copy(values.at[:, at], v_ref.at[:, at], sems.at[2 * q + 2]))
    loads.append(pltpu.make_async_copy(queries, q_ref, sems.at[2 * plan.group + 1]))
    for load in loads:
        load.start()
    loads[0].wait()
    cum, _ = running_pair(codes_ref)
    fall = jnp.exp(cum[plan.tok - 1 : plan.tok, :] - cum)

    def cols(h):
        return slice(h * plan.width, (h + 1) * plan.width)

    def arrive(q):
        loads[2 * q + 1].wait()
        loads[2 * q + 2].wait()

    def left(h):
        return (fall[:, h : h + 1] * k_ref[:, cols(h)].astype(F32)).astype(BF16)

    rank = positions(plan, 1)[0]
    put_summaries(plan, rank, left, lambda h: v_ref[:, cols(h)], cum, outs, scratch, arrive)
    loads[-1].wait()


def combine_kernel(plan, way, *rest):
    group, width = plan.group, plan.width
    ins, (pre_ref, total_ref, scratch) = rest[:group], rest[group:]
    rank = positions(plan, way)[0]
    for j in range(group):
        scratch[aligned(rank ^ j, plan.rows), :] = ins[j][...].astype(F32)
    decays = []
    for i in range(plan.quarter):
        held = jnp.zeros((width, width), F32)
        decay = jnp.ones((1, width), F32)
        per_member = []
        for m in range(group):
            base = m * plan.rows
            at = slice(base + i * width, base + (i + 1) * width)
            pre_ref[at, :] = held
            per_member.append(decay)
            total = read_tail(plan, scratch, base, i)
            held = total * held + scratch[at, :]
            decay = decay * total
        decays.append(per_member + [decay])
        total_ref[i * width : (i + 1) * width, :] = held.astype(BF16)
    for m in range(group):
        base = m * plan.rows + plan.body
        pre_ref[base : base + plan.tail, :] = tail_rows(plan, [d[m] for d in decays])
    total_ref[plan.body : plan.rows, :] = tail_rows(plan, [d[group] for d in decays]).astype(BF16)


def spread_kernel(plan, way, entry_ref, pre_ref, *rest):
    group, width = plan.group, plan.width
    outs, scratch = rest[:group], rest[group]
    rank, turn = positions(plan, way)
    enters = turn > 0
    for i in range(plan.quarter):
        at = slice(i * width, (i + 1) * width)
        entry = jnp.where(enters, entry_ref[at, :].astype(F32), 0.0)
        for m in range(group):
            base = m * plan.rows
            state = read_tail(plan, pre_ref, base, i) * entry
            state = state + pre_ref[base + i * width : base + (i + 1) * width, :]
            to = m * plan.body + i * width
            scratch[to : to + width, :] = state.astype(BF16)
    for j in range(group):
        outs[j][...] = scratch[aligned(rank ^ j, plan.body), :]


def swap(value, axis, offset):
    count = lax.axis_size(axis)
    return lax.ppermute(value, axis, [(i, i ^ offset) for i in range(count)])


def join(plan, earlier, later):
    earlier, later = earlier.astype(F32), later.astype(F32)
    bodies, totals = [], []
    for i in range(plan.quarter):
        at = slice(i * plan.width, (i + 1) * plan.width)
        mine = read_tail(plan, later, 0, i)
        bodies.append(mine * earlier[at] + later[at])
        totals.append(mine * read_tail(plan, earlier, 0, i))
    return jnp.concatenate(bodies + [tail_rows(plan, totals)]).astype(BF16)


def group_entry(plan, total, way, turn):
    count, span = plan.seq, plan.group

    def shift(value, by):
        hop = way * by * span
        return lax.ppermute(value, "seq", [(i, (i + hop) % count) for i in range(count)])

    entry = shift(total, 1)
    by = 1
    while by < plan.groups - 1:
        entry = jnp.where(turn > by, join(plan, shift(entry, by), entry), entry)
        by *= 2
    return entry


def scan_states(plan, summaries, way):
    turn = positions(plan, way)[1]
    others = range(1, plan.group)
    got = [summaries[0]] + [swap(summaries[j], "seq", j) for j in others]
    rows, body = (plan.rows, plan.width), (plan.body, plan.width)
    pre, total = call(
        functools.partial(combine_kernel, plan, way),
        [shape((plan.group * plan.rows, plan.width), F32), shape(rows, BF16)],
        [VMEM] * plan.group,
        got,
        [pltpu.VMEM((plan.group * plan.rows, plan.width), F32)],
    )
    entry = group_entry(plan, total, way, turn)
    states = call(
        functools.partial(spread_kernel, plan, way),
        [shape(body, BF16)] * plan.group,
        [VMEM, VMEM],
        [entry, pre],
        [pltpu.VMEM((plan.group * plan.body, plan.width), BF16)],
    )
    return [states[0]] + [swap(states[j], "seq", j) for j in others]


def gather_states(plan, way, ins, scratch):
    rank = positions(plan, way)[0]
    for j in range(plan.group):
        scratch[aligned(rank ^ j, plan.body), :] = ins[j][...]


def mask_of(plan, cum, cum_t, h):
    size = (plan.tok, plan.tok)
    lower = lax.broadcasted_iota(jnp.int32, size, 0) >= lax.broadcasted_iota(jnp.int32, size, 1)
    gap = cum[:, h : h + 1] - cum_t[h : h + 1, :]
    return jnp.where(lower, jnp.exp(jnp.where(lower, gap, 0.0)), 0.0)


def forward_local_kernel(plan, codes_ref, q_ref, k_ref, v_ref, attn_ref, out_ref, rise_ref):
    scale = 1.0 / plan.width
    cum, cum_t = running_pair(codes_ref)
    rise = scale * jnp.exp(cum)
    for h in range(plan.heads):
        at = slice(h * plan.width, (h + 1) * plan.width)
        rows = slice(h * plan.tok, (h + 1) * plan.tok)
        q = q_ref[:, at]
        scores = dot(q, k_ref[:, at], 1, 1)
        attn = (scale * scores * mask_of(plan, cum, cum_t, h)).astype(BF16)
        attn_ref[rows, :] = attn
        out_ref[:, at] = dot(attn, v_ref[:, at], 1, 0)
        rise_ref[:, at] = (rise[:, h : h + 1] * q.astype(F32)).astype(BF16)


def weight_columns(offset, width):
    return aligned(lax.axis_index("head") ^ offset, width)


def near_grad_kernel(near, far, weight, first, *rest):
    shards, (sum_ref, weight_ref, first_ref, sems, first_sem) = rest[:-5], rest[-5:]
    width, rows = first.shape[1], weight.shape[0] // 2
    load_first = pltpu.make_async_copy(first, first_ref, first_sem)
    load_first.start()
    loads = []
    for offset in near + far:
        columns = weight_columns(offset, width)
        for part in range(2):
            at = (slice(part * rows, (part + 1) * rows), columns)
            sem = sems.at[len(loads)]
            loads.append(pltpu.make_async_copy(weight.at[at], weight_ref.at[at], sem))
    ahead = 2 * len(near)
    for load in loads[:ahead]:
        load.start()
    load_first.wait()
    for i, offset in enumerate(near):
        shard = (first_ref if i == 0 else shards[i - 1])[...]
        columns = weight_columns(offset, width)
        for part in range(2):
            at = slice(part * rows, (part + 1) * rows)
            loads[2 * i + part].wait()
            loads[ahead + 2 * i + part].start()
            product = dot(shard, weight_ref[at, columns], 1, 1)
            sum_ref[:, at] = product if i == 0 else sum_ref[:, at] + product
    for load in loads[ahead:]:
        load.wait()


def far_grad_kernel(plan, offsets, weight_ref, *rest):
    count = len(offsets)
    shards, (before_ref, codes_ref, q_ref, grad_ref) = rest[:count], rest[count : count + 4]
    outs, scratch = rest[count + 4 : -1], rest[-1]
    width = shards[0].shape[1]
    total = before_ref[...]
    for offset, shard in zip(offsets, shards):
        total = total + dot(shard[...], weight_ref[:, weight_columns(offset, width)], 1, 1)
    grad_ref[...] = total.astype(BF16)
    cum, _ = running_pair(codes_ref)
    rise = (1.0 / plan.width) * jnp.exp(cum)

    def cols(h):
        return slice(h * plan.width, (h + 1) * plan.width)

    def left(h):
        return (rise[:, h : h + 1] * q_ref[:, cols(h)].astype(F32)).astype(BF16)

    put_summaries(plan, positions(plan, -1)[0], left, lambda h: grad_ref[:, cols(h)], cum, outs, scratch)


def backward_local_kernel(
    plan, codes_ref, q_ref, k_ref, v_ref, grad_ref, attn_ref, lq_ref, lk_ref, lv_ref
):
    scale = 1.0 / plan.width
    cum, cum_t = running_pair(codes_ref)
    for h in range(plan.heads):
        at = slice(h * plan.width, (h + 1) * plan.width)
        rows = slice(h * plan.tok, (h + 1) * plan.tok)
        grad = grad_ref[:, at]
        scores = dot(grad, v_ref[:, at], 1, 1)
        pmat = (scale * scores * mask_of(plan, cum, cum_t, h)).astype(BF16)
        lq_ref[:, at] = dot(pmat, k_ref[:, at], 1, 0)
        lk_ref[:, at] = dot(pmat, q_ref[:, at], 0, 0)
        lv_ref[:, at] = dot(attn_ref[rows, :], grad, 0, 0)


def mix(offsets, weight_ref, flat_ref, outs):
    for offset, out in zip(offsets, outs):
        columns = weight_ref[:, weight_columns(offset, out.shape[1])]
        out[...] = dot(flat_ref[...], columns, 1, 0).astype(out.dtype)


def mix_first_kernel(plan, offsets, weight_ref, local_ref, rise_ref, *rest):
    ins, (flat_ref, *outs, states) = rest[: plan.group], rest[plan.group :]
    gather_states(plan, 1, ins, states)
    for h in range(plan.heads):
        at = slice(h * plan.width, (h + 1) * plan.width)
        cross = dot(rise_ref[:, at], states[at, :], 1, 0)
        flat_ref[:, at] = (local_ref[:, at] + cross).astype(BF16)
    mix(offsets, weight_ref, flat_ref, outs)


def mix_second_kernel(offsets, weight_ref, flat_ref, *outs):
    mix(offsets, weight_ref, flat_ref, outs)


def query_grad_kernel(plan, codes_ref, local_ref, grad_ref, *rest):
    ins, (out_ref, states) = rest[: plan.group], rest[plan.group :]
    gather_states(plan, 1, ins, states)
    rise = (1.0 / plan.width) * jnp.exp(running_pair(codes_ref)[0])
    for h in range(plan.heads):
        at = slice(h * plan.width, (h + 1) * plan.width)
        g_rise = (rise[:, h : h + 1] * grad_ref[:, at].astype(F32)).astype(BF16)
        out_ref[:, at] = (local_ref[:, at] + dot(g_rise, states[at, :], 1, 1)).astype(BF16)


def key_value_grad_kernel(plan, codes_ref, k_ref, v_ref, lk_ref, lv_ref, *rest):
    ins, (kg_ref, vg_ref, states) = rest[: plan.group], rest[plan.group :]
    gather_states(plan, -1, ins, states)
    cum, _ = running_pair(codes_ref)
    fall = jnp.exp(cum[plan.tok - 1 : plan.tok, :] - cum)
    for h in range(plan.heads):
        at = slice(h * plan.width, (h + 1) * plan.width)
        carry = states[at, :]
        v_fall = (fall[:, h : h + 1] * v_ref[:, at].astype(F32)).astype(BF16)
        k_fall = (fall[:, h : h + 1] * k_ref[:, at].astype(F32)).astype(BF16)
        kg_ref[:, at] = (lk_ref[:, at] + dot(v_fall, carry, 1, 1)).astype(BF16)
        vg_ref[:, at] = (lv_ref[:, at] + dot(k_fall, carry, 1, 0)).astype(BF16)


def local(queries, keys, values, decay_codes, out_weight, out_grad):
    tok, flat = queries.shape
    heads = decay_codes.shape[1]
    plan = Plan(tok, heads, flat // heads, lax.axis_size("seq"))
    across, feat = lax.axis_size("head"), out_grad.shape[1]
    codes = decay_codes.T
    half = across // 2
    wide = (tok, flat)
    near, far = list(range(half)), list(range(half, across))

    shards = {0: out_grad}
    hop = half
    while hop:
        for o, part in list(shards.items()):
            shards[o ^ hop] = swap(part, "head", hop)
        hop //= 2

    *summaries, codes, keys, values, queries = call(
        functools.partial(forward_summary_kernel, plan),
        summary_shapes(plan) + [shape(x.shape, x.dtype) for x in (codes, keys, values, queries)],
        [HBM] * 4,
        [in_hbm(x) for x in (codes, keys, values, queries)],
        [summary_scratch(plan), pltpu.SemaphoreType.DMA((2 * plan.group + 2,))],
        flops=2 * tok * flat * plan.width,
        nbytes=4 * tok * flat,
    )
    states = scan_states(plan, summaries, 1)

    matmul = dict(flops=2 * tok * flat * feat * half, nbytes=2 * flat * feat * half)
    part, out_weight = call(
        functools.partial(near_grad_kernel, near, far),
        [shape(wide, F32), shape(out_weight.shape, BF16)],
        [HBM] * 2 + [VMEM] * (half - 1),
        [in_hbm(out_weight), in_hbm(out_grad)] + [shards[o] for o in near[1:]],
        [
            pltpu.VMEM(out_grad.shape, BF16),
            pltpu.SemaphoreType.DMA((2 * across,)),
            pltpu.SemaphoreType.DMA,
        ],
        **matmul,
    )
    grad, *summaries_back = call(
        functools.partial(far_grad_kernel, plan, far),
        [shape(wide, BF16)] + summary_shapes(plan),
        [VMEM] * (half + 4),
        [out_weight] + [shards[o] for o in far] + [part, codes, queries],
        [summary_scratch(plan)],
        **matmul,
    )
    carries = scan_states(plan, summaries_back, -1)

    attn, local_out, q_rise = call(
        functools.partial(forward_local_kernel, plan),
        [shape((heads * tok, tok), BF16), shape(wide, F32), shape(wide, BF16)],
        [VMEM] * 4,
        [codes, queries, keys, values],
        flops=4 * tok * flat * plan.width,
        nbytes=14 * tok * flat,
    )
    local_q, local_k, local_v = call(
        functools.partial(backward_local_kernel, plan),
        [shape(wide, F32)] * 3,
        [VMEM] * 6,
        [codes, queries, keys, values, grad, attn],
        flops=8 * tok * flat * plan.width,
        nbytes=22 * tok * flat,
    )

    held = pltpu.VMEM((flat, plan.width), BF16)
    far, near = far[::-1], near[::-1]
    attn_out, *sent = call(
        functools.partial(mix_first_kernel, plan, far),
        [shape(wide, BF16)] + [shape((tok, feat), BF16)] * half,
        [VMEM] * (3 + plan.group),
        [out_weight, local_out, q_rise] + states,
        [held],
        **matmul,
    )
    kept = call(
        functools.partial(mix_second_kernel, near),
        [shape((tok, feat), F32 if o == 0 else BF16) for o in near],
        [VMEM] * 2,
        [out_weight, attn_out],
        **matmul,
    )

    def halve(parts, hop):
        moved = {o: swap(part, "head", hop) for o, part in parts.items() if o & hop}
        return {
            o: (part.astype(F32) + moved[o | hop].astype(F32)).astype(F32 if o == 0 else BF16)
            for o, part in parts.items()
            if not o & hop
        }

    far_parts, near_parts = dict(zip(far, sent)), dict(zip(near, kept))
    hop = 1
    while hop < half:
        far_parts, near_parts = halve(far_parts, hop), halve(near_parts, hop)
        hop *= 2
    mixed = halve({**far_parts, **near_parts}, half)[0].astype(BF16)

    (query_grad,) = call(
        functools.partial(query_grad_kernel, plan),
        [shape(wide, BF16)],
        [VMEM] * (3 + plan.group),
        [codes, local_q, grad] + states,
        [held],
        flops=2 * tok * flat * plan.width,
        nbytes=10 * tok * flat,
    )
    key_grad, value_grad = call(
        functools.partial(key_value_grad_kernel, plan),
        [shape(wide, BF16)] * 2,
        [VMEM] * (5 + plan.group),
        [codes, keys, values, local_k, local_v] + carries,
        [held],
        flops=4 * tok * flat * plan.width,
        nbytes=18 * tok * flat,
    )
    return mixed, query_grad, key_grad, value_grad


def solution(mesh):
    whole = P("seq", "head")

    return jax.shard_map(
        local,
        mesh=mesh,
        in_specs=(whole, whole, whole, whole, P("head", None), whole),
        out_specs=(whole,) * 4,
        check_vma=False,
    )
```

time: 69.5 us -> 57.2 us (0.82)
  local copies, waits for them, and re-layouts: 11.9 us -> 0 us
  Pallas kernels: 15.9 us -> 17.1 us
  waiting for transfers between devices: 15.1 us -> 14.4 us
    unnamed x29 -> x0, local copies, waits for them, and re-layouts: 11.9 us -> none
    pallas_call x13, Pallas kernels: 15.9 us -> 17.1 us  [call(): pl.pallas_call(kernel, out_shape=outs, in_specs=specs, out_specs=[VMEM] *...]
    ppermute x2, waiting for transfers between devices: 4.32 us -> 3.37 us  [shift(): lax.ppermute(value, 'seq', [(i, (i + hop) % count) for i in range(count)])]
  transfers between devices with their start and end apart: 20 -> 20, of which waited for: 10 -> 10; matrix products, arithmetic and copies ran while one was open for 2% -> 1% of each run, Pallas kernels for 20% -> 27%
where the time goes in v2:
time: 57.2 us; the launch traced here: 57 us
  starting transfers between devices  23.9 us (42%)
  Pallas kernels  17.1 us (30%)
  waiting for transfers between devices  14.4 us (25%)
  other arithmetic  0.79 us (1%)
  between operations  0.77 us (1%)
    ppermute x18, starting transfers between devices, swap(): return lax.ppermute(value, axis, [(i, i ^ offset) for i in range(count)])  18.2 us
    pallas_call x13, Pallas kernels, call(): pl.pallas_call(kernel, out_shape=outs, in_specs=specs, out_specs=[VMEM] *...  17.1 us
    ppermute x18, waiting for transfers between devices, swap(): return lax.ppermute(value, axis, [(i, i ^ offset) for i in range(count)])  11.1 us
    ppermute x2, starting transfers between devices, shift(): lax.ppermute(value, 'seq', [(i, (i + hop) % count) for i in range(count)])  5.79 us
    ppermute x2, waiting for transfers between devices, shift(): lax.ppermute(value, 'seq', [(i, (i + hop) % count) for i in range(count)])  3.37 us
  transfers between devices with their start and end apart: 20, of which 10 were waited for; matrix products, arithmetic and copies ran while one was open for 1% of the time, Pallas kernels for 27%

profile of v2, /device:TPU:0, one launch (start us, length us, event | category | flops | bytes accessed | tf_op | source)
XLA Modules:
  0.0 57.0 jit_solution(5248084165046867838)
XLA Ops:
  0.6 0.6 collective-permute-start
  1.2 2.6 %shard_map.94 = (f32[272,128]{1,0:T(8,128)S(1)}, bf16[272,128]{1,0:T(8,128)(2,1)S(1)}, bf16[272,128]{1,0:T(8,128)(2,1)S(1)}, bf16[272,128]{1,0:T(8,128)(2,1)S(1)...) custom-call(s32[8,128]{1,0:T(8,128)} %bitcast.1, ...), custom_call_target="tpu_custom_call" | custom-call | flops 33554432 | bytes 524288 | tf_op jit(solution)/shard_map/pallas_call | solution.py:27
  3.8 2.6 %collective-permute-start.1 = (bf16[272,128]{1,0:T(8,128)(2,1)S(1)}, bf16[272,128]{1,0:T(8,128)(2,1)S(1)}, u32[]{:S(2)}, u32[]{:S(2)}) collective-permute-start(bf16[272,128]{1,0:T(8,128)(2,1)S(1)} %get-tuple-element.52), channel_id=1, source_target_pairs={{0,4},{4,0},{8,12},{12,8},{16,20},{20,16},{24,28},{28,24},{1,5},{5... | collective-permute-start | bytes 208904 | tf_op jit(solution)/shard_map/ppermute | solution.py:200
  6.4 1.6 %collective-permute-start.2 = (bf16[272,128]{1,0:T(8,128)(2,1)S(1)}, bf16[272,128]{1,0:T(8,128)(2,1)S(1)}, u32[]{:S(2)}, u32[]{:S(2)}) collective-permute-start(bf16[272,128]{1,0:T(8,128)(2,1)S(1)} %get-tuple-element.53), channel_id=1, source_target_pairs={{0,8},{4,12},{8,0},{12,4},{16,24},{20,28},{24,16},{28,20},{1,9},{5... | collective-permute-start | bytes 208904 | tf_op jit(solution)/shard_map/ppermute | solution.py:200
  8.0 1.3 %collective-permute-done.1.rest_1_ = bf16[272,128]{1,0:T(8,128)(2,1)S(1)} collective-permute-done((bf16[272,128]{1,0:T(8,128)(2,1)S(1)}, bf16[272,128]{1,0:T(8,128)(2,1)S(1)}, u32[]{:S(2)}, u32[]{:S(2)}) %collective-permute-start.1) | collective-permute-done | bytes 69664 | tf_op jit(solution)/shard_map/ppermute | solution.py:200
  9.2 1.7 %collective-permute-done.2.rest_2_ = bf16[272,128]{1,0:T(8,128)(2,1)S(1)} collective-permute-done((bf16[272,128]{1,0:T(8,128)(2,1)S(1)}, bf16[272,128]{1,0:T(8,128)(2,1)S(1)}, u32[]{:S(2)}, u32[]{:S(2)}) %collective-permute-start.2) | collective-permute-done | bytes 69664 | tf_op jit(solution)/shard_map/ppermute | solution.py:200
  10.9 2.2 %collective-permute-done.3.rest_3_ = bf16[272,128]{1,0:T(8,128)(2,1)S(1)} collective-permute-done((bf16[272,128]{1,0:T(8,128)(2,1)S(1)}, bf16[272,128]{1,0:T(8,128)(2,1)S(1)}, u32[]{:S(2)}, u32[]{:S(2)}) %collective-permute-start.3) | collective-permute-done | bytes 69664 | tf_op jit(solution)/shard_map/ppermute | solution.py:200
  13.3 2.7 %collective-permute-start.4 = (bf16[272,128]{1,0:T(8,128)(2,1)S(1)}, bf16[272,128]{1,0:T(8,128)(2,1)S(1)}, u32[]{:S(2)}, u32[]{:S(2)}) collective-permute-start(bf16[272,128]{1,0:T(8,128)(2,1)S(1)} %get-tuple-element.55), channel_id=1, source_target_pairs={{0,16},{4,20},{8,24},{12,28},{16,0},{20,4},{24,8},{28,12},{1,17},{... | collective-permute-start | bytes 208904 | tf_op jit(solution)/shard_map/ppermute | solution.py:219
  15.9 3.4 %collective-permute-done.4.entry_ref = bf16[272,128]{1,0:T(8,128)(2,1)S(1)} collective-permute-done((bf16[272,128]{1,0:T(8,128)(2,1)S(1)}, bf16[272,128]{1,0:T(8,128)(2,1)S(1)}, u32[]{:S(2)}, u32[]{:S(2)}) %collective-permute-start.4) | collective-permute-done | bytes 69664 | tf_op jit(solution)/shard_map/ppermute | solution.py:219
  19.5 1.3 %collective-permute-start.6 = (bf16[256,128]{1,0:T(8,128)(2,1)S(1)}, bf16[256,128]{1,0:T(8,128)(2,1)S(1)}, u32[]{:S(2)}, u32[]{:S(2)}) collective-permute-start(bf16[256,128]{1,0:T(8,128)(2,1)S(1)} %get-tuple-element.59), channel_id=1, source_target_pairs={{0,8},{4,12},{8,0},{12,4},{16,24},{20,28},{24,16},{28,20},{1,9},{5... | collective-permute-start | bytes 196616 | tf_op jit(solution)/shard_map/ppermute | solution.py:200
  20.8 2.2 %collective-permute-start.7 = (bf16[256,128]{1,0:T(8,128)(2,1)S(1)}, bf16[256,128]{1,0:T(8,128)(2,1)S(1)}, u32[]{:S(2)}, u32[]{:S(2)}) collective-permute-start(bf16[256,128]{1,0:T(8,128)(2,1)S(1)} %get-tuple-element.60), channel_id=1, source_target_pairs={{0,12},{4,8},{8,4},{12,0},{16,28},{20,24},{24,20},{28,16},{1,13},{... | collective-permute-start | bytes 196616 | tf_op jit(solution)/shard_map/ppermute | solution.py:200
  22.9 1.5 %collective-permute-start.11 = (bf16[128,768]{1,0:T(8,128)(2,1)}, bf16[128,768]{1,0:T(8,128)(2,1)S(1)}, u32[]{:S(2)}, u32[]{:S(2)}) collective-permute-start(bf16[128,768]{1,0:T(8,128)(2,1)} %first.1), channel_id=1, source_target_pairs={{0,2},{1,3},{2,0},{3,1},{4,6},{5,7},{6,4},{7,5},{8,10},{9,11},{10,... | collective-permute-start | bytes 589832 | tf_op jit(solution)/shard_map/ppermute | solution.py:200
  24.5 1.9 %shard_map.95 = (bf16[1024,128]{1,0:T(8,128)(2,1)S(1)}, f32[128,1024]{1,0:T(8,128)S(1)}, bf16[128,1024]{1,0:T(8,128)(2,1)S(1)}) custom-call(s32[8,128]{1,0:T(8,128)S(1)} %get-tuple-element.45.codes_ref.rest_3_, bf16[128,1024]{1,0:T(8,128)(2,1)S(1)} %get-tuple-element.46.q_ref.rest_4_, bf16[128,1024]{1,0:T(8,128)(2,1)S(1)} %get-tuple-element.47.k_ref, ...), custom_call_target="tpu_custom_call" | custom-call | flops 67108864 | bytes 1835008 | tf_op jit(solution)/shard_map/pallas_call | solution.py:27
  26.3 3.6 %shard_map.93 = (f32[128,1024]{1,0:T(8,128)S(1)}, bf16[1024,3072]{1,0:T(8,128)(2,1)S(1)}) custom-call(bf16[1024,3072]{1,0:T(8,128)(2,1)} %weight.1, bf16[128,768]{1,0:T(8,128)(2,1)} %first.1, bf16[128,768]{1,0:T(8,128)(2,1)S(1)} %collective-permute-done.rest_0_), custom_call_target="tpu_custom_call" | custom-call | flops 402653184 | bytes 3145728 | tf_op jit(solution)/shard_map/pallas_call | solution.py:27
  30.0 0.7 %shard_map.98 = (bf16[128,1024]{1,0:T(8,128)(2,1)S(1)}, bf16[128,768]{1,0:T(8,128)(2,1)S(1)}, bf16[128,768]{1,0:T(8,128)(2,1)S(1)}) custom-call(bf16[1024,3072]{1,0:T(8,128)(2,1)S(1)} %get-tuple-element.44.weight_ref, f32[128,1024]{1,0:T(8,128)S(1)} %get-tuple-element.49.local_ref, bf16[128,1024]{1,0:T(8,128)(2,1)S(1)} %get-tuple-element.50.rise_ref, ...), custom_call_target="tpu_custom_call" | custom-call | flops 402653184 | bytes 3145728 | tf_op jit(solution)/shard_map/pallas_call | solution.py:27
  30.8 0.5 collective-permute-start.12
  31.3 0.6 %shard_map.99 = (bf16[128,768]{1,0:T(8,128)(2,1)S(1)}, f32[128,768]{1,0:T(8,128)S(1)}) custom-call(bf16[1024,3072]{1,0:T(8,128)(2,1)S(1)} %get-tuple-element.44.weight_ref, bf16[128,1024]{1,0:T(8,128)(2,1)S(1)} %get-tuple-element.61.flat_ref), custom_call_target="tpu_custom_call" | custom-call | flops 402653184 | bytes 3145728 | tf_op jit(solution)/shard_map/pallas_call | solution.py:27
  32.3 0.6 %collective-permute-start.10 = (bf16[128,768]{1,0:T(8,128)(2,1)S(1)}, bf16[128,768]{1,0:T(8,128)(2,1)S(1)}, u32[]{:S(2)}, u32[]{:S(2)}) collective-permute-start(bf16[128,768]{1,0:T(8,128)(2,1)S(1)} %add_convert_fusion.1), channel_id=1, source_target_pairs={{0,2},{1,3},{2,0},{3,1},{4,6},{5,7},{6,4},{7,5},{8,10},{9,11},{10,... | collective-permute-start | bytes 589832 | tf_op jit(solution)/shard_map/ppermute | solution.py:200
  32.9 1.5 %shard_map.100 = (bf16[128,1024]{1,0:T(8,128)(2,1)S(1)}, f32[272,128]{1,0:T(8,128)S(1)}, bf16[272,128]{1,0:T(8,128)(2,1)S(1)}, bf16[272,128]{1,0:T(8,128)(2,1)S(1)}, bf16[272,128]{1,0:T(8,128)(2,1)S(1)}) custom-call(bf16[1024,3072]{1,0:T(8,128)(2,1)S(1)} %get-tuple-element.44.weight_ref, bf16[128,768]{1,0:T(8,128)(2,1)S(1)} %collective-permute-done.11.rest_0_, ...), custom_call_target="tpu_custom_call" | custom-call | flops 402653184 | bytes 3145728 | tf_op jit(solution)/shard_map/pallas_call | solution.py:27
  34.5 1.2 %collective-permute-start.14 = (bf16[272,128]{1,0:T(8,128)(2,1)S(1)}, bf16[272,128]{1,0:T(8,128)(2,1)S(1)}, u32[]{:S(2)}, u32[]{:S(2)}) collective-permute-start(bf16[272,128]{1,0:T(8,128)(2,1)S(1)} %get-tuple-element.74), channel_id=1, source_target_pairs={{0,8},{4,12},{8,0},{12,4},{16,24},{20,28},{24,16},{28,20},{1,9},{5... | collective-permute-start | bytes 208904 | tf_op jit(solution)/shard_map/ppermute | solution.py:200
  35.7 2.2 %collective-permute-start.15 = (bf16[272,128]{1,0:T(8,128)(2,1)S(1)}, bf16[272,128]{1,0:T(8,128)(2,1)S(1)}, u32[]{:S(2)}, u32[]{:S(2)}) collective-permute-start(bf16[272,128]{1,0:T(8,128)(2,1)S(1)} %get-tuple-element.75), channel_id=1, source_target_pairs={{0,12},{4,8},{8,4},{12,0},{16,28},{20,24},{24,20},{28,16},{1,13},{... | collective-permute-start | bytes 208904 | tf_op jit(solution)/shard_map/ppermute | solution.py:200
  37.9 0.8 %collective-permute-done.13.rest_1_ = bf16[272,128]{1,0:T(8,128)(2,1)S(1)} collective-permute-done((bf16[272,128]{1,0:T(8,128)(2,1)S(1)}, bf16[272,128]{1,0:T(8,128)(2,1)S(1)}, u32[]{:S(2)}, u32[]{:S(2)}) %collective-permute-start.13) | collective-permute-done | bytes 69664 | tf_op jit(solution)/shard_map/ppermute | solution.py:200
  38.7 0.7 %collective-permute-done.14.rest_2_ = bf16[272,128]{1,0:T(8,128)(2,1)S(1)} collective-permute-done((bf16[272,128]{1,0:T(8,128)(2,1)S(1)}, bf16[272,128]{1,0:T(8,128)(2,1)S(1)}, u32[]{:S(2)}, u32[]{:S(2)}) %collective-permute-start.14) | collective-permute-done | bytes 69664 | tf_op jit(solution)/shard_map/ppermute | solution.py:200
  39.4 1.7 %collective-permute-done.15.rest_3_ = bf16[272,128]{1,0:T(8,128)(2,1)S(1)} collective-permute-done((bf16[272,128]{1,0:T(8,128)(2,1)S(1)}, bf16[272,128]{1,0:T(8,128)(2,1)S(1)}, u32[]{:S(2)}, u32[]{:S(2)}) %collective-permute-start.15) | collective-permute-done | bytes 69664 | tf_op jit(solution)/shard_map/ppermute | solution.py:200
  41.3 3.1 %collective-permute-start.16 = (bf16[272,128]{1,0:T(8,128)(2,1)S(1)}, bf16[272,128]{1,0:T(8,128)(2,1)S(1)}, u32[]{:S(2)}, u32[]{:S(2)}) collective-permute-start(bf16[272,128]{1,0:T(8,128)(2,1)S(1)} %get-tuple-element.76), channel_id=1, source_target_pairs={{0,16},{4,20},{8,24},{12,28},{16,0},{20,4},{24,8},{28,12},{1,17},{... | collective-permute-start | bytes 208904 | tf_op jit(solution)/shard_map/ppermute | solution.py:219
  44.4 2.3 %shard_map.101 = (f32[128,1024]{1,0:T(8,128)S(1)}, f32[128,1024]{1,0:T(8,128)S(1)}, f32[128,1024]{1,0:T(8,128)S(1)}) custom-call(s32[8,128]{1,0:T(8,128)S(1)} %get-tuple-element.45.codes_ref.rest_3_, bf16[128,1024]{1,0:T(8,128)(2,1)S(1)} %get-tuple-element.46.q_ref.rest_4_, bf16[128,1024]{1,0:T(8,128)(2,1)S(1)} %get-tuple-element.47.k_ref, ...), custom_call_target="tpu_custom_call" | custom-call | flops 134217728 | bytes 2883584 | tf_op jit(solution)/shard_map/pallas_call | solution.py:27
  46.7 1.7 %shard_map.102 = bf16[128,1024]{1,0:T(8,128)(2,1)} custom-call(s32[8,128]{1,0:T(8,128)S(1)} %get-tuple-element.45.codes_ref.rest_3_, f32[128,1024]{1,0:T(8,128)S(1)} %get-tuple-element.69.local_ref, bf16[128,1024]{1,0:T(8,128)(2,1)S(1)} %get-tuple-element.67.grad_ref, bf16[256,128]{1,0:T(8,128)(2,1)S(1)} %get-tuple-element.57.rest_0_, ...), custom_call_target="tpu_custom_call" | custom-call | flops 33554432 | bytes 1310720 | tf_op jit(solution)/shard_map/pallas_call | solution.py:27
  48.6 1.4 %collective-permute-start.18 = (bf16[256,128]{1,0:T(8,128)(2,1)S(1)}, bf16[256,128]{1,0:T(8,128)(2,1)S(1)}, u32[]{:S(2)}, u32[]{:S(2)}) collective-permute-start(bf16[256,128]{1,0:T(8,128)(2,1)S(1)} %get-tuple-element.80), channel_id=1, source_target_pairs={{0,8},{4,12},{8,0},{12,4},{16,24},{20,28},{24,16},{28,20},{1,9},{5... | collective-permute-start | bytes 196616 | tf_op jit(solution)/shard_map/ppermute | solution.py:200
  50.0 2.0 %collective-permute-start.19 = (bf16[256,128]{1,0:T(8,128)(2,1)S(1)}, bf16[256,128]{1,0:T(8,128)(2,1)S(1)}, u32[]{:S(2)}, u32[]{:S(2)}) collective-permute-start(bf16[256,128]{1,0:T(8,128)(2,1)S(1)} %get-tuple-element.81), channel_id=1, source_target_pairs={{0,12},{4,8},{8,4},{12,0},{16,28},{20,24},{24,20},{28,16},{1,13},{... | collective-permute-start | bytes 196616 | tf_op jit(solution)/shard_map/ppermute | solution.py:200
  52.0 0.7 %add_convert_fusion = bf16[128,768]{1,0:T(8,128)(2,1)} fusion(bf16[128,768]{1,0:T(8,128)(2,1)S(1)} %collective-permute-done.10, f32[128,768]{1,0:T(8,128)S(1)} %get-tuple-element.62, bf16[128,768]{1,0:T(8,128)(2,1)S(1)} %collective-permute-done.8), kind=kLoop, calls=%fused_computation | loop fusion | flops 491520 | bytes 983040 | tf_op jit(solution)/shard_map/convert_element_type | solution.py:493
  52.9 2.3 %collective-permute-done.19.rest_3_ = bf16[256,128]{1,0:T(8,128)(2,1)S(1)} collective-permute-done((bf16[256,128]{1,0:T(8,128)(2,1)S(1)}, bf16[256,128]{1,0:T(8,128)(2,1)S(1)}, u32[]{:S(2)}, u32[]{:S(2)}) %collective-permute-start.19) | collective-permute-done | bytes 65568 | tf_op jit(solution)/shard_map/ppermute | solution.py:200
  55.2 1.8 %shard_map.105 = (bf16[128,1024]{1,0:T(8,128)(2,1)}, bf16[128,1024]{1,0:T(8,128)(2,1)}) custom-call(s32[8,128]{1,0:T(8,128)S(1)} %get-tuple-element.45.codes_ref.rest_3_, bf16[128,1024]{1,0:T(8,128)(2,1)S(1)} %get-tuple-element.47.k_ref, bf16[128,1024]{1,0:T(8,128)(2,1)S(1)} %get-tuple-element.48.v_ref, f32[128,1024]{1,0:T(8,128)S(1)} %get-tuple-element.70.lk_ref, ...), custom_call_target="tpu_custom_call" | custom-call | flops 67108864 | bytes 2359296 | tf_op jit(solution)/shard_map/pallas_call | solution.py:27
  (23 shorter events, 1.3 us)
Async XLA Ops:
  0.6 25.7 %collective-permute-start = (bf16[128,768]{1,0:T(8,128)(2,1)}, bf16[128,768]{1,0:T(8,128)(2,1)S(1)}, u32[]{:S(2)}, u32[]{:S(2)}) collective-permute-start(bf16[128,768]{1,0:T(8,128)(2,1)} %first.1), channel_id=1, source_target_pairs={{0,1},{1,0},{2,3},{3,2},{4,5},{5,4},{6,7},{7,6},{8,9},{9,8},{10,11... | collective-permute-start | bytes 589832 | tf_op jit(solution)/shard_map/ppermute | solution.py:200
  3.8 5.4 %collective-permute-start.1 = (bf16[272,128]{1,0:T(8,128)(2,1)S(1)}, bf16[272,128]{1,0:T(8,128)(2,1)S(1)}, u32[]{:S(2)}, u32[]{:S(2)}) collective-permute-start(bf16[272,128]{1,0:T(8,128)(2,1)S(1)} %get-tuple-element.52), channel_id=1, source_target_pairs={{0,4},{4,0},{8,12},{12,8},{16,20},{20,16},{24,28},{28,24},{1,5},{5... | collective-permute-start | bytes 208904 | tf_op jit(solution)/shard_map/ppermute | solution.py:200
  6.4 4.5 %collective-permute-start.2 = (bf16[272,128]{1,0:T(8,128)(2,1)S(1)}, bf16[272,128]{1,0:T(8,128)(2,1)S(1)}, u32[]{:S(2)}, u32[]{:S(2)}) collective-permute-start(bf16[272,128]{1,0:T(8,128)(2,1)S(1)} %get-tuple-element.53), channel_id=1, source_target_pairs={{0,8},{4,12},{8,0},{12,4},{16,24},{20,28},{24,16},{28,20},{1,9},{5... | collective-permute-start | bytes 208904 | tf_op jit(solution)/shard_map/ppermute | solution.py:200
  8.0 5.2 %collective-permute-start.3 = (bf16[272,128]{1,0:T(8,128)(2,1)S(1)}, bf16[272,128]{1,0:T(8,128)(2,1)S(1)}, u32[]{:S(2)}, u32[]{:S(2)}) collective-permute-start(bf16[272,128]{1,0:T(8,128)(2,1)S(1)} %get-tuple-element.54), channel_id=1, source_target_pairs={{0,12},{4,8},{8,4},{12,0},{16,28},{20,24},{24,20},{28,16},{1,13},{... | collective-permute-start | bytes 208904 | tf_op jit(solution)/shard_map/ppermute | solution.py:200
  13.3 6.0 %collective-permute-start.4 = (bf16[272,128]{1,0:T(8,128)(2,1)S(1)}, bf16[272,128]{1,0:T(8,128)(2,1)S(1)}, u32[]{:S(2)}, u32[]{:S(2)}) collective-permute-start(bf16[272,128]{1,0:T(8,128)(2,1)S(1)} %get-tuple-element.55), channel_id=1, source_target_pairs={{0,16},{4,20},{8,24},{12,28},{16,0},{20,4},{24,8},{28,12},{1,17},{... | collective-permute-start | bytes 208904 | tf_op jit(solution)/shard_map/ppermute | solution.py:219
  19.4 10.6 %collective-permute-start.5 = (bf16[256,128]{1,0:T(8,128)(2,1)S(1)}, bf16[256,128]{1,0:T(8,128)(2,1)S(1)}, u32[]{:S(2)}, u32[]{:S(2)}) collective-permute-start(bf16[256,128]{1,0:T(8,128)(2,1)S(1)} %get-tuple-element.58), channel_id=1, source_target_pairs={{0,4},{4,0},{8,12},{12,8},{16,20},{20,16},{24,28},{28,24},{1,5},{5... | collective-permute-start | bytes 196616 | tf_op jit(solution)/shard_map/ppermute | solution.py:200
  19.5 10.5 %collective-permute-start.6 = (bf16[256,128]{1,0:T(8,128)(2,1)S(1)}, bf16[256,128]{1,0:T(8,128)(2,1)S(1)}, u32[]{:S(2)}, u32[]{:S(2)}) collective-permute-start(bf16[256,128]{1,0:T(8,128)(2,1)S(1)} %get-tuple-element.59), channel_id=1, source_target_pairs={{0,8},{4,12},{8,0},{12,4},{16,24},{20,28},{24,16},{28,20},{1,9},{5... | collective-permute-start | bytes 196616 | tf_op jit(solution)/shard_map/ppermute | solution.py:200
  20.8 9.2 %collective-permute-start.7 = (bf16[256,128]{1,0:T(8,128)(2,1)S(1)}, bf16[256,128]{1,0:T(8,128)(2,1)S(1)}, u32[]{:S(2)}, u32[]{:S(2)}) collective-permute-start(bf16[256,128]{1,0:T(8,128)(2,1)S(1)} %get-tuple-element.60), channel_id=1, source_target_pairs={{0,12},{4,8},{8,4},{12,0},{16,28},{20,24},{24,20},{28,16},{1,13},{... | collective-permute-start | bytes 196616 | tf_op jit(solution)/shard_map/ppermute | solution.py:200
  22.9 7.9 %collective-permute-start.11 = (bf16[128,768]{1,0:T(8,128)(2,1)}, bf16[128,768]{1,0:T(8,128)(2,1)S(1)}, u32[]{:S(2)}, u32[]{:S(2)}) collective-permute-start(bf16[128,768]{1,0:T(8,128)(2,1)} %first.1), channel_id=1, source_target_pairs={{0,2},{1,3},{2,0},{3,1},{4,6},{5,7},{6,4},{7,5},{8,10},{9,11},{10,... | collective-permute-start | bytes 589832 | tf_op jit(solution)/shard_map/ppermute | solution.py:200
  30.7 1.5 %collective-permute-start.9 = (bf16[128,768]{1,0:T(8,128)(2,1)S(1)}, bf16[128,768]{1,0:T(8,128)(2,1)S(1)}, u32[]{:S(2)}, u32[]{:S(2)}) collective-permute-start(bf16[128,768]{1,0:T(8,128)(2,1)S(1)} %get-tuple-element.65), channel_id=1, source_target_pairs={{0,1},{1,0},{2,3},{3,2},{4,5},{5,4},{6,7},{7,6},{8,9},{9,8},{10,11... | collective-permute-start | bytes 589832 | tf_op jit(solution)/shard_map/ppermute | solution.py:200
  30.8 2.0 %collective-permute-start.12 = (bf16[128,768]{1,0:T(8,128)(2,1)S(1)}, bf16[128,768]{1,0:T(8,128)(2,1)S(1)}, u32[]{:S(2)}, u32[]{:S(2)}) collective-permute-start(bf16[128,768]{1,0:T(8,128)(2,1)S(1)} %collective-permute-done.11.rest_0_), channel_id=1, source_target_pairs={{0,1},{1,0},{2,3},{3,2},{4,5},{5,4},{6,7},{7,6},{8,9},{9,8},{10,11... | collective-permute-start | bytes 589832 | tf_op jit(solution)/shard_map/ppermute | solution.py:200
  31.9 20.1 %collective-permute-start.8 = (bf16[128,768]{1,0:T(8,128)(2,1)S(1)}, bf16[128,768]{1,0:T(8,128)(2,1)S(1)}, u32[]{:S(2)}, u32[]{:S(2)}) collective-permute-start(bf16[128,768]{1,0:T(8,128)(2,1)S(1)} %get-tuple-element.63), channel_id=1, source_target_pairs={{0,1},{1,0},{2,3},{3,2},{4,5},{5,4},{6,7},{7,6},{8,9},{9,8},{10,11... | collective-permute-start | bytes 589832 | tf_op jit(solution)/shard_map/ppermute | solution.py:200
  32.3 19.7 %collective-permute-start.10 = (bf16[128,768]{1,0:T(8,128)(2,1)S(1)}, bf16[128,768]{1,0:T(8,128)(2,1)S(1)}, u32[]{:S(2)}, u32[]{:S(2)}) collective-permute-start(bf16[128,768]{1,0:T(8,128)(2,1)S(1)} %add_convert_fusion.1), channel_id=1, source_target_pairs={{0,2},{1,3},{2,0},{3,1},{4,6},{5,7},{6,4},{7,5},{8,10},{9,11},{10,... | collective-permute-start | bytes 589832 | tf_op jit(solution)/shard_map/ppermute | solution.py:200
  34.4 4.4 %collective-permute-start.13 = (bf16[272,128]{1,0:T(8,128)(2,1)S(1)}, bf16[272,128]{1,0:T(8,128)(2,1)S(1)}, u32[]{:S(2)}, u32[]{:S(2)}) collective-permute-start(bf16[272,128]{1,0:T(8,128)(2,1)S(1)} %get-tuple-element.73), channel_id=1, source_target_pairs={{0,4},{4,0},{8,12},{12,8},{16,20},{20,16},{24,28},{28,24},{1,5},{5... | collective-permute-start | bytes 208904 | tf_op jit(solution)/shard_map/ppermute | solution.py:200
  34.5 5.0 %collective-permute-start.14 = (bf16[272,128]{1,0:T(8,128)(2,1)S(1)}, bf16[272,128]{1,0:T(8,128)(2,1)S(1)}, u32[]{:S(2)}, u32[]{:S(2)}) collective-permute-start(bf16[272,128]{1,0:T(8,128)(2,1)S(1)} %get-tuple-element.74), channel_id=1, source_target_pairs={{0,8},{4,12},{8,0},{12,4},{16,24},{20,28},{24,16},{28,20},{1,9},{5... | collective-permute-start | bytes 208904 | tf_op jit(solution)/shard_map/ppermute | solution.py:200
  35.7 5.4 %collective-permute-start.15 = (bf16[272,128]{1,0:T(8,128)(2,1)S(1)}, bf16[272,128]{1,0:T(8,128)(2,1)S(1)}, u32[]{:S(2)}, u32[]{:S(2)}) collective-permute-start(bf16[272,128]{1,0:T(8,128)(2,1)S(1)} %get-tuple-element.75), channel_id=1, source_target_pairs={{0,12},{4,8},{8,4},{12,0},{16,28},{20,24},{24,20},{28,16},{1,13},{... | collective-permute-start | bytes 208904 | tf_op jit(solution)/shard_map/ppermute | solution.py:200
  41.3 7.1 %collective-permute-start.16 = (bf16[272,128]{1,0:T(8,128)(2,1)S(1)}, bf16[272,128]{1,0:T(8,128)(2,1)S(1)}, u32[]{:S(2)}, u32[]{:S(2)}) collective-permute-start(bf16[272,128]{1,0:T(8,128)(2,1)S(1)} %get-tuple-element.76), channel_id=1, source_target_pairs={{0,16},{4,20},{8,24},{12,28},{16,0},{20,4},{24,8},{28,12},{1,17},{... | collective-permute-start | bytes 208904 | tf_op jit(solution)/shard_map/ppermute | solution.py:219
  48.5 4.3 %collective-permute-start.17 = (bf16[256,128]{1,0:T(8,128)(2,1)S(1)}, bf16[256,128]{1,0:T(8,128)(2,1)S(1)}, u32[]{:S(2)}, u32[]{:S(2)}) collective-permute-start(bf16[256,128]{1,0:T(8,128)(2,1)S(1)} %get-tuple-element.79), channel_id=1, source_target_pairs={{0,4},{4,0},{8,12},{12,8},{16,20},{20,16},{24,28},{28,24},{1,5},{5... | collective-permute-start | bytes 196616 | tf_op jit(solution)/shard_map/ppermute | solution.py:200
  48.6 4.3 %collective-permute-start.18 = (bf16[256,128]{1,0:T(8,128)(2,1)S(1)}, bf16[256,128]{1,0:T(8,128)(2,1)S(1)}, u32[]{:S(2)}, u32[]{:S(2)}) collective-permute-start(bf16[256,128]{1,0:T(8,128)(2,1)S(1)} %get-tuple-element.80), channel_id=1, source_target_pairs={{0,8},{4,12},{8,0},{12,4},{16,24},{20,28},{24,16},{28,20},{1,9},{5... | collective-permute-start | bytes 196616 | tf_op jit(solution)/shard_map/ppermute | solution.py:200
  50.0 5.2 %collective-permute-start.19 = (bf16[256,128]{1,0:T(8,128)(2,1)S(1)}, bf16[256,128]{1,0:T(8,128)(2,1)S(1)}, u32[]{:S(2)}, u32[]{:S(2)}) collective-permute-start(bf16[256,128]{1,0:T(8,128)(2,1)S(1)} %get-tuple-element.81), channel_id=1, source_target_pairs={{0,12},{4,8},{8,4},{12,0},{16,28},{20,24},{24,20},{28,16},{1,13},{... | collective-permute-start | bytes 196616 | tf_op jit(solution)/shard_map/ppermute | solution.py:200

commit v3 on v2

v3 whole, which is shorter than its diff:
```python
import functools

import jax
import jax.numpy as jnp
from jax import lax
from jax.experimental import pallas as pl
from jax.experimental.pallas import tpu as pltpu
from jax.sharding import PartitionSpec as P


F32 = jnp.float32
BF16 = jnp.bfloat16
VMEM = pl.BlockSpec(memory_space=pltpu.VMEM)
SMEM = pl.BlockSpec(memory_space=pltpu.SMEM)
HBM = pl.BlockSpec(memory_space=pltpu.HBM)


def dot(a, b, ca, cb):
    return lax.dot_general(a, b, (((ca,), (cb,)), ((), ())), preferred_element_type=F32)


def aligned(index, size):
    return pl.ds(pl.multiple_of(index * size, size), size)


def call(kernel, outs, specs, args, scratch=(), limit=16, out_specs=None):
    return pl.pallas_call(
        kernel,
        out_shape=outs,
        in_specs=specs,
        out_specs=out_specs or [VMEM] * len(outs),
        scratch_shapes=list(scratch),
        compiler_params=pltpu.CompilerParams(vmem_limit_bytes=limit << 20),
        cost_estimate=pl.CostEstimate(flops=2_400_000_000, bytes_accessed=8_000_000, transcendentals=0),
    )(*args)


def in_hbm(array):
    return pltpu.with_memory_space_constraint(array, pltpu.HBM)


def shape(dims, dtype):
    return jax.ShapeDtypeStruct(dims, dtype)


def running_log(codes):
    rest = jnp.log(1.0 - codes.astype(F32) / 4096.0)
    size = (codes.shape[1], codes.shape[1])
    place, other = (lax.broadcasted_iota(jnp.int32, size, axis) for axis in (0, 1))
    lower = (other <= place).astype(F32).astype(BF16)
    columns = rows = None
    for _ in range(3):
        part = rest.astype(BF16)
        rest = rest - part.astype(F32)
        column, row = dot(lower, part, 1, 1), dot(part, lower, 1, 1)
        columns = column if columns is None else columns + column
        rows = row if rows is None else rows + row
    return columns, rows


def positions(plan, way):
    place = lax.axis_index("seq")
    turn = place if way > 0 else plan.seq - 1 - place
    return lax.rem(turn, plan.group), lax.div(turn, plan.group)


class Plan:
    def __init__(self, tok, heads, width, seq):
        self.tok, self.heads, self.width, self.seq = tok, heads, width, seq
        self.group = next(g for g in (4, 2, 1) if heads % g == 0 and seq % g == 0)
        self.groups = seq // self.group
        self.quarter = heads // self.group
        self.half_tail = 8 * pl.cdiv(self.quarter, 8)
        self.tail = 2 * self.half_tail
        self.body = self.quarter * width
        self.rows = self.body + self.tail


def tail_rows(plan, totals):
    place = lax.broadcasted_iota(jnp.int32, (plan.tail, plan.width), 0)
    rows = jnp.zeros((plan.tail, plan.width), F32)
    for i, total in enumerate(totals):
        high = total.astype(BF16).astype(F32)
        rows = jnp.where(place == i, high, rows)
        rows = jnp.where(place == plan.half_tail + i, total - high, rows)
    return rows


def read_tail(plan, ref, base, i):
    at = base + plan.body + i
    return ref[at : at + 1, :] + ref[at + plan.half_tail : at + plan.half_tail + 1, :]


def put_summaries(plan, rank, left, right, cum, outs, scratch, arrive=None):
    width = plan.width
    last = jnp.exp(cum[plan.tok - 1 : plan.tok, :])
    for q in range(plan.group):
        base = q * plan.rows
        totals = []
        if arrive is not None:
            arrive(q)
        for i in range(plan.quarter):
            h = q * plan.quarter + i
            scratch[base + i * width : base + (i + 1) * width, :] = dot(left(h), right(h), 0, 0)
            totals.append(jnp.broadcast_to(last[:, h : h + 1], (1, width)))
        scratch[base + plan.body : base + plan.rows, :] = tail_rows(plan, totals)
    outs[0][...] = scratch[aligned(rank, plan.rows), :]
    for j in range(1, plan.group):
        outs[j][...] = scratch[aligned(rank ^ j, plan.rows), :].astype(BF16)


def summary_shapes(plan):
    rows = (plan.rows, plan.width)
    return [shape(rows, F32)] + [shape(rows, BF16)] * (plan.group - 1)


def summary_scratch(plan):
    return pltpu.VMEM((plan.group * plan.rows, plan.width), F32)


def first_kernel(plan, codes, keys, values, queries, *refs):
    outs, refs = refs[: plan.group], refs[plan.group :]
    cum_ref, cum_t_ref, rise_ref, fall_ref, k_fall_ref, k_ref, v_ref, q_ref = refs[:8]
    scratch, codes_ref, sems = refs[8:]
    loads = []

    def load(src, dst):
        copy = pltpu.make_async_copy(src, dst, sems.at[len(loads)])
        copy.start()
        loads.append(copy)
        return copy

    wide = plan.quarter * plan.width
    codes_load = load(codes, codes_ref)
    pieces = []
    for q in range(plan.group):
        at = slice(q * wide, (q + 1) * wide)
        pieces.append((load(keys.at[:, at], k_ref.at[:, at]), load(values.at[:, at], v_ref.at[:, at])))
    late = [load(queries, q_ref)]

    codes_load.wait()
    cum, cum_t = running_log(codes_ref[...])
    fall = jnp.exp(cum[plan.tok - 1 : plan.tok, :] - cum)
    cum_ref[...], cum_t_ref[...] = cum, cum_t
    rise_ref[...] = (1.0 / plan.width) * jnp.exp(cum)
    fall_ref[...] = fall

    def cols(h):
        return slice(h * plan.width, (h + 1) * plan.width)

    def arrive(q):
        for piece in pieces[q]:
            piece.wait()

    def left(h):
        k_fall = (fall[:, h : h + 1] * k_ref[:, cols(h)].astype(F32)).astype(BF16)
        k_fall_ref[:, cols(h)] = k_fall
        return k_fall

    rank = positions(plan, 1)[0]
    put_summaries(plan, rank, left, lambda h: v_ref[:, cols(h)], cum, outs, scratch, arrive)
    for copy in late:
        copy.wait()


def combine_kernel(plan, way, *rest):
    group, width = plan.group, plan.width
    ins, (pre_ref, total_ref, scratch) = rest[:group], rest[group:]
    rank = positions(plan, way)[0]
    for j in range(group):
        scratch[aligned(rank ^ j, plan.rows), :] = ins[j][...].astype(F32)
    decays = []
    for i in range(plan.quarter):
        held = jnp.zeros((width, width), F32)
        decay = jnp.ones((1, width), F32)
        per_member = []
        for m in range(group):
            base = m * plan.rows
            at = slice(base + i * width, base + (i + 1) * width)
            pre_ref[at, :] = held
            per_member.append(decay)
            total = read_tail(plan, scratch, base, i)
            held = total * held + scratch[at, :]
            decay = decay * total
        decays.append(per_member + [decay])
        total_ref[i * width : (i + 1) * width, :] = held.astype(BF16)
    for m in range(group):
        base = m * plan.rows + plan.body
        pre_ref[base : base + plan.tail, :] = tail_rows(plan, [d[m] for d in decays])
    total_ref[plan.body : plan.rows, :] = tail_rows(plan, [d[group] for d in decays]).astype(BF16)


def spread_kernel(plan, way, entry_ref, pre_ref, *rest):
    group, width = plan.group, plan.width
    outs, scratch = rest[:group], rest[group]
    rank, turn = positions(plan, way)
    enters = turn > 0
    for i in range(plan.quarter):
        at = slice(i * width, (i + 1) * width)
        entry = jnp.where(enters, entry_ref[at, :].astype(F32), 0.0)
        for m in range(group):
            base = m * plan.rows
            state = read_tail(plan, pre_ref, base, i) * entry
            state = state + pre_ref[base + i * width : base + (i + 1) * width, :]
            to = m * plan.body + i * width
            scratch[to : to + width, :] = state.astype(BF16)
    for j in range(group):
        outs[j][...] = scratch[aligned(rank ^ j, plan.body), :]


def swap(value, axis, offset):
    count = lax.axis_size(axis)
    return lax.ppermute(value, axis, [(i, i ^ offset) for i in range(count)])


def join(plan, earlier, later):
    earlier, later = earlier.astype(F32), later.astype(F32)
    bodies, totals = [], []
    for i in range(plan.quarter):
        at = slice(i * plan.width, (i + 1) * plan.width)
        mine = read_tail(plan, later, 0, i)
        bodies.append(mine * earlier[at] + later[at])
        totals.append(mine * read_tail(plan, earlier, 0, i))
    return jnp.concatenate(bodies + [tail_rows(plan, totals)]).astype(BF16)


def group_entry(plan, total, way, turn):
    count, span = plan.seq, plan.group

    def shift(value, by):
        hop = way * by * span
        return lax.ppermute(value, "seq", [(i, (i + hop) % count) for i in range(count)])

    entry = shift(total, 1)
    by = 1
    while by < plan.groups - 1:
        entry = jnp.where(turn > by, join(plan, shift(entry, by), entry), entry)
        by *= 2
    return entry


def scan_states(plan, summaries, way):
    turn = positions(plan, way)[1]
    others = range(1, plan.group)
    got = [summaries[0]] + [swap(summaries[j], "seq", j) for j in others]
    rows, body = (plan.rows, plan.width), (plan.body, plan.width)
    pre, total = call(
        functools.partial(combine_kernel, plan, way),
        [shape((plan.group * plan.rows, plan.width), F32), shape(rows, BF16)],
        [VMEM] * plan.group,
        got,
        [pltpu.VMEM((plan.group * plan.rows, plan.width), F32)],
    )
    entry = group_entry(plan, total, way, turn)
    states = call(
        functools.partial(spread_kernel, plan, way),
        [shape(body, BF16)] * plan.group,
        [VMEM, VMEM],
        [entry, pre],
        [pltpu.VMEM((plan.group * plan.body, plan.width), BF16)],
    )
    return [states[0]] + [swap(states[j], "seq", j) for j in others]


def gather_states(plan, way, ins, scratch):
    rank = positions(plan, way)[0]
    for j in range(plan.group):
        scratch[aligned(rank ^ j, plan.body), :] = ins[j][...]


def weight_columns(offset, width):
    return aligned(lax.axis_index("head") ^ offset, width)


def grad_sum(offsets, shards, weight_ref, total=None):
    for offset, shard in zip(offsets, shards):
        part = dot(shard[...], weight_ref[:, weight_columns(offset, shard.shape[1])], 1, 1)
        total = part if total is None else total + part
    return total


def near_grad_kernel(offsets, weight_ref, *rest):
    rest[-1][...] = grad_sum(offsets, rest[:-1], weight_ref)


def grad_kernel(plan, offsets, weight_ref, *rest):
    count = len(offsets)
    shards, (part_ref, cum_ref, rise_ref, q_ref) = rest[:count], rest[count : count + 4]
    grad_ref, q_rise_ref = rest[count + 4 : count + 6]
    outs, scratch = rest[count + 6 : -1], rest[-1]
    grad_ref[...] = grad_sum(offsets, shards, weight_ref, part_ref[...]).astype(BF16)

    def cols(h):
        return slice(h * plan.width, (h + 1) * plan.width)

    def left(h):
        q_rise = (rise_ref[:, h : h + 1] * q_ref[:, cols(h)].astype(F32)).astype(BF16)
        q_rise_ref[:, cols(h)] = q_rise
        return q_rise

    rank = positions(plan, -1)[0]
    put_summaries(plan, rank, left, lambda h: grad_ref[:, cols(h)], cum_ref[...], outs, scratch)


def local_kernel(plan, cum_ref, cum_t_ref, rise_ref, fall_ref, q_ref, k_ref, v_ref, grad_ref, *outs):
    out_ref, lq_ref, lk_ref, lv_ref, g_rise_ref, v_fall_ref = outs
    scale = 1.0 / plan.width
    size = (plan.tok, plan.tok)
    lower = lax.broadcasted_iota(jnp.int32, size, 0) >= lax.broadcasted_iota(jnp.int32, size, 1)
    for h in range(plan.heads):
        at = slice(h * plan.width, (h + 1) * plan.width)
        gap = cum_ref[:, h : h + 1] - cum_t_ref[h : h + 1, :]
        mask = jnp.where(lower, jnp.exp(jnp.where(lower, gap, 0.0)), 0.0)
        q, k, v, grad = q_ref[:, at], k_ref[:, at], v_ref[:, at], grad_ref[:, at]
        attn = (scale * dot(q, k, 1, 1) * mask).astype(BF16)
        pmat = (scale * dot(grad, v, 1, 1) * mask).astype(BF16)
        out_ref[:, at] = dot(attn, v, 1, 0)
        lq_ref[:, at] = dot(pmat, k, 1, 0)
        lk_ref[:, at] = dot(pmat, q, 0, 0)
        lv_ref[:, at] = dot(attn, grad, 0, 0)
        g_rise_ref[:, at] = (rise_ref[:, h : h + 1] * grad.astype(F32)).astype(BF16)
        v_fall_ref[:, at] = (fall_ref[:, h : h + 1] * v.astype(F32)).astype(BF16)


def mix(offsets, weight_ref, flat_ref, outs):
    for offset, out in zip(offsets, outs):
        columns = weight_ref[:, weight_columns(offset, out.shape[1])]
        out[...] = dot(flat_ref[...], columns, 1, 0).astype(out.dtype)


def mix_first_kernel(plan, offsets, weight_ref, local_ref, rise_ref, *rest):
    ins, (flat_ref, *outs, states) = rest[: plan.group], rest[plan.group :]
    gather_states(plan, 1, ins, states)
    for h in range(plan.heads):
        at = slice(h * plan.width, (h + 1) * plan.width)
        cross = dot(rise_ref[:, at], states[at, :], 1, 0)
        flat_ref[:, at] = (local_ref[:, at] + cross).astype(BF16)
    mix(offsets, weight_ref, flat_ref, outs)


def near_mix_kernel(plan, offsets, weight_ref, flat_ref, lq_ref, g_rise_ref, *rest):
    ins, rest = rest[: plan.group], rest[plan.group :]
    query_grad, outs, (states, buffer, sems) = rest[0], rest[1:-3], rest[-3:]
    gather_states(plan, 1, ins, states)
    wide = plan.quarter * plan.width
    copies = []
    for h in range(plan.heads):
        at = slice(h * plan.width, (h + 1) * plan.width)
        cross = dot(g_rise_ref[:, at], states[at, :], 1, 1)
        buffer[:, at] = (lq_ref[:, at] + cross).astype(BF16)
        if (h + 1) % plan.quarter == 0:
            q = h // plan.quarter
            at = slice(q * wide, (q + 1) * wide)
            copies.append(pltpu.make_async_copy(buffer.at[:, at], query_grad.at[:, at], sems.at[q]))
            copies[-1].start()
    mix(offsets, weight_ref, flat_ref, outs)
    for copy in copies:
        copy.wait()


def last_kernel(plan, k_fall_ref, v_fall_ref, lk_ref, lv_ref, *rest):
    ins, rest = rest[: plan.group], rest[plan.group :]
    parts, (mixed, key_grad, value_grad) = rest[:3], rest[3:6]
    states, mixed_buffer, key_buffer, value_buffer, sems = rest[6:]
    copies = []

    def send(src, dst):
        copies.append(pltpu.make_async_copy(src, dst, sems.at[len(copies)]))
        copies[-1].start()

    mixed_buffer[...] = sum(part[...].astype(F32) for part in parts).astype(BF16)
    send(mixed_buffer, mixed)
    gather_states(plan, -1, ins, states)
    wide = plan.quarter * plan.width
    for h in range(plan.heads):
        at = slice(h * plan.width, (h + 1) * plan.width)
        carry = states[at, :]
        key_buffer[:, at] = (lk_ref[:, at] + dot(v_fall_ref[:, at], carry, 1, 1)).astype(BF16)
        value_buffer[:, at] = (lv_ref[:, at] + dot(k_fall_ref[:, at], carry, 1, 0)).astype(BF16)
        if (h + 1) % plan.quarter == 0:
            q = h // plan.quarter
            at = slice(q * wide, (q + 1) * wide)
            send(key_buffer.at[:, at], key_grad.at[:, at])
            send(value_buffer.at[:, at], value_grad.at[:, at])
    for copy in copies:
        copy.wait()


def local(queries, keys, values, decay_codes, out_weight, out_grad):
    tok, flat = queries.shape
    heads = decay_codes.shape[1]
    plan = Plan(tok, heads, flat // heads, lax.axis_size("seq"))
    across, feat = lax.axis_size("head"), out_grad.shape[1]
    codes = decay_codes.T
    half = across // 2
    wide = (tok, flat)

    shards = {0: out_grad}
    hop = half
    while hop:
        for o, part in list(shards.items()):
            shards[o ^ hop] = swap(part, "head", hop)
        hop //= 2

    heads_by = (tok, heads)
    weight = out_weight
    wide_bf = shape(wide, BF16)
    offsets = list(range(across))
    *summaries, cum, cum_t, rise, fall, k_fall, keys, values, queries = call(
        functools.partial(first_kernel, plan),
        summary_shapes(plan)
        + [shape(d, F32) for d in (heads_by, heads_by[::-1], heads_by, heads_by)]
        + [wide_bf] * 4,
        [HBM] * 4,
        [in_hbm(x) for x in (codes, keys, values, queries)],
        [
            summary_scratch(plan),
            pltpu.VMEM(codes.shape, codes.dtype),
            pltpu.SemaphoreType.DMA((2 * plan.group + 2,)),
        ],
    )
    states = scan_states(plan, summaries, 1)

    (part,) = call(
        functools.partial(near_grad_kernel, offsets[:half]),
        [shape(wide, F32)],
        [VMEM] * (1 + half),
        [weight] + [shards[o] for o in offsets[:half]],
    )
    grad, q_rise, *summaries_back = call(
        functools.partial(grad_kernel, plan, offsets[half:]),
        [wide_bf] * 2 + summary_shapes(plan),
        [VMEM] * (half + 5),
        [weight] + [shards[o] for o in offsets[half:]] + [part, cum, rise, queries],
        [summary_scratch(plan)],
    )
    carries = scan_states(plan, summaries_back, -1)

    local_out, local_q, local_k, local_v, g_rise, v_fall = call(
        functools.partial(local_kernel, plan),
        [shape(wide, F32)] * 4 + [wide_bf] * 2,
        [VMEM] * 8,
        [cum, cum_t, rise, fall, queries, keys, values, grad],
    )

    held = pltpu.VMEM((flat, plan.width), BF16)
    far, near = offsets[half:][::-1], offsets[:half][::-1]
    attn_out, *sent = call(
        functools.partial(mix_first_kernel, plan, far),
        [wide_bf] + [shape((tok, feat), BF16)] * half,
        [VMEM] * (3 + plan.group),
        [weight, local_out, q_rise] + states,
        [held],
    )
    query_grad, *kept = call(
        functools.partial(near_mix_kernel, plan, near),
        [wide_bf] + [shape((tok, feat), F32 if o == 0 else BF16) for o in near],
        [VMEM] * (4 + plan.group),
        [weight, attn_out, local_q, g_rise] + states,
        [held, pltpu.VMEM(wide, BF16), pltpu.SemaphoreType.DMA((plan.group,))],
        out_specs=[HBM] + [VMEM] * half,
    )

    def move(parts, hop):
        return {o: swap(part, "head", hop) for o, part in parts.items() if o & hop}

    def halve(parts, hop):
        moved = move(parts, hop)
        return {
            o: (part.astype(F32) + moved[o | hop].astype(F32)).astype(F32 if o == 0 else BF16)
            for o, part in parts.items()
            if not o & hop
        }

    far_parts, near_parts = dict(zip(far, sent)), dict(zip(near, kept))
    hop = 1
    while hop < half:
        far_parts = halve(far_parts, hop)
        if 2 * hop < half:
            near_parts = halve(near_parts, hop)
        hop *= 2
    last_parts = [near_parts[0], move(near_parts, half // 2)[half // 2], move(far_parts, half)[half]]

    mixed, key_grad, value_grad = call(
        functools.partial(last_kernel, plan),
        [shape((tok, feat), BF16)] + [wide_bf] * 2,
        [VMEM] * (7 + plan.group),
        [k_fall, v_fall, local_k, local_v] + carries + last_parts,
        [held, pltpu.VMEM((tok, feat), BF16)]
        + [pltpu.VMEM(wide, BF16)] * 2
        + [pltpu.SemaphoreType.DMA((2 * plan.group + 1,))],
        out_specs=[HBM] * 3,
    )
    return mixed, query_grad, key_grad, value_grad


def solution(mesh):
    whole = P("seq", "head")

    return jax.shard_map(
        local,
        mesh=mesh,
        in_specs=(whole, whole, whole, whole, P("head", None), whole),
        out_specs=(whole,) * 4,
        check_vma=False,
    )
```

time: 57.2 us -> 48.8 us (0.85)
  Pallas kernels: 17.1 us -> 10.2 us
  waiting for transfers between devices: 14.4 us -> 12.6 us
  starting transfers between devices: 23.9 us -> 24.9 us
  other arithmetic: 0.79 us -> 0.05 us
    pallas_call x13 -> x11, Pallas kernels: 17.1 us -> 10.2 us  [call(): pl.pallas_call(kernel, out_shape=outs, in_specs=specs, out_specs=out_spec...]
    ppermute x2, waiting for transfers between devices: 3.37 us -> 2.41 us  [shift(): lax.ppermute(value, 'seq', [(i, (i + hop) % count) for i in range(count)])]
    ppermute x18, waiting for transfers between devices: 11.1 us -> 10.2 us  [swap(): return lax.ppermute(value, axis, [(i, i ^ offset) for i in range(count)])]
    ppermute x18, starting transfers between devices: 18.2 us -> 19 us  [swap(): return lax.ppermute(value, axis, [(i, i ^ offset) for i in range(count)])]
    convert_element_type x1 -> x0, other arithmetic: 0.74 us -> none  [local(): mixed = halve({**far_parts, **near_parts}, half)[0].astype(BF16)]
  transfers between devices with their start and end apart: 20 -> 20, of which waited for: 10 -> 10; matrix products, arithmetic and copies ran while one was open for 1% -> 0% of each run, Pallas kernels for 27% -> 14%
where the time goes in v3:
time: 48.8 us; the launch traced here: 48.6 us
  starting transfers between devices  24.9 us (51%)
  waiting for transfers between devices  12.6 us (26%)
  Pallas kernels  10.2 us (21%)
  between operations  0.77 us (2%)
    ppermute x18, starting transfers between devices, swap(): return lax.ppermute(value, axis, [(i, i ^ offset) for i in range(count)])  19 us
    pallas_call x11, Pallas kernels, call(): pl.pallas_call(kernel, out_shape=outs, in_specs=specs, out_specs=out_spec...  10.2 us
    ppermute x18, waiting for transfers between devices, swap(): return lax.ppermute(value, axis, [(i, i ^ offset) for i in range(count)])  10.2 us
    ppermute x2, starting transfers between devices, shift(): lax.ppermute(value, 'seq', [(i, (i + hop) % count) for i in range(count)])  5.95 us
    ppermute x2, waiting for transfers between devices, shift(): lax.ppermute(value, 'seq', [(i, (i + hop) % count) for i in range(count)])  2.41 us
  transfers between devices with their start and end apart: 20, of which 10 were waited for; matrix products, arithmetic and copies ran while one was open for 0% of the time, Pallas kernels for 14%

profile of v3, /device:TPU:0, one launch (start us, length us, event | category | flops | bytes accessed | tf_op | source)
XLA Modules:
  0.0 48.6 jit_solution(15841907623186478188)
XLA Ops:
  0.6 2.2 %shard_map.93 = (f32[272,128]{1,0:T(8,128)S(1)}, bf16[272,128]{1,0:T(8,128)(2,1)S(1)}, bf16[272,128]{1,0:T(8,128)(2,1)S(1)}, bf16[272,128]{1,0:T(8,128)(2,1)S(1)...) custom-call(s32[8,128]{1,0:T(8,128)} %bitcast.3, ...), custom_call_target="tpu_custom_call" | custom-call | flops 2400000000 | bytes 8000000 | tf_op jit(solution)/shard_map/pallas_call | solution.py:27
  2.9 3.0 %collective-permute-start.10 = (bf16[272,128]{1,0:T(8,128)(2,1)S(1)}, bf16[272,128]{1,0:T(8,128)(2,1)S(1)}, u32[]{:S(2)}, u32[]{:S(2)}) collective-permute-start(bf16[272,128]{1,0:T(8,128)(2,1)S(1)} %get-tuple-element.74), channel_id=1, source_target_pairs={{0,4},{4,0},{8,12},{12,8},{16,20},{20,16},{24,28},{28,24},{1,5},{5... | collective-permute-start | bytes 208904 | tf_op jit(solution)/shard_map/ppermute | solution.py:213
  5.9 1.6 %collective-permute-start.11 = (bf16[272,128]{1,0:T(8,128)(2,1)S(1)}, bf16[272,128]{1,0:T(8,128)(2,1)S(1)}, u32[]{:S(2)}, u32[]{:S(2)}) collective-permute-start(bf16[272,128]{1,0:T(8,128)(2,1)S(1)} %get-tuple-element.75), channel_id=1, source_target_pairs={{0,8},{4,12},{8,0},{12,4},{16,24},{20,28},{24,16},{28,20},{1,9},{5... | collective-permute-start | bytes 208904 | tf_op jit(solution)/shard_map/ppermute | solution.py:213
  7.5 0.7 %collective-permute-done.10.rest_1_ = bf16[272,128]{1,0:T(8,128)(2,1)S(1)} collective-permute-done((bf16[272,128]{1,0:T(8,128)(2,1)S(1)}, bf16[272,128]{1,0:T(8,128)(2,1)S(1)}, u32[]{:S(2)}, u32[]{:S(2)}) %collective-permute-start.10) | collective-permute-done | bytes 69664 | tf_op jit(solution)/shard_map/ppermute | solution.py:213
  8.2 2.6 %collective-permute-done.11.rest_2_ = bf16[272,128]{1,0:T(8,128)(2,1)S(1)} collective-permute-done((bf16[272,128]{1,0:T(8,128)(2,1)S(1)}, bf16[272,128]{1,0:T(8,128)(2,1)S(1)}, u32[]{:S(2)}, u32[]{:S(2)}) %collective-permute-start.11) | collective-permute-done | bytes 69664 | tf_op jit(solution)/shard_map/ppermute | solution.py:213
  10.8 1.9 %collective-permute-done.12.rest_3_ = bf16[272,128]{1,0:T(8,128)(2,1)S(1)} collective-permute-done((bf16[272,128]{1,0:T(8,128)(2,1)S(1)}, bf16[272,128]{1,0:T(8,128)(2,1)S(1)}, u32[]{:S(2)}, u32[]{:S(2)}) %collective-permute-start.12) | collective-permute-done | bytes 69664 | tf_op jit(solution)/shard_map/ppermute | solution.py:213
  12.8 2.7 %collective-permute-start.13 = (bf16[272,128]{1,0:T(8,128)(2,1)S(1)}, bf16[272,128]{1,0:T(8,128)(2,1)S(1)}, u32[]{:S(2)}, u32[]{:S(2)}) collective-permute-start(bf16[272,128]{1,0:T(8,128)(2,1)S(1)} %get-tuple-element.77), channel_id=1, source_target_pairs={{0,16},{4,20},{8,24},{12,28},{16,0},{20,4},{24,8},{28,12},{1,17},{... | collective-permute-start | bytes 208904 | tf_op jit(solution)/shard_map/ppermute | solution.py:232
  15.4 1.5 %collective-permute-start = (bf16[128,768]{1,0:T(8,128)(2,1)S(1)}, bf16[128,768]{1,0:T(8,128)(2,1)S(1)}, u32[]{:S(2)}, u32[]{:S(2)}) collective-permute-start(bf16[128,768]{1,0:T(8,128)(2,1)S(1)} %copy-done), channel_id=1, source_target_pairs={{0,2},{1,3},{2,0},{3,1},{4,6},{5,7},{6,4},{7,5},{8,10},{9,11},{10,... | collective-permute-start | bytes 589832 | tf_op jit(solution)/shard_map/ppermute | solution.py:213
  17.0 1.7 %collective-permute-done.13.entry_ref = bf16[272,128]{1,0:T(8,128)(2,1)S(1)} collective-permute-done((bf16[272,128]{1,0:T(8,128)(2,1)S(1)}, bf16[272,128]{1,0:T(8,128)(2,1)S(1)}, u32[]{:S(2)}, u32[]{:S(2)}) %collective-permute-start.13) | collective-permute-done | bytes 69664 | tf_op jit(solution)/shard_map/ppermute | solution.py:232
  18.8 0.7 %collective-permute-start.14 = (bf16[256,128]{1,0:T(8,128)(2,1)S(1)}, bf16[256,128]{1,0:T(8,128)(2,1)S(1)}, u32[]{:S(2)}, u32[]{:S(2)}) collective-permute-start(bf16[256,128]{1,0:T(8,128)(2,1)S(1)} %get-tuple-element.80), channel_id=1, source_target_pairs={{0,4},{4,0},{8,12},{12,8},{16,20},{20,16},{24,28},{28,24},{1,5},{5... | collective-permute-start | bytes 196616 | tf_op jit(solution)/shard_map/ppermute | solution.py:213
  19.5 0.2 collective-permute-start.15
  19.7 2.6 %collective-permute-start.16 = (bf16[256,128]{1,0:T(8,128)(2,1)S(1)}, bf16[256,128]{1,0:T(8,128)(2,1)S(1)}, u32[]{:S(2)}, u32[]{:S(2)}) collective-permute-start(bf16[256,128]{1,0:T(8,128)(2,1)S(1)} %get-tuple-element.82), channel_id=1, source_target_pairs={{0,12},{4,8},{8,4},{12,0},{16,28},{20,24},{24,20},{28,16},{1,13},{... | collective-permute-start | bytes 196616 | tf_op jit(solution)/shard_map/ppermute | solution.py:213
  22.4 1.2 %shard_map.94.rest_2_ = f32[128,1024]{1,0:T(8,128)S(1)} custom-call(bf16[1024,3072]{1,0:T(8,128)(2,1)S(1)} %bitcast.2, bf16[128,768]{1,0:T(8,128)(2,1)S(1)} %copy-done, bf16[128,768]{1,0:T(8,128)(2,1)S(1)} %collective-permute-done.2.rest_1_), custom_call_target="tpu_custom_call" | custom-call | flops 2400000000 | bytes 8000000 | tf_op jit(solution)/shard_map/pallas_call | solution.py:27
  23.6 0.2 collective-permute-done.1.rest_1_
  23.8 1.4 %shard_map.95 = (bf16[128,1024]{1,0:T(8,128)(2,1)S(1)}, bf16[128,1024]{1,0:T(8,128)(2,1)S(1)}, f32[272,128]{1,0:T(8,128)S(1)}, bf16[272,128]{1,0:T(8,128)(2,1)S(...) custom-call(bf16[1024,3072]{1,0:T(8,128)(2,1)S(1)} %bitcast.2, ...), custom_call_target="tpu_custom_call" | custom-call | flops 2400000000 | bytes 8000000 | tf_op jit(solution)/shard_map/pallas_call | solution.py:27
  25.2 0.7 %collective-permute-start.3 = (bf16[272,128]{1,0:T(8,128)(2,1)S(1)}, bf16[272,128]{1,0:T(8,128)(2,1)S(1)}, u32[]{:S(2)}, u32[]{:S(2)}) collective-permute-start(bf16[272,128]{1,0:T(8,128)(2,1)S(1)} %get-tuple-element.62), channel_id=1, source_target_pairs={{0,4},{4,0},{8,12},{12,8},{16,20},{20,16},{24,28},{28,24},{1,5},{5... | collective-permute-start | bytes 208904 | tf_op jit(solution)/shard_map/ppermute | solution.py:213
  25.9 0.2 collective-permute-start.4
  26.1 2.0 %shard_map.96 = (f32[128,1024]{1,0:T(8,128)S(1)}, f32[128,1024]{1,0:T(8,128)S(1)}, f32[128,1024]{1,0:T(8,128)S(1)}, f32[128,1024]{1,0:T(8,128)S(1)}, bf16[128,10...) custom-call(f32[128,8]{1,0:T(8,128)S(1)} %get-tuple-element.50.rest_3_.cum_ref, ...), custom_call_target="tpu_custom_call" | custom-call | flops 2400000000 | bytes 8000000 | tf_op jit(solution)/shard_map/pallas_call | solution.py:27
  28.2 2.7 %collective-permute-start.5 = (bf16[272,128]{1,0:T(8,128)(2,1)S(1)}, bf16[272,128]{1,0:T(8,128)(2,1)S(1)}, u32[]{:S(2)}, u32[]{:S(2)}) collective-permute-start(bf16[272,128]{1,0:T(8,128)(2,1)S(1)} %get-tuple-element.64), channel_id=1, source_target_pairs={{0,12},{4,8},{8,4},{12,0},{16,28},{20,24},{24,20},{28,16},{1,13},{... | collective-permute-start | bytes 208904 | tf_op jit(solution)/shard_map/ppermute | solution.py:213
  30.9 0.7 %shard_map.101 = (bf16[128,1024]{1,0:T(8,128)(2,1)S(1)}, bf16[128,768]{1,0:T(8,128)(2,1)S(1)}, bf16[128,768]{1,0:T(8,128)(2,1)S(1)}) custom-call(bf16[1024,3072]{1,0:T(8,128)(2,1)S(1)} %bitcast.2, f32[128,1024]{1,0:T(8,128)S(1)} %get-tuple-element.71.local_ref, bf16[128,1024]{1,0:T(8,128)(2,1)S(1)} %get-tuple-element.72.rise_ref, ...), custom_call_target="tpu_custom_call" | custom-call | flops 2400000000 | bytes 8000000 | tf_op jit(solution)/shard_map/pallas_call | solution.py:27
  31.6 1.1 %shard_map.102 = (bf16[128,1024]{1,0:T(8,128)(2,1)}, bf16[128,768]{1,0:T(8,128)(2,1)S(1)}, f32[128,768]{1,0:T(8,128)S(1)}) custom-call(bf16[1024,3072]{1,0:T(8,128)(2,1)S(1)} %bitcast.2, bf16[128,1024]{1,0:T(8,128)(2,1)S(1)} %get-tuple-element.83.flat_ref, f32[128,1024]{1,0:T(8,128)S(1)} %get-tuple-element.84.lq_ref, ...), custom_call_target="tpu_custom_call" | custom-call | flops 2400000000 | bytes 8000000 | tf_op jit(solution)/shard_map/pallas_call | solution.py:27
  32.8 0.5 %collective-permute-start.18 = (bf16[128,768]{1,0:T(8,128)(2,1)S(1)}, bf16[128,768]{1,0:T(8,128)(2,1)S(1)}, u32[]{:S(2)}, u32[]{:S(2)}) collective-permute-start(bf16[128,768]{1,0:T(8,128)(2,1)S(1)} %get-tuple-element.89), channel_id=1, source_target_pairs={{0,1},{1,0},{2,3},{3,2},{4,5},{5,4},{6,7},{7,6},{8,9},{9,8},{10,11... | collective-permute-start | bytes 589832 | tf_op jit(solution)/shard_map/ppermute | solution.py:213
  33.3 0.2 collective-permute-done.5.rest_3_
  33.6 3.3 %collective-permute-start.6 = (bf16[272,128]{1,0:T(8,128)(2,1)S(1)}, bf16[272,128]{1,0:T(8,128)(2,1)S(1)}, u32[]{:S(2)}, u32[]{:S(2)}) collective-permute-start(bf16[272,128]{1,0:T(8,128)(2,1)S(1)} %get-tuple-element.65), channel_id=1, source_target_pairs={{0,16},{4,20},{8,24},{12,28},{16,0},{20,4},{24,8},{28,12},{1,17},{... | collective-permute-start | bytes 208904 | tf_op jit(solution)/shard_map/ppermute | solution.py:232
  36.9 1.6 %collective-permute-start.19 = (bf16[128,768]{1,0:T(8,128)(2,1)S(1)}, bf16[128,768]{1,0:T(8,128)(2,1)S(1)}, u32[]{:S(2)}, u32[]{:S(2)}) collective-permute-start(bf16[128,768]{1,0:T(8,128)(2,1)S(1)} %add_convert_fusion), channel_id=1, source_target_pairs={{0,2},{1,3},{2,0},{3,1},{4,6},{5,7},{6,4},{7,5},{8,10},{9,11},{10,... | collective-permute-start | bytes 589832 | tf_op jit(solution)/shard_map/ppermute | solution.py:213
  38.5 0.7 %collective-permute-done.6.entry_ref = bf16[272,128]{1,0:T(8,128)(2,1)S(1)} collective-permute-done((bf16[272,128]{1,0:T(8,128)(2,1)S(1)}, bf16[272,128]{1,0:T(8,128)(2,1)S(1)}, u32[]{:S(2)}, u32[]{:S(2)}) %collective-permute-start.6) | collective-permute-done | bytes 69664 | tf_op jit(solution)/shard_map/ppermute | solution.py:232
  39.3 0.9 %collective-permute-start.7 = (bf16[256,128]{1,0:T(8,128)(2,1)S(1)}, bf16[256,128]{1,0:T(8,128)(2,1)S(1)}, u32[]{:S(2)}, u32[]{:S(2)}) collective-permute-start(bf16[256,128]{1,0:T(8,128)(2,1)S(1)} %get-tuple-element.68), channel_id=1, source_target_pairs={{0,4},{4,0},{8,12},{12,8},{16,20},{20,16},{24,28},{28,24},{1,5},{5... | collective-permute-start | bytes 196616 | tf_op jit(solution)/shard_map/ppermute | solution.py:213
  40.2 2.0 %collective-permute-start.8 = (bf16[256,128]{1,0:T(8,128)(2,1)S(1)}, bf16[256,128]{1,0:T(8,128)(2,1)S(1)}, u32[]{:S(2)}, u32[]{:S(2)}) collective-permute-start(bf16[256,128]{1,0:T(8,128)(2,1)S(1)} %get-tuple-element.69), channel_id=1, source_target_pairs={{0,8},{4,12},{8,0},{12,4},{16,24},{20,28},{24,16},{28,20},{1,9},{5... | collective-permute-start | bytes 196616 | tf_op jit(solution)/shard_map/ppermute | solution.py:213
  42.2 0.6 %collective-permute-start.9 = (bf16[256,128]{1,0:T(8,128)(2,1)S(1)}, bf16[256,128]{1,0:T(8,128)(2,1)S(1)}, u32[]{:S(2)}, u32[]{:S(2)}) collective-permute-start(bf16[256,128]{1,0:T(8,128)(2,1)S(1)} %get-tuple-element.70), channel_id=1, source_target_pairs={{0,12},{4,8},{8,4},{12,0},{16,28},{20,24},{24,20},{28,16},{1,13},{... | collective-permute-start | bytes 196616 | tf_op jit(solution)/shard_map/ppermute | solution.py:213
  42.8 1.5 %collective-permute-done.7.rest_1_ = bf16[256,128]{1,0:T(8,128)(2,1)S(1)} collective-permute-done((bf16[256,128]{1,0:T(8,128)(2,1)S(1)}, bf16[256,128]{1,0:T(8,128)(2,1)S(1)}, u32[]{:S(2)}, u32[]{:S(2)}) %collective-permute-start.7) | collective-permute-done | bytes 65568 | tf_op jit(solution)/shard_map/ppermute | solution.py:213
  44.4 2.9 %collective-permute-done.9.rest_3_ = bf16[256,128]{1,0:T(8,128)(2,1)S(1)} collective-permute-done((bf16[256,128]{1,0:T(8,128)(2,1)S(1)}, bf16[256,128]{1,0:T(8,128)(2,1)S(1)}, u32[]{:S(2)}, u32[]{:S(2)}) %collective-permute-start.9) | collective-permute-done | bytes 65568 | tf_op jit(solution)/shard_map/ppermute | solution.py:213
  47.3 1.2 %shard_map.103 = (bf16[128,768]{1,0:T(8,128)(2,1)}, bf16[128,1024]{1,0:T(8,128)(2,1)}, bf16[128,1024]{1,0:T(8,128)(2,1)}) custom-call(bf16[128,1024]{1,0:T(8,128)(2,1)S(1)} %get-tuple-element.49.k_fall_ref, bf16[128,1024]{1,0:T(8,128)(2,1)S(1)} %get-tuple-element.58.v_fall_ref, f32[128,1024]{1,0:T(8,128)S(1)} %get-tuple-element.59.lk_ref, ...), custom_call_target="tpu_custom_call" | custom-call | flops 2400000000 | bytes 8000000 | tf_op jit(solution)/shard_map/pallas_call | solution.py:27
  (27 shorter events, 0.7 us)
Async XLA Ops:
  2.8 12.6 %copy-start = (bf16[128,768]{1,0:T(8,128)(2,1)S(1)}, bf16[128,768]{1,0:T(8,128)(2,1)}, u32[]{:S(2)}) copy-start(bf16[128,768]{1,0:T(8,128)(2,1)} %rest_0_.1) | copy-start | bytes 589828
  2.9 5.3 %collective-permute-start.10 = (bf16[272,128]{1,0:T(8,128)(2,1)S(1)}, bf16[272,128]{1,0:T(8,128)(2,1)S(1)}, u32[]{:S(2)}, u32[]{:S(2)}) collective-permute-start(bf16[272,128]{1,0:T(8,128)(2,1)S(1)} %get-tuple-element.74), channel_id=1, source_target_pairs={{0,4},{4,0},{8,12},{12,8},{16,20},{20,16},{24,28},{28,24},{1,5},{5... | collective-permute-start | bytes 208904 | tf_op jit(solution)/shard_map/ppermute | solution.py:213
  5.9 4.9 %collective-permute-start.11 = (bf16[272,128]{1,0:T(8,128)(2,1)S(1)}, bf16[272,128]{1,0:T(8,128)(2,1)S(1)}, u32[]{:S(2)}, u32[]{:S(2)}) collective-permute-start(bf16[272,128]{1,0:T(8,128)(2,1)S(1)} %get-tuple-element.75), channel_id=1, source_target_pairs={{0,8},{4,12},{8,0},{12,4},{16,24},{20,28},{24,16},{28,20},{1,9},{5... | collective-permute-start | bytes 208904 | tf_op jit(solution)/shard_map/ppermute | solution.py:213
  7.5 5.2 %collective-permute-start.12 = (bf16[272,128]{1,0:T(8,128)(2,1)S(1)}, bf16[272,128]{1,0:T(8,128)(2,1)S(1)}, u32[]{:S(2)}, u32[]{:S(2)}) collective-permute-start(bf16[272,128]{1,0:T(8,128)(2,1)S(1)} %get-tuple-element.76), channel_id=1, source_target_pairs={{0,12},{4,8},{8,4},{12,0},{16,28},{20,24},{24,20},{28,16},{1,13},{... | collective-permute-start | bytes 208904 | tf_op jit(solution)/shard_map/ppermute | solution.py:213
  12.7 9.7 %slice-start = ((s8[6291456]{0:T(1024)(128)(4,1)}), s8[4194304]{0:T(1024)(128)(4,1)S(1)}, s32[]{:S(2)}) async-start(s8[6291456]{0:T(1024)(128)(4,1)} %bitcast.1), calls=%async_computation | async-start | bytes 8388608
  12.8 5.9 %collective-permute-start.13 = (bf16[272,128]{1,0:T(8,128)(2,1)S(1)}, bf16[272,128]{1,0:T(8,128)(2,1)S(1)}, u32[]{:S(2)}, u32[]{:S(2)}) collective-permute-start(bf16[272,128]{1,0:T(8,128)(2,1)S(1)} %get-tuple-element.77), channel_id=1, source_target_pairs={{0,16},{4,20},{8,24},{12,28},{16,0},{20,4},{24,8},{28,12},{1,17},{... | collective-permute-start | bytes 208904 | tf_op jit(solution)/shard_map/ppermute | solution.py:232
  15.4 6.9 %collective-permute-start = (bf16[128,768]{1,0:T(8,128)(2,1)S(1)}, bf16[128,768]{1,0:T(8,128)(2,1)S(1)}, u32[]{:S(2)}, u32[]{:S(2)}) collective-permute-start(bf16[128,768]{1,0:T(8,128)(2,1)S(1)} %copy-done), channel_id=1, source_target_pairs={{0,2},{1,3},{2,0},{3,1},{4,6},{5,7},{6,4},{7,5},{8,10},{9,11},{10,... | collective-permute-start | bytes 589832 | tf_op jit(solution)/shard_map/ppermute | solution.py:213
  17.0 5.4 %collective-permute-start.2 = (bf16[128,768]{1,0:T(8,128)(2,1)S(1)}, bf16[128,768]{1,0:T(8,128)(2,1)S(1)}, u32[]{:S(2)}, u32[]{:S(2)}) collective-permute-start(bf16[128,768]{1,0:T(8,128)(2,1)S(1)} %copy-done), channel_id=1, source_target_pairs={{0,1},{1,0},{2,3},{3,2},{4,5},{5,4},{6,7},{7,6},{8,9},{9,8},{10,11... | collective-permute-start | bytes 589832 | tf_op jit(solution)/shard_map/ppermute | solution.py:213
  18.7 3.7 %slice-start.1 = ((s8[6291456]{0:T(1024)(128)(4,1)}), s8[2097152]{0:T(1024)(128)(4,1)S(1)}, s32[]{:S(2)}) async-start(s8[6291456]{0:T(1024)(128)(4,1)} %bitcast.1), calls=%async_computation.1 | async-start | bytes 4194304
  18.8 9.4 %collective-permute-start.14 = (bf16[256,128]{1,0:T(8,128)(2,1)S(1)}, bf16[256,128]{1,0:T(8,128)(2,1)S(1)}, u32[]{:S(2)}, u32[]{:S(2)}) collective-permute-start(bf16[256,128]{1,0:T(8,128)(2,1)S(1)} %get-tuple-element.80), channel_id=1, source_target_pairs={{0,4},{4,0},{8,12},{12,8},{16,20},{20,16},{24,28},{28,24},{1,5},{5... | collective-permute-start | bytes 196616 | tf_op jit(solution)/shard_map/ppermute | solution.py:213
  19.5 11.4 %collective-permute-start.15 = (bf16[256,128]{1,0:T(8,128)(2,1)S(1)}, bf16[256,128]{1,0:T(8,128)(2,1)S(1)}, u32[]{:S(2)}, u32[]{:S(2)}) collective-permute-start(bf16[256,128]{1,0:T(8,128)(2,1)S(1)} %get-tuple-element.81), channel_id=1, source_target_pairs={{0,8},{4,12},{8,0},{12,4},{16,24},{20,28},{24,16},{28,20},{1,9},{5... | collective-permute-start | bytes 196616 | tf_op jit(solution)/shard_map/ppermute | solution.py:213
  19.7 11.2 %collective-permute-start.16 = (bf16[256,128]{1,0:T(8,128)(2,1)S(1)}, bf16[256,128]{1,0:T(8,128)(2,1)S(1)}, u32[]{:S(2)}, u32[]{:S(2)}) collective-permute-start(bf16[256,128]{1,0:T(8,128)(2,1)S(1)} %get-tuple-element.82), channel_id=1, source_target_pairs={{0,12},{4,8},{8,4},{12,0},{16,28},{20,24},{24,20},{28,16},{1,13},{... | collective-permute-start | bytes 196616 | tf_op jit(solution)/shard_map/ppermute | solution.py:213
  22.3 1.4 %collective-permute-start.1 = (bf16[128,768]{1,0:T(8,128)(2,1)S(1)}, bf16[128,768]{1,0:T(8,128)(2,1)S(1)}, u32[]{:S(2)}, u32[]{:S(2)}) collective-permute-start(bf16[128,768]{1,0:T(8,128)(2,1)S(1)} %collective-permute-done.rest_0_), channel_id=1, source_target_pairs={{0,1},{1,0},{2,3},{3,2},{4,5},{5,4},{6,7},{7,6},{8,9},{9,8},{10,11... | collective-permute-start | bytes 589832 | tf_op jit(solution)/shard_map/ppermute | solution.py:213
  25.2 8.0 %collective-permute-start.3 = (bf16[272,128]{1,0:T(8,128)(2,1)S(1)}, bf16[272,128]{1,0:T(8,128)(2,1)S(1)}, u32[]{:S(2)}, u32[]{:S(2)}) collective-permute-start(bf16[272,128]{1,0:T(8,128)(2,1)S(1)} %get-tuple-element.62), channel_id=1, source_target_pairs={{0,4},{4,0},{8,12},{12,8},{16,20},{20,16},{24,28},{28,24},{1,5},{5... | collective-permute-start | bytes 208904 | tf_op jit(solution)/shard_map/ppermute | solution.py:213
  25.9 7.3 %collective-permute-start.4 = (bf16[272,128]{1,0:T(8,128)(2,1)S(1)}, bf16[272,128]{1,0:T(8,128)(2,1)S(1)}, u32[]{:S(2)}, u32[]{:S(2)}) collective-permute-start(bf16[272,128]{1,0:T(8,128)(2,1)S(1)} %get-tuple-element.63), channel_id=1, source_target_pairs={{0,8},{4,12},{8,0},{12,4},{16,24},{20,28},{24,16},{28,20},{1,9},{5... | collective-permute-start | bytes 208904 | tf_op jit(solution)/shard_map/ppermute | solution.py:213
  28.2 5.3 %collective-permute-start.5 = (bf16[272,128]{1,0:T(8,128)(2,1)S(1)}, bf16[272,128]{1,0:T(8,128)(2,1)S(1)}, u32[]{:S(2)}, u32[]{:S(2)}) collective-permute-start(bf16[272,128]{1,0:T(8,128)(2,1)S(1)} %get-tuple-element.64), channel_id=1, source_target_pairs={{0,12},{4,8},{8,4},{12,0},{16,28},{20,24},{24,20},{28,16},{1,13},{... | collective-permute-start | bytes 208904 | tf_op jit(solution)/shard_map/ppermute | solution.py:213
  32.7 10.1 %collective-permute-start.17 = (bf16[128,768]{1,0:T(8,128)(2,1)S(1)}, bf16[128,768]{1,0:T(8,128)(2,1)S(1)}, u32[]{:S(2)}, u32[]{:S(2)}) collective-permute-start(bf16[128,768]{1,0:T(8,128)(2,1)S(1)} %get-tuple-element.87), channel_id=1, source_target_pairs={{0,1},{1,0},{2,3},{3,2},{4,5},{5,4},{6,7},{7,6},{8,9},{9,8},{10,11... | collective-permute-start | bytes 589832 | tf_op jit(solution)/shard_map/ppermute | solution.py:213
  32.8 4.1 %collective-permute-start.18 = (bf16[128,768]{1,0:T(8,128)(2,1)S(1)}, bf16[128,768]{1,0:T(8,128)(2,1)S(1)}, u32[]{:S(2)}, u32[]{:S(2)}) collective-permute-start(bf16[128,768]{1,0:T(8,128)(2,1)S(1)} %get-tuple-element.89), channel_id=1, source_target_pairs={{0,1},{1,0},{2,3},{3,2},{4,5},{5,4},{6,7},{7,6},{8,9},{9,8},{10,11... | collective-permute-start | bytes 589832 | tf_op jit(solution)/shard_map/ppermute | solution.py:213
  33.6 5.6 %collective-permute-start.6 = (bf16[272,128]{1,0:T(8,128)(2,1)S(1)}, bf16[272,128]{1,0:T(8,128)(2,1)S(1)}, u32[]{:S(2)}, u32[]{:S(2)}) collective-permute-start(bf16[272,128]{1,0:T(8,128)(2,1)S(1)} %get-tuple-element.65), channel_id=1, source_target_pairs={{0,16},{4,20},{8,24},{12,28},{16,0},{20,4},{24,8},{28,12},{1,17},{... | collective-permute-start | bytes 208904 | tf_op jit(solution)/shard_map/ppermute | solution.py:232
  36.9 10.4 %collective-permute-start.19 = (bf16[128,768]{1,0:T(8,128)(2,1)S(1)}, bf16[128,768]{1,0:T(8,128)(2,1)S(1)}, u32[]{:S(2)}, u32[]{:S(2)}) collective-permute-start(bf16[128,768]{1,0:T(8,128)(2,1)S(1)} %add_convert_fusion), channel_id=1, source_target_pairs={{0,2},{1,3},{2,0},{3,1},{4,6},{5,7},{6,4},{7,5},{8,10},{9,11},{10,... | collective-permute-start | bytes 589832 | tf_op jit(solution)/shard_map/ppermute | solution.py:213
  39.3 5.0 %collective-permute-start.7 = (bf16[256,128]{1,0:T(8,128)(2,1)S(1)}, bf16[256,128]{1,0:T(8,128)(2,1)S(1)}, u32[]{:S(2)}, u32[]{:S(2)}) collective-permute-start(bf16[256,128]{1,0:T(8,128)(2,1)S(1)} %get-tuple-element.68), channel_id=1, source_target_pairs={{0,4},{4,0},{8,12},{12,8},{16,20},{20,16},{24,28},{28,24},{1,5},{5... | collective-permute-start | bytes 196616 | tf_op jit(solution)/shard_map/ppermute | solution.py:213
  40.2 4.3 %collective-permute-start.8 = (bf16[256,128]{1,0:T(8,128)(2,1)S(1)}, bf16[256,128]{1,0:T(8,128)(2,1)S(1)}, u32[]{:S(2)}, u32[]{:S(2)}) collective-permute-start(bf16[256,128]{1,0:T(8,128)(2,1)S(1)} %get-tuple-element.69), channel_id=1, source_target_pairs={{0,8},{4,12},{8,0},{12,4},{16,24},{20,28},{24,16},{28,20},{1,9},{5... | collective-permute-start | bytes 196616 | tf_op jit(solution)/shard_map/ppermute | solution.py:213
  42.2 5.2 %collective-permute-start.9 = (bf16[256,128]{1,0:T(8,128)(2,1)S(1)}, bf16[256,128]{1,0:T(8,128)(2,1)S(1)}, u32[]{:S(2)}, u32[]{:S(2)}) collective-permute-start(bf16[256,128]{1,0:T(8,128)(2,1)S(1)} %get-tuple-element.70), channel_id=1, source_target_pairs={{0,12},{4,8},{8,4},{12,0},{16,28},{20,24},{24,20},{28,16},{1,13},{... | collective-permute-start | bytes 196616 | tf_op jit(solution)/shard_map/ppermute | solution.py:213

commit v4 on v3

--- a/solution.py
+++ b/solution.py
@@ -35,19 +35,12 @@
     )(*args)
 
 
-def in_hbm(array):
-    return pltpu.with_memory_space_constraint(array, pltpu.HBM)
-
-
 def shape(dims, dtype):
     return jax.ShapeDtypeStruct(dims, dtype)
 
 
-def running_log(codes):
+def running_log(codes, lower):
     rest = jnp.log(1.0 - codes.astype(F32) / 4096.0)
-    size = (codes.shape[1], codes.shape[1])
-    place, other = (lax.broadcasted_iota(jnp.int32, size, axis) for axis in (0, 1))
-    lower = (other <= place).astype(F32).astype(BF16)
     columns = rows = None
     for _ in range(3):
         part = rest.astype(BF16)
@@ -91,14 +84,12 @@
     return ref[at : at + 1, :] + ref[at + plan.half_tail : at + plan.half_tail + 1, :]
 
 
-def put_summaries(plan, rank, left, right, cum, outs, scratch, arrive=None):
+def put_summaries(plan, rank, left, right, cum, outs, scratch):
     width = plan.width
     last = jnp.exp(cum[plan.tok - 1 : plan.tok, :])
     for q in range(plan.group):
         base = q * plan.rows
         totals = []
-        if arrive is not None:
-            arrive(q)
         for i in range(plan.quarter):
             h = q * plan.quarter + i
             scratch[base + i * width : base + (i + 1) * width, :] = dot(left(h), right(h), 0, 0)
@@ -118,28 +109,14 @@
     return pltpu.VMEM((plan.group * plan.rows, plan.width), F32)
 
 
-def first_kernel(plan, codes, keys, values, queries, *refs):
-    outs, refs = refs[: plan.group], refs[plan.group :]
-    cum_ref, cum_t_ref, rise_ref, fall_ref, k_fall_ref, k_ref, v_ref, q_ref = refs[:8]
-    scratch, codes_ref, sems = refs[8:]
-    loads = []
-
-    def load(src, dst):
-        copy = pltpu.make_async_copy(src, dst, sems.at[len(loads)])
-        copy.start()
-        loads.append(copy)
-        return copy
-
-    wide = plan.quarter * plan.width
-    codes_load = load(codes, codes_ref)
-    pieces = []
-    for q in range(plan.group):
-        at = slice(q * wide, (q + 1) * wide)
-        pieces.append((load(keys.at[:, at], k_ref.at[:, at]), load(values.at[:, at], v_ref.at[:, at])))
-    late = [load(queries, q_ref)]
-
-    codes_load.wait()
-    cum, cum_t = running_log(codes_ref[...])
+def lower_kernel(lower_ref):
+    place, other = (lax.broadcasted_iota(jnp.int32, lower_ref.shape, axis) for axis in (0, 1))
+    lower_ref[...] = (other <= place).astype(F32).astype(BF16)
+
+
+def first_kernel(plan, lower_ref, codes_ref, k_ref, v_ref, *refs):
+    outs, (cum_ref, cum_t_ref, rise_ref, fall_ref, k_fall_ref, scratch) = refs[:-6], refs[-6:]
+    cum, cum_t = running_log(codes_ref[...], lower_ref[...])
     fall = jnp.exp(cum[plan.tok - 1 : plan.tok, :] - cum)
     cum_ref[...], cum_t_ref[...] = cum, cum_t
     rise_ref[...] = (1.0 / plan.width) * jnp.exp(cum)
@@ -148,24 +125,22 @@
     def cols(h):
         return slice(h * plan.width, (h + 1) * plan.width)
 
-    def arrive(q):
-        for piece in pieces[q]:
-            piece.wait()
-
     def left(h):
         k_fall = (fall[:, h : h + 1] * k_ref[:, cols(h)].astype(F32)).astype(BF16)
         k_fall_ref[:, cols(h)] = k_fall
         return k_fall
 
     rank = positions(plan, 1)[0]
-    put_summaries(plan, rank, left, lambda h: v_ref[:, cols(h)], cum, outs, scratch, arrive)
-    for copy in late:
-        copy.wait()
+    put_summaries(plan, rank, left, lambda h: v_ref[:, cols(h)], cum, outs, scratch)
+
+
+def hold_kernel(mark_ref):
+    mark_ref[...] = jnp.zeros_like(mark_ref)
 
 
 def combine_kernel(plan, way, *rest):
     group, width = plan.group, plan.width
-    ins, (pre_ref, total_ref, scratch) = rest[:group], rest[group:]
+    ins, (pre_ref, total_ref, scratch) = rest[:group], rest[-3:]
     rank = positions(plan, way)[0]
     for j in range(group):
         scratch[aligned(rank ^ j, plan.rows), :] = ins[j][...].astype(F32)
@@ -244,11 +219,12 @@
     others = range(1, plan.group)
     got = [summaries[0]] + [swap(summaries[j], "seq", j) for j in others]
     rows, body = (plan.rows, plan.width), (plan.body, plan.width)
+    mark = call(hold_kernel, [shape((8, 128), F32)], [], [])
     pre, total = call(
         functools.partial(combine_kernel, plan, way),
         [shape((plan.group * plan.rows, plan.width), F32), shape(rows, BF16)],
-        [VMEM] * plan.group,
-        got,
+        [VMEM] * (plan.group + 1),
+        got + list(mark),
         [pltpu.VMEM((plan.group * plan.rows, plan.width), F32)],
     )
     entry = group_entry(plan, total, way, turn)
@@ -406,18 +382,15 @@
     weight = out_weight
     wide_bf = shape(wide, BF16)
     offsets = list(range(across))
-    *summaries, cum, cum_t, rise, fall, k_fall, keys, values, queries = call(
+    (lower,) = call(lower_kernel, [shape((tok, tok), BF16)], [], [])
+    *summaries, cum, cum_t, rise, fall, k_fall = call(
         functools.partial(first_kernel, plan),
         summary_shapes(plan)
         + [shape(d, F32) for d in (heads_by, heads_by[::-1], heads_by, heads_by)]
-        + [wide_bf] * 4,
-        [HBM] * 4,
-        [in_hbm(x) for x in (codes, keys, values, queries)],
-        [
-            summary_scratch(plan),
-            pltpu.VMEM(codes.shape, codes.dtype),
-            pltpu.SemaphoreType.DMA((2 * plan.group + 2,)),
-        ],
+        + [wide_bf],
+        [VMEM] * 4,
+        [lower, codes, keys, values],
+        [summary_scratch(plan)],
     )
     states = scan_states(plan, summaries, 1)
 

time: 48.8 us -> 49 us (level)
  waiting for transfers between devices: 12.6 us -> 14.7 us
  Pallas kernels: 10.2 us -> 8.76 us
    ppermute x2, waiting for transfers between devices: 2.41 us -> 5.57 us  [shift(): lax.ppermute(value, 'seq', [(i, (i + hop) % count) for i in range(count)])]
    pallas_call x11 -> x14, Pallas kernels: 10.2 us -> 8.76 us  [call(): pl.pallas_call(kernel, out_shape=outs, in_specs=specs, out_specs=out_spec...]
    ppermute x18, waiting for transfers between devices: 10.2 us -> 9.11 us  [swap(): return lax.ppermute(value, axis, [(i, i ^ offset) for i in range(count)])]
  transfers between devices with their start and end apart: 20 -> 20, of which waited for: 10 -> 10; matrix products, arithmetic and copies ran while one was open for 0% -> 0% of each run, Pallas kernels for 14% -> 15%
where the time goes in v4:
time: 49 us; the launch traced here: 48.9 us
  starting transfers between devices  24.5 us (50%)
  waiting for transfers between devices  14.7 us (30%)
  Pallas kernels  8.76 us (18%)
  between operations  0.84 us (2%)
    ppermute x18, starting transfers between devices, swap(): return lax.ppermute(value, axis, [(i, i ^ offset) for i in range(count)])  18.5 us
    ppermute x18, waiting for transfers between devices, swap(): return lax.ppermute(value, axis, [(i, i ^ offset) for i in range(count)])  9.11 us
    pallas_call x14, Pallas kernels, call(): pl.pallas_call(kernel, out_shape=outs, in_specs=specs, out_specs=out_spec...  8.76 us
    ppermute x2, starting transfers between devices, shift(): lax.ppermute(value, 'seq', [(i, (i + hop) % count) for i in range(count)])  5.97 us
    ppermute x2, waiting for transfers between devices, shift(): lax.ppermute(value, 'seq', [(i, (i + hop) % count) for i in range(count)])  5.57 us
  transfers between devices with their start and end apart: 20, of which 10 were waited for; matrix products, arithmetic and copies ran while one was open for 0% of the time, Pallas kernels for 15%

profile of v4, /device:TPU:0, one launch (start us, length us, event | category | flops | bytes accessed | tf_op | source)
XLA Modules:
  0.0 48.9 jit_solution(1166274880662156827)
XLA Ops:
  0.7 3.1 %collective-permute-start = (bf16[128,768]{1,0:T(8,128)(2,1)}, bf16[128,768]{1,0:T(8,128)(2,1)S(1)}, u32[]{:S(2)}, u32[]{:S(2)}) collective-permute-start(bf16[128,768]{1,0:T(8,128)(2,1)} %rest_0_.1), channel_id=1, source_target_pairs={{0,2},{1,3},{2,0},{3,1},{4,6},{5,7},{6,4},{7,5},{8,10},{9,11},{10,... | collective-permute-start | bytes 589832 | tf_op jit(solution)/shard_map/ppermute | solution.py:188
  3.8 0.7 %shard_map.94 = (f32[272,128]{1,0:T(8,128)S(1)}, bf16[272,128]{1,0:T(8,128)(2,1)S(1)}, bf16[272,128]{1,0:T(8,128)(2,1)S(1)}, bf16[272,128]{1,0:T(8,128)(2,1)S(1)...) custom-call(bf16[128,128]{1,0:T(8,128)(2,1)S(1)} %shard_map.93.lower, ...), custom_call_target="tpu_custom_call" | custom-call | flops 2400000000 | bytes 8000000 | tf_op jit(solution)/shard_map/pallas_call | solution.py:27
  4.5 1.6 %collective-permute-start.10 = (bf16[272,128]{1,0:T(8,128)(2,1)S(1)}, bf16[272,128]{1,0:T(8,128)(2,1)S(1)}, u32[]{:S(2)}, u32[]{:S(2)}) collective-permute-start(bf16[272,128]{1,0:T(8,128)(2,1)S(1)} %get-tuple-element.68), channel_id=1, source_target_pairs={{0,4},{4,0},{8,12},{12,8},{16,20},{20,16},{24,28},{28,24},{1,5},{5... | collective-permute-start | bytes 208904 | tf_op jit(solution)/shard_map/ppermute | solution.py:188
  6.0 1.6 %collective-permute-start.11 = (bf16[272,128]{1,0:T(8,128)(2,1)S(1)}, bf16[272,128]{1,0:T(8,128)(2,1)S(1)}, u32[]{:S(2)}, u32[]{:S(2)}) collective-permute-start(bf16[272,128]{1,0:T(8,128)(2,1)S(1)} %get-tuple-element.69), channel_id=1, source_target_pairs={{0,8},{4,12},{8,0},{12,4},{16,24},{20,28},{24,16},{28,20},{1,9},{5... | collective-permute-start | bytes 208904 | tf_op jit(solution)/shard_map/ppermute | solution.py:188
  7.6 0.4 collective-permute-start.12
  8.0 1.1 %collective-permute-done.10.rest_1_ = bf16[272,128]{1,0:T(8,128)(2,1)S(1)} collective-permute-done((bf16[272,128]{1,0:T(8,128)(2,1)S(1)}, bf16[272,128]{1,0:T(8,128)(2,1)S(1)}, u32[]{:S(2)}, u32[]{:S(2)}) %collective-permute-start.10) | collective-permute-done | bytes 69664 | tf_op jit(solution)/shard_map/ppermute | solution.py:188
  9.1 1.4 %collective-permute-done.11.rest_2_ = bf16[272,128]{1,0:T(8,128)(2,1)S(1)} collective-permute-done((bf16[272,128]{1,0:T(8,128)(2,1)S(1)}, bf16[272,128]{1,0:T(8,128)(2,1)S(1)}, u32[]{:S(2)}, u32[]{:S(2)}) %collective-permute-start.11) | collective-permute-done | bytes 69664 | tf_op jit(solution)/shard_map/ppermute | solution.py:188
  10.6 2.3 %collective-permute-done.12.rest_3_ = bf16[272,128]{1,0:T(8,128)(2,1)S(1)} collective-permute-done((bf16[272,128]{1,0:T(8,128)(2,1)S(1)}, bf16[272,128]{1,0:T(8,128)(2,1)S(1)}, u32[]{:S(2)}, u32[]{:S(2)}) %collective-permute-start.12) | collective-permute-done | bytes 69664 | tf_op jit(solution)/shard_map/ppermute | solution.py:188
  12.9 2.7 %collective-permute-start.13 = (bf16[272,128]{1,0:T(8,128)(2,1)S(1)}, bf16[272,128]{1,0:T(8,128)(2,1)S(1)}, u32[]{:S(2)}, u32[]{:S(2)}) collective-permute-start(bf16[272,128]{1,0:T(8,128)(2,1)S(1)} %get-tuple-element.71), channel_id=1, source_target_pairs={{0,16},{4,20},{8,24},{12,28},{16,0},{20,4},{24,8},{28,12},{1,17},{... | collective-permute-start | bytes 208904 | tf_op jit(solution)/shard_map/ppermute | solution.py:207
  15.6 3.3 %collective-permute-done.13.entry_ref = bf16[272,128]{1,0:T(8,128)(2,1)S(1)} collective-permute-done((bf16[272,128]{1,0:T(8,128)(2,1)S(1)}, bf16[272,128]{1,0:T(8,128)(2,1)S(1)}, u32[]{:S(2)}, u32[]{:S(2)}) %collective-permute-start.13) | collective-permute-done | bytes 69664 | tf_op jit(solution)/shard_map/ppermute | solution.py:207
  19.1 1.3 %collective-permute-start.15 = (bf16[256,128]{1,0:T(8,128)(2,1)S(1)}, bf16[256,128]{1,0:T(8,128)(2,1)S(1)}, u32[]{:S(2)}, u32[]{:S(2)}) collective-permute-start(bf16[256,128]{1,0:T(8,128)(2,1)S(1)} %get-tuple-element.75), channel_id=1, source_target_pairs={{0,8},{4,12},{8,0},{12,4},{16,24},{20,28},{24,16},{28,20},{1,9},{5... | collective-permute-start | bytes 196616 | tf_op jit(solution)/shard_map/ppermute | solution.py:188
  20.5 2.2 %collective-permute-start.16 = (bf16[256,128]{1,0:T(8,128)(2,1)S(1)}, bf16[256,128]{1,0:T(8,128)(2,1)S(1)}, u32[]{:S(2)}, u32[]{:S(2)}) collective-permute-start(bf16[256,128]{1,0:T(8,128)(2,1)S(1)} %get-tuple-element.76), channel_id=1, source_target_pairs={{0,12},{4,8},{8,4},{12,0},{16,28},{20,24},{24,20},{28,16},{1,13},{... | collective-permute-start | bytes 196616 | tf_op jit(solution)/shard_map/ppermute | solution.py:188
  22.7 1.2 %shard_map.95.rest_2_ = f32[128,1024]{1,0:T(8,128)S(1)} custom-call(bf16[1024,3072]{1,0:T(8,128)(2,1)S(1)} %bitcast.2, bf16[128,768]{1,0:T(8,128)(2,1)S(1)} %copy-done.3, bf16[128,768]{1,0:T(8,128)(2,1)S(1)} %collective-permute-done.2.rest_1_), custom_call_target="tpu_custom_call" | custom-call | flops 2400000000 | bytes 8000000 | tf_op jit(solution)/shard_map/pallas_call | solution.py:27
  23.8 0.2 collective-permute-done.1.rest_1_
  24.1 1.4 %shard_map.96 = (bf16[128,1024]{1,0:T(8,128)(2,1)S(1)}, bf16[128,1024]{1,0:T(8,128)(2,1)S(1)}, f32[272,128]{1,0:T(8,128)S(1)}, bf16[272,128]{1,0:T(8,128)(2,1)S(...) custom-call(bf16[1024,3072]{1,0:T(8,128)(2,1)S(1)} %bitcast.2, ...), custom_call_target="tpu_custom_call" | custom-call | flops 2400000000 | bytes 8000000 | tf_op jit(solution)/shard_map/pallas_call | solution.py:27
  25.5 0.1 collective-permute-start.3
  25.6 1.3 %collective-permute-start.4 = (bf16[272,128]{1,0:T(8,128)(2,1)S(1)}, bf16[272,128]{1,0:T(8,128)(2,1)S(1)}, u32[]{:S(2)}, u32[]{:S(2)}) collective-permute-start(bf16[272,128]{1,0:T(8,128)(2,1)S(1)} %get-tuple-element.57), channel_id=1, source_target_pairs={{0,8},{4,12},{8,0},{12,4},{16,24},{20,28},{24,16},{28,20},{1,9},{5... | collective-permute-start | bytes 208904 | tf_op jit(solution)/shard_map/ppermute | solution.py:188
  26.9 2.0 %shard_map.97 = (f32[128,1024]{1,0:T(8,128)S(1)}, f32[128,1024]{1,0:T(8,128)S(1)}, f32[128,1024]{1,0:T(8,128)S(1)}, f32[128,1024]{1,0:T(8,128)S(1)}, bf16[128,10...) custom-call(f32[128,8]{1,0:T(8,128)S(1)} %get-tuple-element.47.rest_3_.cum_ref, ...), custom_call_target="tpu_custom_call" | custom-call | flops 2400000000 | bytes 8000000 | tf_op jit(solution)/shard_map/pallas_call | solution.py:27
  28.9 2.2 %collective-permute-start.5 = (bf16[272,128]{1,0:T(8,128)(2,1)S(1)}, bf16[272,128]{1,0:T(8,128)(2,1)S(1)}, u32[]{:S(2)}, u32[]{:S(2)}) collective-permute-start(bf16[272,128]{1,0:T(8,128)(2,1)S(1)} %get-tuple-element.58), channel_id=1, source_target_pairs={{0,12},{4,8},{8,4},{12,0},{16,28},{20,24},{24,20},{28,16},{1,13},{... | collective-permute-start | bytes 208904 | tf_op jit(solution)/shard_map/ppermute | solution.py:188
  31.1 0.7 %shard_map.104 = (bf16[128,1024]{1,0:T(8,128)(2,1)S(1)}, bf16[128,768]{1,0:T(8,128)(2,1)S(1)}, bf16[128,768]{1,0:T(8,128)(2,1)S(1)}) custom-call(bf16[1024,3072]{1,0:T(8,128)(2,1)S(1)} %bitcast.2, f32[128,1024]{1,0:T(8,128)S(1)} %get-tuple-element.65.local_ref, bf16[128,1024]{1,0:T(8,128)(2,1)S(1)} %get-tuple-element.66.rise_ref, ...), custom_call_target="tpu_custom_call" | custom-call | flops 2400000000 | bytes 8000000 | tf_op jit(solution)/shard_map/pallas_call | solution.py:27
  31.9 1.1 %shard_map.105 = (bf16[128,1024]{1,0:T(8,128)(2,1)}, bf16[128,768]{1,0:T(8,128)(2,1)S(1)}, f32[128,768]{1,0:T(8,128)S(1)}) custom-call(bf16[1024,3072]{1,0:T(8,128)(2,1)S(1)} %bitcast.2, bf16[128,1024]{1,0:T(8,128)(2,1)S(1)} %get-tuple-element.77.flat_ref, f32[128,1024]{1,0:T(8,128)S(1)} %get-tuple-element.78.lq_ref, ...), custom_call_target="tpu_custom_call" | custom-call | flops 2400000000 | bytes 8000000 | tf_op jit(solution)/shard_map/pallas_call | solution.py:27
  33.1 0.5 %collective-permute-start.18 = (bf16[128,768]{1,0:T(8,128)(2,1)S(1)}, bf16[128,768]{1,0:T(8,128)(2,1)S(1)}, u32[]{:S(2)}, u32[]{:S(2)}) collective-permute-start(bf16[128,768]{1,0:T(8,128)(2,1)S(1)} %get-tuple-element.83), channel_id=1, source_target_pairs={{0,1},{1,0},{2,3},{3,2},{4,5},{5,4},{6,7},{7,6},{8,9},{9,8},{10,11... | collective-permute-start | bytes 589832 | tf_op jit(solution)/shard_map/ppermute | solution.py:188
  33.6 0.6 %collective-permute-done.5.rest_3_ = bf16[272,128]{1,0:T(8,128)(2,1)S(1)} collective-permute-done((bf16[272,128]{1,0:T(8,128)(2,1)S(1)}, bf16[272,128]{1,0:T(8,128)(2,1)S(1)}, u32[]{:S(2)}, u32[]{:S(2)}) %collective-permute-start.5) | collective-permute-done | bytes 69664 | tf_op jit(solution)/shard_map/ppermute | solution.py:188
  34.2 0.1 shard_map.99
  34.3 3.3 %collective-permute-start.6 = (bf16[272,128]{1,0:T(8,128)(2,1)S(1)}, bf16[272,128]{1,0:T(8,128)(2,1)S(1)}, u32[]{:S(2)}, u32[]{:S(2)}) collective-permute-start(bf16[272,128]{1,0:T(8,128)(2,1)S(1)} %get-tuple-element.59), channel_id=1, source_target_pairs={{0,16},{4,20},{8,24},{12,28},{16,0},{20,4},{24,8},{28,12},{1,17},{... | collective-permute-start | bytes 208904 | tf_op jit(solution)/shard_map/ppermute | solution.py:207
  37.7 0.6 %collective-permute-start.19 = (bf16[128,768]{1,0:T(8,128)(2,1)S(1)}, bf16[128,768]{1,0:T(8,128)(2,1)S(1)}, u32[]{:S(2)}, u32[]{:S(2)}) collective-permute-start(bf16[128,768]{1,0:T(8,128)(2,1)S(1)} %add_convert_fusion), channel_id=1, source_target_pairs={{0,2},{1,3},{2,0},{3,1},{4,6},{5,7},{6,4},{7,5},{8,10},{9,11},{10,... | collective-permute-start | bytes 589832 | tf_op jit(solution)/shard_map/ppermute | solution.py:188
  38.3 2.2 %collective-permute-done.6.entry_ref = bf16[272,128]{1,0:T(8,128)(2,1)S(1)} collective-permute-done((bf16[272,128]{1,0:T(8,128)(2,1)S(1)}, bf16[272,128]{1,0:T(8,128)(2,1)S(1)}, u32[]{:S(2)}, u32[]{:S(2)}) %collective-permute-start.6) | collective-permute-done | bytes 69664 | tf_op jit(solution)/shard_map/ppermute | solution.py:207
  40.7 1.7 %collective-permute-start.8 = (bf16[256,128]{1,0:T(8,128)(2,1)S(1)}, bf16[256,128]{1,0:T(8,128)(2,1)S(1)}, u32[]{:S(2)}, u32[]{:S(2)}) collective-permute-start(bf16[256,128]{1,0:T(8,128)(2,1)S(1)} %get-tuple-element.63), channel_id=1, source_target_pairs={{0,8},{4,12},{8,0},{12,4},{16,24},{20,28},{24,16},{28,20},{1,9},{5... | collective-permute-start | bytes 196616 | tf_op jit(solution)/shard_map/ppermute | solution.py:188
  42.5 1.7 %collective-permute-start.9 = (bf16[256,128]{1,0:T(8,128)(2,1)S(1)}, bf16[256,128]{1,0:T(8,128)(2,1)S(1)}, u32[]{:S(2)}, u32[]{:S(2)}) collective-permute-start(bf16[256,128]{1,0:T(8,128)(2,1)S(1)} %get-tuple-element.64), channel_id=1, source_target_pairs={{0,12},{4,8},{8,4},{12,0},{16,28},{20,24},{24,20},{28,16},{1,13},{... | collective-permute-start | bytes 196616 | tf_op jit(solution)/shard_map/ppermute | solution.py:188
  44.2 0.8 %collective-permute-done.7.rest_1_ = bf16[256,128]{1,0:T(8,128)(2,1)S(1)} collective-permute-done((bf16[256,128]{1,0:T(8,128)(2,1)S(1)}, bf16[256,128]{1,0:T(8,128)(2,1)S(1)}, u32[]{:S(2)}, u32[]{:S(2)}) %collective-permute-start.7) | collective-permute-done | bytes 65568 | tf_op jit(solution)/shard_map/ppermute | solution.py:188
  45.0 2.6 %collective-permute-done.9.rest_3_ = bf16[256,128]{1,0:T(8,128)(2,1)S(1)} collective-permute-done((bf16[256,128]{1,0:T(8,128)(2,1)S(1)}, bf16[256,128]{1,0:T(8,128)(2,1)S(1)}, u32[]{:S(2)}, u32[]{:S(2)}) %collective-permute-start.9) | collective-permute-done | bytes 65568 | tf_op jit(solution)/shard_map/ppermute | solution.py:188
  47.6 1.2 %shard_map.106 = (bf16[128,768]{1,0:T(8,128)(2,1)}, bf16[128,1024]{1,0:T(8,128)(2,1)}, bf16[128,1024]{1,0:T(8,128)(2,1)}) custom-call(bf16[128,1024]{1,0:T(8,128)(2,1)S(1)} %get-tuple-element.46.k_fall_ref, bf16[128,1024]{1,0:T(8,128)(2,1)S(1)} %get-tuple-element.52.v_fall_ref, f32[128,1024]{1,0:T(8,128)S(1)} %get-tuple-element.53.lk_ref, ...), custom_call_target="tpu_custom_call" | custom-call | flops 2400000000 | bytes 8000000 | tf_op jit(solution)/shard_map/pallas_call | solution.py:27
  (38 shorter events, 0.7 us)
Async XLA Ops:
  0.6 3.1 %copy-start.1 = (bf16[128,1024]{1,0:T(8,128)(2,1)S(1)}, bf16[128,1024]{1,0:T(8,128)(2,1)}, u32[]{:S(2)}) copy-start(bf16[128,1024]{1,0:T(8,128)(2,1)} %v_ref.3) | copy-start | bytes 786436
  0.6 3.1 %copy-start = (bf16[128,1024]{1,0:T(8,128)(2,1)S(1)}, bf16[128,1024]{1,0:T(8,128)(2,1)}, u32[]{:S(2)}) copy-start(bf16[128,1024]{1,0:T(8,128)(2,1)} %k_ref.3) | copy-start | bytes 786436
  0.7 3.1 %copy-start.4 = (s32[128,8]{0,1:T(8,128)S(1)}, s32[128,8]{0,1:T(8,128)}, u32[]{:S(2)}) copy-start(s32[128,8]{0,1:T(8,128)} %param.9) | copy-start | bytes 12292
  0.7 22.0 %collective-permute-start = (bf16[128,768]{1,0:T(8,128)(2,1)}, bf16[128,768]{1,0:T(8,128)(2,1)S(1)}, u32[]{:S(2)}, u32[]{:S(2)}) collective-permute-start(bf16[128,768]{1,0:T(8,128)(2,1)} %rest_0_.1), channel_id=1, source_target_pairs={{0,2},{1,3},{2,0},{3,1},{4,6},{5,7},{6,4},{7,5},{8,10},{9,11},{10,... | collective-permute-start | bytes 589832 | tf_op jit(solution)/shard_map/ppermute | solution.py:188
  3.7 18.9 %collective-permute-start.2 = (bf16[128,768]{1,0:T(8,128)(2,1)}, bf16[128,768]{1,0:T(8,128)(2,1)S(1)}, u32[]{:S(2)}, u32[]{:S(2)}) collective-permute-start(bf16[128,768]{1,0:T(8,128)(2,1)} %rest_0_.1), channel_id=1, source_target_pairs={{0,1},{1,0},{2,3},{3,2},{4,5},{5,4},{6,7},{7,6},{8,9},{9,8},{10,11... | collective-permute-start | bytes 589832 | tf_op jit(solution)/shard_map/ppermute | solution.py:188
  4.5 4.7 %collective-permute-start.10 = (bf16[272,128]{1,0:T(8,128)(2,1)S(1)}, bf16[272,128]{1,0:T(8,128)(2,1)S(1)}, u32[]{:S(2)}, u32[]{:S(2)}) collective-permute-start(bf16[272,128]{1,0:T(8,128)(2,1)S(1)} %get-tuple-element.68), channel_id=1, source_target_pairs={{0,4},{4,0},{8,12},{12,8},{16,20},{20,16},{24,28},{28,24},{1,5},{5... | collective-permute-start | bytes 208904 | tf_op jit(solution)/shard_map/ppermute | solution.py:188
  6.0 4.5 %collective-permute-start.11 = (bf16[272,128]{1,0:T(8,128)(2,1)S(1)}, bf16[272,128]{1,0:T(8,128)(2,1)S(1)}, u32[]{:S(2)}, u32[]{:S(2)}) collective-permute-start(bf16[272,128]{1,0:T(8,128)(2,1)S(1)} %get-tuple-element.69), channel_id=1, source_target_pairs={{0,8},{4,12},{8,0},{12,4},{16,24},{20,28},{24,16},{28,20},{1,9},{5... | collective-permute-start | bytes 208904 | tf_op jit(solution)/shard_map/ppermute | solution.py:188
  7.6 5.2 %collective-permute-start.12 = (bf16[272,128]{1,0:T(8,128)(2,1)S(1)}, bf16[272,128]{1,0:T(8,128)(2,1)S(1)}, u32[]{:S(2)}, u32[]{:S(2)}) collective-permute-start(bf16[272,128]{1,0:T(8,128)(2,1)S(1)} %get-tuple-element.70), channel_id=1, source_target_pairs={{0,12},{4,8},{8,4},{12,0},{16,28},{20,24},{24,20},{28,16},{1,13},{... | collective-permute-start | bytes 208904 | tf_op jit(solution)/shard_map/ppermute | solution.py:188
  12.9 6.0 %collective-permute-start.13 = (bf16[272,128]{1,0:T(8,128)(2,1)S(1)}, bf16[272,128]{1,0:T(8,128)(2,1)S(1)}, u32[]{:S(2)}, u32[]{:S(2)}) collective-permute-start(bf16[272,128]{1,0:T(8,128)(2,1)S(1)} %get-tuple-element.71), channel_id=1, source_target_pairs={{0,16},{4,20},{8,24},{12,28},{16,0},{20,4},{24,8},{28,12},{1,17},{... | collective-permute-start | bytes 208904 | tf_op jit(solution)/shard_map/ppermute | solution.py:207
  15.6 7.0 %slice-start = ((s8[6291456]{0:T(1024)(128)(4,1)}), s8[4194304]{0:T(1024)(128)(4,1)S(1)}, s32[]{:S(2)}) async-start(s8[6291456]{0:T(1024)(128)(4,1)} %bitcast.1), calls=%async_computation | async-start | bytes 8388608
  15.6 7.0 %copy-start.3 = (bf16[128,768]{1,0:T(8,128)(2,1)S(1)}, bf16[128,768]{1,0:T(8,128)(2,1)}, u32[]{:S(2)}) copy-start(bf16[128,768]{1,0:T(8,128)(2,1)} %rest_0_.1) | copy-start | bytes 589828
  19.0 3.7 %slice-start.1 = ((s8[6291456]{0:T(1024)(128)(4,1)}), s8[2097152]{0:T(1024)(128)(4,1)S(1)}, s32[]{:S(2)}) async-start(s8[6291456]{0:T(1024)(128)(4,1)} %bitcast.1), calls=%async_computation.1 | async-start | bytes 4194304
  19.1 5.0 %copy-start.2 = (bf16[128,1024]{1,0:T(8,128)(2,1)S(1)}, bf16[128,1024]{1,0:T(8,128)(2,1)}, u32[]{:S(2)}) copy-start(bf16[128,1024]{1,0:T(8,128)(2,1)} %q_ref.1) | copy-start | bytes 786436
  19.1 9.8 %collective-permute-start.14 = (bf16[256,128]{1,0:T(8,128)(2,1)S(1)}, bf16[256,128]{1,0:T(8,128)(2,1)S(1)}, u32[]{:S(2)}, u32[]{:S(2)}) collective-permute-start(bf16[256,128]{1,0:T(8,128)(2,1)S(1)} %get-tuple-element.74), channel_id=1, source_target_pairs={{0,4},{4,0},{8,12},{12,8},{16,20},{20,16},{24,28},{28,24},{1,5},{5... | collective-permute-start | bytes 196616 | tf_op jit(solution)/shard_map/ppermute | solution.py:188
  19.1 12.0 %collective-permute-start.15 = (bf16[256,128]{1,0:T(8,128)(2,1)S(1)}, bf16[256,128]{1,0:T(8,128)(2,1)S(1)}, u32[]{:S(2)}, u32[]{:S(2)}) collective-permute-start(bf16[256,128]{1,0:T(8,128)(2,1)S(1)} %get-tuple-element.75), channel_id=1, source_target_pairs={{0,8},{4,12},{8,0},{12,4},{16,24},{20,28},{24,16},{28,20},{1,9},{5... | collective-permute-start | bytes 196616 | tf_op jit(solution)/shard_map/ppermute | solution.py:188
  20.5 10.7 %collective-permute-start.16 = (bf16[256,128]{1,0:T(8,128)(2,1)S(1)}, bf16[256,128]{1,0:T(8,128)(2,1)S(1)}, u32[]{:S(2)}, u32[]{:S(2)}) collective-permute-start(bf16[256,128]{1,0:T(8,128)(2,1)S(1)} %get-tuple-element.76), channel_id=1, source_target_pairs={{0,12},{4,8},{8,4},{12,0},{16,28},{20,24},{24,20},{28,16},{1,13},{... | collective-permute-start | bytes 196616 | tf_op jit(solution)/shard_map/ppermute | solution.py:188
  22.6 1.4 %collective-permute-start.1 = (bf16[128,768]{1,0:T(8,128)(2,1)S(1)}, bf16[128,768]{1,0:T(8,128)(2,1)S(1)}, u32[]{:S(2)}, u32[]{:S(2)}) collective-permute-start(bf16[128,768]{1,0:T(8,128)(2,1)S(1)} %collective-permute-done.rest_0_), channel_id=1, source_target_pairs={{0,1},{1,0},{2,3},{3,2},{4,5},{5,4},{6,7},{7,6},{8,9},{9,8},{10,11... | collective-permute-start | bytes 589832 | tf_op jit(solution)/shard_map/ppermute | solution.py:188
  25.5 8.1 %collective-permute-start.3 = (bf16[272,128]{1,0:T(8,128)(2,1)S(1)}, bf16[272,128]{1,0:T(8,128)(2,1)S(1)}, u32[]{:S(2)}, u32[]{:S(2)}) collective-permute-start(bf16[272,128]{1,0:T(8,128)(2,1)S(1)} %get-tuple-element.56), channel_id=1, source_target_pairs={{0,4},{4,0},{8,12},{12,8},{16,20},{20,16},{24,28},{28,24},{1,5},{5... | collective-permute-start | bytes 208904 | tf_op jit(solution)/shard_map/ppermute | solution.py:188
  25.6 7.9 %collective-permute-start.4 = (bf16[272,128]{1,0:T(8,128)(2,1)S(1)}, bf16[272,128]{1,0:T(8,128)(2,1)S(1)}, u32[]{:S(2)}, u32[]{:S(2)}) collective-permute-start(bf16[272,128]{1,0:T(8,128)(2,1)S(1)} %get-tuple-element.57), channel_id=1, source_target_pairs={{0,8},{4,12},{8,0},{12,4},{16,24},{20,28},{24,16},{28,20},{1,9},{5... | collective-permute-start | bytes 208904 | tf_op jit(solution)/shard_map/ppermute | solution.py:188
  28.9 5.3 %collective-permute-start.5 = (bf16[272,128]{1,0:T(8,128)(2,1)S(1)}, bf16[272,128]{1,0:T(8,128)(2,1)S(1)}, u32[]{:S(2)}, u32[]{:S(2)}) collective-permute-start(bf16[272,128]{1,0:T(8,128)(2,1)S(1)} %get-tuple-element.58), channel_id=1, source_target_pairs={{0,12},{4,8},{8,4},{12,0},{16,28},{20,24},{24,20},{28,16},{1,13},{... | collective-permute-start | bytes 208904 | tf_op jit(solution)/shard_map/ppermute | solution.py:188
  33.0 11.2 %collective-permute-start.17 = (bf16[128,768]{1,0:T(8,128)(2,1)S(1)}, bf16[128,768]{1,0:T(8,128)(2,1)S(1)}, u32[]{:S(2)}, u32[]{:S(2)}) collective-permute-start(bf16[128,768]{1,0:T(8,128)(2,1)S(1)} %get-tuple-element.81), channel_id=1, source_target_pairs={{0,1},{1,0},{2,3},{3,2},{4,5},{5,4},{6,7},{7,6},{8,9},{9,8},{10,11... | collective-permute-start | bytes 589832 | tf_op jit(solution)/shard_map/ppermute | solution.py:188
  33.1 4.6 %collective-permute-start.18 = (bf16[128,768]{1,0:T(8,128)(2,1)S(1)}, bf16[128,768]{1,0:T(8,128)(2,1)S(1)}, u32[]{:S(2)}, u32[]{:S(2)}) collective-permute-start(bf16[128,768]{1,0:T(8,128)(2,1)S(1)} %get-tuple-element.83), channel_id=1, source_target_pairs={{0,1},{1,0},{2,3},{3,2},{4,5},{5,4},{6,7},{7,6},{8,9},{9,8},{10,11... | collective-permute-start | bytes 589832 | tf_op jit(solution)/shard_map/ppermute | solution.py:188
  34.3 6.2 %collective-permute-start.6 = (bf16[272,128]{1,0:T(8,128)(2,1)S(1)}, bf16[272,128]{1,0:T(8,128)(2,1)S(1)}, u32[]{:S(2)}, u32[]{:S(2)}) collective-permute-start(bf16[272,128]{1,0:T(8,128)(2,1)S(1)} %get-tuple-element.59), channel_id=1, source_target_pairs={{0,16},{4,20},{8,24},{12,28},{16,0},{20,4},{24,8},{28,12},{1,17},{... | collective-permute-start | bytes 208904 | tf_op jit(solution)/shard_map/ppermute | solution.py:207
  37.7 9.9 %collective-permute-start.19 = (bf16[128,768]{1,0:T(8,128)(2,1)S(1)}, bf16[128,768]{1,0:T(8,128)(2,1)S(1)}, u32[]{:S(2)}, u32[]{:S(2)}) collective-permute-start(bf16[128,768]{1,0:T(8,128)(2,1)S(1)} %add_convert_fusion), channel_id=1, source_target_pairs={{0,2},{1,3},{2,0},{3,1},{4,6},{5,7},{6,4},{7,5},{8,10},{9,11},{10,... | collective-permute-start | bytes 589832 | tf_op jit(solution)/shard_map/ppermute | solution.py:188
  40.6 4.3 %collective-permute-start.7 = (bf16[256,128]{1,0:T(8,128)(2,1)S(1)}, bf16[256,128]{1,0:T(8,128)(2,1)S(1)}, u32[]{:S(2)}, u32[]{:S(2)}) collective-permute-start(bf16[256,128]{1,0:T(8,128)(2,1)S(1)} %get-tuple-element.62), channel_id=1, source_target_pairs={{0,4},{4,0},{8,12},{12,8},{16,20},{20,16},{24,28},{28,24},{1,5},{5... | collective-permute-start | bytes 196616 | tf_op jit(solution)/shard_map/ppermute | solution.py:188
  40.7 4.3 %collective-permute-start.8 = (bf16[256,128]{1,0:T(8,128)(2,1)S(1)}, bf16[256,128]{1,0:T(8,128)(2,1)S(1)}, u32[]{:S(2)}, u32[]{:S(2)}) collective-permute-start(bf16[256,128]{1,0:T(8,128)(2,1)S(1)} %get-tuple-element.63), channel_id=1, source_target_pairs={{0,8},{4,12},{8,0},{12,4},{16,24},{20,28},{24,16},{28,20},{1,9},{5... | collective-permute-start | bytes 196616 | tf_op jit(solution)/shard_map/ppermute | solution.py:188
  42.5 5.2 %collective-permute-start.9 = (bf16[256,128]{1,0:T(8,128)(2,1)S(1)}, bf16[256,128]{1,0:T(8,128)(2,1)S(1)}, u32[]{:S(2)}, u32[]{:S(2)}) collective-permute-start(bf16[256,128]{1,0:T(8,128)(2,1)S(1)} %get-tuple-element.64), channel_id=1, source_target_pairs={{0,12},{4,8},{8,4},{12,0},{16,28},{20,24},{24,20},{28,16},{1,13},{... | collective-permute-start | bytes 196616 | tf_op jit(solution)/shard_map/ppermute | solution.py:188

commit v5 on v4

--- a/solution.py
+++ b/solution.py
@@ -259,6 +259,10 @@
     rest[-1][...] = grad_sum(offsets, rest[:-1], weight_ref)
 
 
+def more_grad_kernel(offsets, weight_ref, *rest):
+    rest[-1][...] = grad_sum(offsets, rest[:-2], weight_ref, rest[-2][...])
+
+
 def grad_kernel(plan, offsets, weight_ref, *rest):
     count = len(offsets)
     shards, (part_ref, cum_ref, rise_ref, q_ref) = rest[:count], rest[count : count + 4]
@@ -314,6 +318,10 @@
     mix(offsets, weight_ref, flat_ref, outs)
 
 
+def mix_kernel(offsets, weight_ref, flat_ref, *outs):
+    mix(offsets, weight_ref, flat_ref, outs)
+
+
 def near_mix_kernel(plan, offsets, weight_ref, flat_ref, lq_ref, g_rise_ref, *rest):
     ins, rest = rest[: plan.group], rest[plan.group :]
     query_grad, outs, (states, buffer, sems) = rest[0], rest[1:-3], rest[-3:]
@@ -334,30 +342,45 @@
         copy.wait()
 
 
-def last_kernel(plan, k_fall_ref, v_fall_ref, lk_ref, lv_ref, *rest):
-    ins, rest = rest[: plan.group], rest[plan.group :]
-    parts, (mixed, key_grad, value_grad) = rest[:3], rest[3:6]
-    states, mixed_buffer, key_buffer, value_buffer, sems = rest[6:]
+def key_value_part(plan, members, k_fall_ref, v_fall_ref, lk_ref, lv_ref, carries, key_out, value_out):
+    rank = positions(plan, -1)[0]
+    for slot, j in enumerate(members):
+        for i in range(plan.quarter):
+            at = aligned((rank ^ j) * plan.quarter + i, plan.width)
+            carry = carries[slot][i * plan.width : (i + 1) * plan.width, :]
+            start = (slot * plan.quarter + i) * plan.width
+            to = slice(start, start + plan.width)
+            key_out[:, to] = (lk_ref[:, at] + dot(v_fall_ref[:, at], carry, 1, 1)).astype(BF16)
+            value_out[:, to] = (lv_ref[:, at] + dot(k_fall_ref[:, at], carry, 1, 0)).astype(BF16)
+
+
+def early_kernel(plan, members, *refs):
+    key_value_part(plan, members, *refs[:4], refs[4:-2], *refs[-2:])
+
+
+def last_kernel(plan, early, late, k_fall_ref, v_fall_ref, lk_ref, lv_ref, *refs):
+    carries, refs = refs[: len(late)], refs[len(late) :]
+    done, parts, (mixed, key_grad, value_grad) = refs[:2], refs[2:5], refs[5:8]
+    mixed_buffer, key_buffer, value_buffer, sems = refs[8:]
+    rank, wide = positions(plan, -1)[0], plan.quarter * plan.width
     copies = []
 
     def send(src, dst):
         copies.append(pltpu.make_async_copy(src, dst, sems.at[len(copies)]))
         copies[-1].start()
 
+    def send_quarters(members, buffers):
+        for slot, j in enumerate(members):
+            at, to = slice(slot * wide, (slot + 1) * wide), aligned(rank ^ j, wide)
+            send(buffers[0].at[:, at], key_grad.at[:, to])
+            send(buffers[1].at[:, at], value_grad.at[:, to])
+
+    send_quarters(early, done)
     mixed_buffer[...] = sum(part[...].astype(F32) for part in parts).astype(BF16)
     send(mixed_buffer, mixed)
-    gather_states(plan, -1, ins, states)
-    wide = plan.quarter * plan.width
-    for h in range(plan.heads):
-        at = slice(h * plan.width, (h + 1) * plan.width)
-        carry = states[at, :]
-        key_buffer[:, at] = (lk_ref[:, at] + dot(v_fall_ref[:, at], carry, 1, 1)).astype(BF16)
-        value_buffer[:, at] = (lv_ref[:, at] + dot(k_fall_ref[:, at], carry, 1, 0)).astype(BF16)
-        if (h + 1) % plan.quarter == 0:
-            q = h // plan.quarter
-            at = slice(q * wide, (q + 1) * wide)
-            send(key_buffer.at[:, at], key_grad.at[:, at])
-            send(value_buffer.at[:, at], value_grad.at[:, at])
+    buffers = (key_buffer, value_buffer)
+    key_value_part(plan, late, k_fall_ref, v_fall_ref, lk_ref, lv_ref, carries, *buffers)
+    send_quarters(late, buffers)
     for copy in copies:
         copy.wait()
 
@@ -400,11 +423,17 @@
         [VMEM] * (1 + half),
         [weight] + [shards[o] for o in offsets[:half]],
     )
+    (part,) = call(
+        functools.partial(more_grad_kernel, [half]),
+        [shape(wide, F32)],
+        [VMEM] * 3,
+        [weight, shards[half], part],
+    )
     grad, q_rise, *summaries_back = call(
-        functools.partial(grad_kernel, plan, offsets[half:]),
+        functools.partial(grad_kernel, plan, offsets[half + 1 :]),
         [wide_bf] * 2 + summary_shapes(plan),
-        [VMEM] * (half + 5),
-        [weight] + [shards[o] for o in offsets[half:]] + [part, cum, rise, queries],
+        [VMEM] * (half + 4),
+        [weight] + [shards[o] for o in offsets[half + 1 :]] + [part, cum, rise, queries],
         [summary_scratch(plan)],
     )
     carries = scan_states(plan, summaries_back, -1)
@@ -417,13 +446,22 @@
     )
 
     held = pltpu.VMEM((flat, plan.width), BF16)
-    far, near = offsets[half:][::-1], offsets[:half][::-1]
+    far = [o for o in offsets[half:] if o & 1] + [o for o in offsets[half:] if not o & 1]
+    near = [o for o in offsets[:half] if o & 1] + [o for o in offsets[:half] if not o & 1]
+    odd = half // 2
+    feat_bf = shape((tok, feat), BF16)
     attn_out, *sent = call(
-        functools.partial(mix_first_kernel, plan, far),
-        [wide_bf] + [shape((tok, feat), BF16)] * half,
+        functools.partial(mix_first_kernel, plan, far[:odd]),
+        [wide_bf] + [feat_bf] * odd,
         [VMEM] * (3 + plan.group),
         [weight, local_out, q_rise] + states,
         [held],
+    )
+    sent += call(
+        functools.partial(mix_kernel, far[odd:]),
+        [feat_bf] * (half - odd),
+        [VMEM] * 2,
+        [weight, attn_out],
     )
     query_grad, *kept = call(
         functools.partial(near_mix_kernel, plan, near),
@@ -454,13 +492,23 @@
         hop *= 2
     last_parts = [near_parts[0], move(near_parts, half // 2)[half // 2], move(far_parts, half)[half]]
 
+    early = sorted({0, plan.group - 1})
+    late = [j for j in range(plan.group) if j not in early]
+    piece = plan.quarter * plan.width
+    falls = [k_fall, v_fall, local_k, local_v]
+    done = call(
+        functools.partial(early_kernel, plan, early),
+        [shape((tok, len(early) * piece), BF16)] * 2,
+        [VMEM] * (4 + len(early)),
+        falls + [carries[j] for j in early],
+    )
     mixed, key_grad, value_grad = call(
-        functools.partial(last_kernel, plan),
+        functools.partial(last_kernel, plan, early, late),
         [shape((tok, feat), BF16)] + [wide_bf] * 2,
-        [VMEM] * (7 + plan.group),
-        [k_fall, v_fall, local_k, local_v] + carries + last_parts,
-        [held, pltpu.VMEM((tok, feat), BF16)]
-        + [pltpu.VMEM(wide, BF16)] * 2
+        [VMEM] * (9 + len(late)),
+        falls + [carries[j] for j in late] + list(done) + last_parts,
+        [pltpu.VMEM((tok, feat), BF16)]
+        + [pltpu.VMEM((tok, max(1, len(late)) * piece), BF16)] * 2
         + [pltpu.SemaphoreType.DMA((2 * plan.group + 1,))],
         out_specs=[HBM] * 3,
     )

time: 49 us -> 51.5 us (1.051)
  waiting for transfers between devices: 14.7 us -> 16.2 us
    ppermute x18, waiting for transfers between devices: 9.11 us -> 11.5 us  [swap(): return lax.ppermute(value, axis, [(i, i ^ offset) for i in range(count)])]
    ppermute x2, waiting for transfers between devices: 5.57 us -> 4.62 us  [shift(): lax.ppermute(value, 'seq', [(i, (i + hop) % count) for i in range(count)])]
    pallas_call x14 -> x17, Pallas kernels: 8.76 us -> 9.26 us  [call(): pl.pallas_call(kernel, out_shape=outs, in_specs=specs, out_specs=out_spec...]
  transfers between devices with their start and end apart: 20 -> 20, of which waited for: 10 -> 8; matrix products, arithmetic and copies ran while one was open for 0% -> 0% of each run, Pallas kernels for 15% -> 16%
where the time goes in v5:
time: 51.5 us; the launch traced here: 51.3 us
  starting transfers between devices  24.7 us (48%)
  waiting for transfers between devices  16.2 us (31%)
  Pallas kernels  9.26 us (18%)
  between operations  0.91 us (2%)
    ppermute x18, starting transfers between devices, swap(): return lax.ppermute(value, axis, [(i, i ^ offset) for i in range(count)])  18.7 us
    ppermute x18, waiting for transfers between devices, swap(): return lax.ppermute(value, axis, [(i, i ^ offset) for i in range(count)])  11.5 us
    pallas_call x17, Pallas kernels, call(): pl.pallas_call(kernel, out_shape=outs, in_specs=specs, out_specs=out_spec...  9.26 us
    ppermute x2, starting transfers between devices, shift(): lax.ppermute(value, 'seq', [(i, (i + hop) % count) for i in range(count)])  5.96 us
    ppermute x2, waiting for transfers between devices, shift(): lax.ppermute(value, 'seq', [(i, (i + hop) % count) for i in range(count)])  4.62 us
  transfers between devices with their start and end apart: 20, of which 8 were waited for; matrix products, arithmetic and copies ran while one was open for 0% of the time, Pallas kernels for 16%

profile of v5, /device:TPU:0, one launch (start us, length us, event | category | flops | bytes accessed | tf_op | source)
XLA Modules:
  0.0 51.3 jit_solution(14837063685669801358)
XLA Ops:
  0.7 3.1 %collective-permute-start = (bf16[128,768]{1,0:T(8,128)(2,1)}, bf16[128,768]{1,0:T(8,128)(2,1)S(1)}, u32[]{:S(2)}, u32[]{:S(2)}) collective-permute-start(bf16[128,768]{1,0:T(8,128)(2,1)} %rest_0_.1), channel_id=1, source_target_pairs={{0,2},{1,3},{2,0},{3,1},{4,6},{5,7},{6,4},{7,5},{8,10},{9,11},{10,... | collective-permute-start | bytes 589832 | tf_op jit(solution)/shard_map/ppermute | solution.py:188
  3.8 0.7 %shard_map.94 = (f32[272,128]{1,0:T(8,128)S(1)}, bf16[272,128]{1,0:T(8,128)(2,1)S(1)}, bf16[272,128]{1,0:T(8,128)(2,1)S(1)}, bf16[272,128]{1,0:T(8,128)(2,1)S(1)...) custom-call(bf16[128,128]{1,0:T(8,128)(2,1)S(1)} %shard_map.93.lower, ...), custom_call_target="tpu_custom_call" | custom-call | flops 2400000000 | bytes 8000000 | tf_op jit(solution)/shard_map/pallas_call | solution.py:27
  4.5 1.6 %collective-permute-start.10 = (bf16[272,128]{1,0:T(8,128)(2,1)S(1)}, bf16[272,128]{1,0:T(8,128)(2,1)S(1)}, u32[]{:S(2)}, u32[]{:S(2)}) collective-permute-start(bf16[272,128]{1,0:T(8,128)(2,1)S(1)} %get-tuple-element.71), channel_id=1, source_target_pairs={{0,4},{4,0},{8,12},{12,8},{16,20},{20,16},{24,28},{28,24},{1,5},{5... | collective-permute-start | bytes 208904 | tf_op jit(solution)/shard_map/ppermute | solution.py:188
  6.0 1.6 %collective-permute-start.11 = (bf16[272,128]{1,0:T(8,128)(2,1)S(1)}, bf16[272,128]{1,0:T(8,128)(2,1)S(1)}, u32[]{:S(2)}, u32[]{:S(2)}) collective-permute-start(bf16[272,128]{1,0:T(8,128)(2,1)S(1)} %get-tuple-element.72), channel_id=1, source_target_pairs={{0,8},{4,12},{8,0},{12,4},{16,24},{20,28},{24,16},{28,20},{1,9},{5... | collective-permute-start | bytes 208904 | tf_op jit(solution)/shard_map/ppermute | solution.py:188
  7.6 0.4 collective-permute-start.12
  8.0 1.1 %collective-permute-done.10.rest_1_ = bf16[272,128]{1,0:T(8,128)(2,1)S(1)} collective-permute-done((bf16[272,128]{1,0:T(8,128)(2,1)S(1)}, bf16[272,128]{1,0:T(8,128)(2,1)S(1)}, u32[]{:S(2)}, u32[]{:S(2)}) %collective-permute-start.10) | collective-permute-done | bytes 69664 | tf_op jit(solution)/shard_map/ppermute | solution.py:188
  9.1 1.4 %collective-permute-done.11.rest_2_ = bf16[272,128]{1,0:T(8,128)(2,1)S(1)} collective-permute-done((bf16[272,128]{1,0:T(8,128)(2,1)S(1)}, bf16[272,128]{1,0:T(8,128)(2,1)S(1)}, u32[]{:S(2)}, u32[]{:S(2)}) %collective-permute-start.11) | collective-permute-done | bytes 69664 | tf_op jit(solution)/shard_map/ppermute | solution.py:188
  10.6 2.3 %collective-permute-done.12.rest_3_ = bf16[272,128]{1,0:T(8,128)(2,1)S(1)} collective-permute-done((bf16[272,128]{1,0:T(8,128)(2,1)S(1)}, bf16[272,128]{1,0:T(8,128)(2,1)S(1)}, u32[]{:S(2)}, u32[]{:S(2)}) %collective-permute-start.12) | collective-permute-done | bytes 69664 | tf_op jit(solution)/shard_map/ppermute | solution.py:188
  12.9 2.7 %collective-permute-start.13 = (bf16[272,128]{1,0:T(8,128)(2,1)S(1)}, bf16[272,128]{1,0:T(8,128)(2,1)S(1)}, u32[]{:S(2)}, u32[]{:S(2)}) collective-permute-start(bf16[272,128]{1,0:T(8,128)(2,1)S(1)} %get-tuple-element.74), channel_id=1, source_target_pairs={{0,16},{4,20},{8,24},{12,28},{16,0},{20,4},{24,8},{28,12},{1,17},{... | collective-permute-start | bytes 208904 | tf_op jit(solution)/shard_map/ppermute | solution.py:207
  15.6 3.3 %collective-permute-done.13.entry_ref = bf16[272,128]{1,0:T(8,128)(2,1)S(1)} collective-permute-done((bf16[272,128]{1,0:T(8,128)(2,1)S(1)}, bf16[272,128]{1,0:T(8,128)(2,1)S(1)}, u32[]{:S(2)}, u32[]{:S(2)}) %collective-permute-start.13) | collective-permute-done | bytes 69664 | tf_op jit(solution)/shard_map/ppermute | solution.py:207
  19.1 1.3 %collective-permute-start.15 = (bf16[256,128]{1,0:T(8,128)(2,1)S(1)}, bf16[256,128]{1,0:T(8,128)(2,1)S(1)}, u32[]{:S(2)}, u32[]{:S(2)}) collective-permute-start(bf16[256,128]{1,0:T(8,128)(2,1)S(1)} %get-tuple-element.78), channel_id=1, source_target_pairs={{0,8},{4,12},{8,0},{12,4},{16,24},{20,28},{24,16},{28,20},{1,9},{5... | collective-permute-start | bytes 196616 | tf_op jit(solution)/shard_map/ppermute | solution.py:188
  20.4 2.2 %collective-permute-start.16 = (bf16[256,128]{1,0:T(8,128)(2,1)S(1)}, bf16[256,128]{1,0:T(8,128)(2,1)S(1)}, u32[]{:S(2)}, u32[]{:S(2)}) collective-permute-start(bf16[256,128]{1,0:T(8,128)(2,1)S(1)} %get-tuple-element.79), channel_id=1, source_target_pairs={{0,12},{4,8},{8,4},{12,0},{16,28},{20,24},{24,20},{28,16},{1,13},{... | collective-permute-start | bytes 196616 | tf_op jit(solution)/shard_map/ppermute | solution.py:188
  22.7 1.2 %shard_map.95.rest_1_ = f32[128,1024]{1,0:T(8,128)S(1)} custom-call(bf16[1024,3072]{1,0:T(8,128)(2,1)S(1)} %bitcast.2, bf16[128,768]{1,0:T(8,128)(2,1)S(1)} %copy-done.3, bf16[128,768]{1,0:T(8,128)(2,1)S(1)} %collective-permute-done.2.rest_1_), custom_call_target="tpu_custom_call" | custom-call | flops 2400000000 | bytes 8000000 | tf_op jit(solution)/shard_map/pallas_call | solution.py:27
  23.8 0.7 %shard_map.96.rest_1_ = f32[128,1024]{1,0:T(8,128)S(1)} custom-call(bf16[1024,3072]{1,0:T(8,128)(2,1)S(1)} %bitcast.2, bf16[128,768]{1,0:T(8,128)(2,1)S(1)} %collective-permute-done.rest_0_, f32[128,1024]{1,0:T(8,128)S(1)} %shard_map.95.rest_1_), custom_call_target="tpu_custom_call" | custom-call | flops 2400000000 | bytes 8000000 | tf_op jit(solution)/shard_map/pallas_call | solution.py:27
  24.5 0.3 copy-done.2
  24.8 0.9 %shard_map.97 = (bf16[128,1024]{1,0:T(8,128)(2,1)S(1)}, bf16[128,1024]{1,0:T(8,128)(2,1)S(1)}, f32[272,128]{1,0:T(8,128)S(1)}, bf16[272,128]{1,0:T(8,128)(2,1)S(...) custom-call(bf16[1024,3072]{1,0:T(8,128)(2,1)S(1)} %bitcast.2, ...), custom_call_target="tpu_custom_call" | custom-call | flops 2400000000 | bytes 8000000 | tf_op jit(solution)/shard_map/pallas_call | solution.py:27
  25.8 1.3 %collective-permute-start.4 = (bf16[272,128]{1,0:T(8,128)(2,1)S(1)}, bf16[272,128]{1,0:T(8,128)(2,1)S(1)}, u32[]{:S(2)}, u32[]{:S(2)}) collective-permute-start(bf16[272,128]{1,0:T(8,128)(2,1)S(1)} %get-tuple-element.58), channel_id=1, source_target_pairs={{0,8},{4,12},{8,0},{12,4},{16,24},{20,28},{24,16},{28,20},{1,9},{5... | collective-permute-start | bytes 208904 | tf_op jit(solution)/shard_map/ppermute | solution.py:188
  27.1 2.0 %shard_map.98 = (f32[128,1024]{1,0:T(8,128)S(1)}, f32[128,1024]{1,0:T(8,128)S(1)}, f32[128,1024]{1,0:T(8,128)S(1)}, f32[128,1024]{1,0:T(8,128)S(1)}, bf16[128,10...) custom-call(f32[128,8]{1,0:T(8,128)S(1)} %get-tuple-element.48.rest_2_.cum_ref, ...), custom_call_target="tpu_custom_call" | custom-call | flops 2400000000 | bytes 8000000 | tf_op jit(solution)/shard_map/pallas_call | solution.py:27
  29.1 2.2 %collective-permute-start.5 = (bf16[272,128]{1,0:T(8,128)(2,1)S(1)}, bf16[272,128]{1,0:T(8,128)(2,1)S(1)}, u32[]{:S(2)}, u32[]{:S(2)}) collective-permute-start(bf16[272,128]{1,0:T(8,128)(2,1)S(1)} %get-tuple-element.59), channel_id=1, source_target_pairs={{0,12},{4,8},{8,4},{12,0},{16,28},{20,24},{24,20},{28,16},{1,13},{... | collective-permute-start | bytes 208904 | tf_op jit(solution)/shard_map/ppermute | solution.py:188
  31.3 0.6 %shard_map.106 = (bf16[128,1024]{1,0:T(8,128)(2,1)S(1)}, bf16[128,768]{1,0:T(8,128)(2,1)S(1)}) custom-call(bf16[1024,3072]{1,0:T(8,128)(2,1)S(1)} %bitcast.2, f32[128,1024]{1,0:T(8,128)S(1)} %get-tuple-element.68.local_ref, bf16[128,1024]{1,0:T(8,128)(2,1)S(1)} %get-tuple-element.69.rise_ref, bf16[256,128]{1,0:T(8,128)(2,1)S(1)} %get-tuple-element.76.rest_0_, ...), custom_call_target="tpu_custom_call" | custom-call | flops 2400000000 | bytes 8000000 | tf_op jit(solution)/shard_map/pallas_call | solution.py:27
  31.9 0.4 shard_map.108
  32.3 2.0 %collective-permute-done.5.rest_3_ = bf16[272,128]{1,0:T(8,128)(2,1)S(1)} collective-permute-done((bf16[272,128]{1,0:T(8,128)(2,1)S(1)}, bf16[272,128]{1,0:T(8,128)(2,1)S(1)}, u32[]{:S(2)}, u32[]{:S(2)}) %collective-permute-start.5) | collective-permute-done | bytes 69664 | tf_op jit(solution)/shard_map/ppermute | solution.py:188
  34.5 3.3 %collective-permute-start.6 = (bf16[272,128]{1,0:T(8,128)(2,1)S(1)}, bf16[272,128]{1,0:T(8,128)(2,1)S(1)}, u32[]{:S(2)}, u32[]{:S(2)}) collective-permute-start(bf16[272,128]{1,0:T(8,128)(2,1)S(1)} %get-tuple-element.60), channel_id=1, source_target_pairs={{0,16},{4,20},{8,24},{12,28},{16,0},{20,4},{24,8},{28,12},{1,17},{... | collective-permute-start | bytes 208904 | tf_op jit(solution)/shard_map/ppermute | solution.py:207
  37.8 1.1 %shard_map.107 = (bf16[128,1024]{1,0:T(8,128)(2,1)}, bf16[128,768]{1,0:T(8,128)(2,1)S(1)}, f32[128,768]{1,0:T(8,128)S(1)}) custom-call(bf16[1024,3072]{1,0:T(8,128)(2,1)S(1)} %bitcast.2, bf16[128,1024]{1,0:T(8,128)(2,1)S(1)} %get-tuple-element.80.flat_ref, f32[128,1024]{1,0:T(8,128)S(1)} %get-tuple-element.81.lq_ref, ...), custom_call_target="tpu_custom_call" | custom-call | flops 2400000000 | bytes 8000000 | tf_op jit(solution)/shard_map/pallas_call | solution.py:27
  38.9 0.5 collective-permute-start.18
  39.4 1.3 %collective-permute-done.6.entry_ref = bf16[272,128]{1,0:T(8,128)(2,1)S(1)} collective-permute-done((bf16[272,128]{1,0:T(8,128)(2,1)S(1)}, bf16[272,128]{1,0:T(8,128)(2,1)S(1)}, u32[]{:S(2)}, u32[]{:S(2)}) %collective-permute-start.6) | collective-permute-done | bytes 69664 | tf_op jit(solution)/shard_map/ppermute | solution.py:207
  40.9 1.7 %collective-permute-start.8 = (bf16[256,128]{1,0:T(8,128)(2,1)S(1)}, bf16[256,128]{1,0:T(8,128)(2,1)S(1)}, u32[]{:S(2)}, u32[]{:S(2)}) collective-permute-start(bf16[256,128]{1,0:T(8,128)(2,1)S(1)} %get-tuple-element.63), channel_id=1, source_target_pairs={{0,8},{4,12},{8,0},{12,4},{16,24},{20,28},{24,16},{28,20},{1,9},{5... | collective-permute-start | bytes 196616 | tf_op jit(solution)/shard_map/ppermute | solution.py:188
  42.6 1.7 %collective-permute-start.9 = (bf16[256,128]{1,0:T(8,128)(2,1)S(1)}, bf16[256,128]{1,0:T(8,128)(2,1)S(1)}, u32[]{:S(2)}, u32[]{:S(2)}) collective-permute-start(bf16[256,128]{1,0:T(8,128)(2,1)S(1)} %get-tuple-element.65), channel_id=1, source_target_pairs={{0,12},{4,8},{8,4},{12,0},{16,28},{20,24},{24,20},{28,16},{1,13},{... | collective-permute-start | bytes 196616 | tf_op jit(solution)/shard_map/ppermute | solution.py:188
  44.4 0.8 %collective-permute-start.19 = (bf16[128,768]{1,0:T(8,128)(2,1)S(1)}, bf16[128,768]{1,0:T(8,128)(2,1)S(1)}, u32[]{:S(2)}, u32[]{:S(2)}) collective-permute-start(bf16[128,768]{1,0:T(8,128)(2,1)S(1)} %add_convert_fusion), channel_id=1, source_target_pairs={{0,2},{1,3},{2,0},{3,1},{4,6},{5,7},{6,4},{7,5},{8,10},{9,11},{10,... | collective-permute-start | bytes 589832 | tf_op jit(solution)/shard_map/ppermute | solution.py:188
  45.2 2.6 %collective-permute-done.9.refs_5_ = bf16[256,128]{1,0:T(8,128)(2,1)S(1)} collective-permute-done((bf16[256,128]{1,0:T(8,128)(2,1)S(1)}, bf16[256,128]{1,0:T(8,128)(2,1)S(1)}, u32[]{:S(2)}, u32[]{:S(2)}) %collective-permute-start.9) | collective-permute-done | bytes 65568 | tf_op jit(solution)/shard_map/ppermute | solution.py:188
  48.1 2.1 %collective-permute-done.19.refs_6_ = bf16[128,768]{1,0:T(8,128)(2,1)S(1)} collective-permute-done((bf16[128,768]{1,0:T(8,128)(2,1)S(1)}, bf16[128,768]{1,0:T(8,128)(2,1)S(1)}, u32[]{:S(2)}, u32[]{:S(2)}) %collective-permute-start.19) | collective-permute-done | bytes 196640 | tf_op jit(solution)/shard_map/ppermute | solution.py:188
  50.2 1.1 %shard_map.109 = (bf16[128,768]{1,0:T(8,128)(2,1)}, bf16[128,1024]{1,0:T(8,128)(2,1)}, bf16[128,1024]{1,0:T(8,128)(2,1)}) custom-call(bf16[128,1024]{1,0:T(8,128)(2,1)S(1)} %get-tuple-element.47.refs_0_.k_fall_ref, bf16[128,1024]{1,0:T(8,128)(2,1)S(1)} %get-tuple-element.53.refs_1_.v_fall_ref, f32[128,1024]{1,0:T(8,128)S(1)} %get-tuple-element.54.refs_2_.lk_ref, ...), custom_call_target="tpu_custom_call" | custom-call | flops 2400000000 | bytes 8000000 | tf_op jit(solution)/shard_map/pallas_call | solution.py:27
  (41 shorter events, 1.1 us)
Async XLA Ops:
  0.6 3.1 %copy-start.1 = (bf16[128,1024]{1,0:T(8,128)(2,1)S(1)}, bf16[128,1024]{1,0:T(8,128)(2,1)}, u32[]{:S(2)}) copy-start(bf16[128,1024]{1,0:T(8,128)(2,1)} %v_ref.3) | copy-start | bytes 786436
  0.6 3.1 %copy-start = (bf16[128,1024]{1,0:T(8,128)(2,1)S(1)}, bf16[128,1024]{1,0:T(8,128)(2,1)}, u32[]{:S(2)}) copy-start(bf16[128,1024]{1,0:T(8,128)(2,1)} %k_ref.3) | copy-start | bytes 786436
  0.7 3.1 %copy-start.4 = (s32[128,8]{0,1:T(8,128)S(1)}, s32[128,8]{0,1:T(8,128)}, u32[]{:S(2)}) copy-start(s32[128,8]{0,1:T(8,128)} %param.9) | copy-start | bytes 12292
  0.7 21.9 %collective-permute-start = (bf16[128,768]{1,0:T(8,128)(2,1)}, bf16[128,768]{1,0:T(8,128)(2,1)S(1)}, u32[]{:S(2)}, u32[]{:S(2)}) collective-permute-start(bf16[128,768]{1,0:T(8,128)(2,1)} %rest_0_.1), channel_id=1, source_target_pairs={{0,2},{1,3},{2,0},{3,1},{4,6},{5,7},{6,4},{7,5},{8,10},{9,11},{10,... | collective-permute-start | bytes 589832 | tf_op jit(solution)/shard_map/ppermute | solution.py:188
  3.7 18.9 %collective-permute-start.2 = (bf16[128,768]{1,0:T(8,128)(2,1)}, bf16[128,768]{1,0:T(8,128)(2,1)S(1)}, u32[]{:S(2)}, u32[]{:S(2)}) collective-permute-start(bf16[128,768]{1,0:T(8,128)(2,1)} %rest_0_.1), channel_id=1, source_target_pairs={{0,1},{1,0},{2,3},{3,2},{4,5},{5,4},{6,7},{7,6},{8,9},{9,8},{10,11... | collective-permute-start | bytes 589832 | tf_op jit(solution)/shard_map/ppermute | solution.py:188
  4.5 4.7 %collective-permute-start.10 = (bf16[272,128]{1,0:T(8,128)(2,1)S(1)}, bf16[272,128]{1,0:T(8,128)(2,1)S(1)}, u32[]{:S(2)}, u32[]{:S(2)}) collective-permute-start(bf16[272,128]{1,0:T(8,128)(2,1)S(1)} %get-tuple-element.71), channel_id=1, source_target_pairs={{0,4},{4,0},{8,12},{12,8},{16,20},{20,16},{24,28},{28,24},{1,5},{5... | collective-permute-start | bytes 208904 | tf_op jit(solution)/shard_map/ppermute | solution.py:188
  6.0 4.5 %collective-permute-start.11 = (bf16[272,128]{1,0:T(8,128)(2,1)S(1)}, bf16[272,128]{1,0:T(8,128)(2,1)S(1)}, u32[]{:S(2)}, u32[]{:S(2)}) collective-permute-start(bf16[272,128]{1,0:T(8,128)(2,1)S(1)} %get-tuple-element.72), channel_id=1, source_target_pairs={{0,8},{4,12},{8,0},{12,4},{16,24},{20,28},{24,16},{28,20},{1,9},{5... | collective-permute-start | bytes 208904 | tf_op jit(solution)/shard_map/ppermute | solution.py:188
  7.6 5.2 %collective-permute-start.12 = (bf16[272,128]{1,0:T(8,128)(2,1)S(1)}, bf16[272,128]{1,0:T(8,128)(2,1)S(1)}, u32[]{:S(2)}, u32[]{:S(2)}) collective-permute-start(bf16[272,128]{1,0:T(8,128)(2,1)S(1)} %get-tuple-element.73), channel_id=1, source_target_pairs={{0,12},{4,8},{8,4},{12,0},{16,28},{20,24},{24,20},{28,16},{1,13},{... | collective-permute-start | bytes 208904 | tf_op jit(solution)/shard_map/ppermute | solution.py:188
  12.9 6.0 %collective-permute-start.13 = (bf16[272,128]{1,0:T(8,128)(2,1)S(1)}, bf16[272,128]{1,0:T(8,128)(2,1)S(1)}, u32[]{:S(2)}, u32[]{:S(2)}) collective-permute-start(bf16[272,128]{1,0:T(8,128)(2,1)S(1)} %get-tuple-element.74), channel_id=1, source_target_pairs={{0,16},{4,20},{8,24},{12,28},{16,0},{20,4},{24,8},{28,12},{1,17},{... | collective-permute-start | bytes 208904 | tf_op jit(solution)/shard_map/ppermute | solution.py:207
  15.6 7.0 %slice-start = ((s8[6291456]{0:T(1024)(128)(4,1)}), s8[4194304]{0:T(1024)(128)(4,1)S(1)}, s32[]{:S(2)}) async-start(s8[6291456]{0:T(1024)(128)(4,1)} %bitcast.1), calls=%async_computation | async-start | bytes 8388608
  15.6 7.0 %copy-start.3 = (bf16[128,768]{1,0:T(8,128)(2,1)S(1)}, bf16[128,768]{1,0:T(8,128)(2,1)}, u32[]{:S(2)}) copy-start(bf16[128,768]{1,0:T(8,128)(2,1)} %rest_0_.1) | copy-start | bytes 589828
  19.0 3.7 %slice-start.1 = ((s8[6291456]{0:T(1024)(128)(4,1)}), s8[2097152]{0:T(1024)(128)(4,1)S(1)}, s32[]{:S(2)}) async-start(s8[6291456]{0:T(1024)(128)(4,1)} %bitcast.1), calls=%async_computation.1 | async-start | bytes 4194304
  19.0 10.1 %collective-permute-start.14 = (bf16[256,128]{1,0:T(8,128)(2,1)S(1)}, bf16[256,128]{1,0:T(8,128)(2,1)S(1)}, u32[]{:S(2)}, u32[]{:S(2)}) collective-permute-start(bf16[256,128]{1,0:T(8,128)(2,1)S(1)} %get-tuple-element.77), channel_id=1, source_target_pairs={{0,4},{4,0},{8,12},{12,8},{16,20},{20,16},{24,28},{28,24},{1,5},{5... | collective-permute-start | bytes 196616 | tf_op jit(solution)/shard_map/ppermute | solution.py:188
  19.1 12.2 %collective-permute-start.15 = (bf16[256,128]{1,0:T(8,128)(2,1)S(1)}, bf16[256,128]{1,0:T(8,128)(2,1)S(1)}, u32[]{:S(2)}, u32[]{:S(2)}) collective-permute-start(bf16[256,128]{1,0:T(8,128)(2,1)S(1)} %get-tuple-element.78), channel_id=1, source_target_pairs={{0,8},{4,12},{8,0},{12,4},{16,24},{20,28},{24,16},{28,20},{1,9},{5... | collective-permute-start | bytes 196616 | tf_op jit(solution)/shard_map/ppermute | solution.py:188
  20.4 10.9 %collective-permute-start.16 = (bf16[256,128]{1,0:T(8,128)(2,1)S(1)}, bf16[256,128]{1,0:T(8,128)(2,1)S(1)}, u32[]{:S(2)}, u32[]{:S(2)}) collective-permute-start(bf16[256,128]{1,0:T(8,128)(2,1)S(1)} %get-tuple-element.79), channel_id=1, source_target_pairs={{0,12},{4,8},{8,4},{12,0},{16,28},{20,24},{24,20},{28,16},{1,13},{... | collective-permute-start | bytes 196616 | tf_op jit(solution)/shard_map/ppermute | solution.py:188
  22.6 1.9 %collective-permute-start.1 = (bf16[128,768]{1,0:T(8,128)(2,1)S(1)}, bf16[128,768]{1,0:T(8,128)(2,1)S(1)}, u32[]{:S(2)}, u32[]{:S(2)}) collective-permute-start(bf16[128,768]{1,0:T(8,128)(2,1)S(1)} %collective-permute-done.rest_0_), channel_id=1, source_target_pairs={{0,1},{1,0},{2,3},{3,2},{4,5},{5,4},{6,7},{7,6},{8,9},{9,8},{10,11... | collective-permute-start | bytes 589832 | tf_op jit(solution)/shard_map/ppermute | solution.py:188
  23.8 1.0 %copy-start.2 = (bf16[128,1024]{1,0:T(8,128)(2,1)S(1)}, bf16[128,1024]{1,0:T(8,128)(2,1)}, u32[]{:S(2)}) copy-start(bf16[128,1024]{1,0:T(8,128)(2,1)} %q_ref.1) | copy-start | bytes 786436
  25.7 6.6 %collective-permute-start.3 = (bf16[272,128]{1,0:T(8,128)(2,1)S(1)}, bf16[272,128]{1,0:T(8,128)(2,1)S(1)}, u32[]{:S(2)}, u32[]{:S(2)}) collective-permute-start(bf16[272,128]{1,0:T(8,128)(2,1)S(1)} %get-tuple-element.57), channel_id=1, source_target_pairs={{0,4},{4,0},{8,12},{12,8},{16,20},{20,16},{24,28},{28,24},{1,5},{5... | collective-permute-start | bytes 208904 | tf_op jit(solution)/shard_map/ppermute | solution.py:188
  25.8 6.5 %collective-permute-start.4 = (bf16[272,128]{1,0:T(8,128)(2,1)S(1)}, bf16[272,128]{1,0:T(8,128)(2,1)S(1)}, u32[]{:S(2)}, u32[]{:S(2)}) collective-permute-start(bf16[272,128]{1,0:T(8,128)(2,1)S(1)} %get-tuple-element.58), channel_id=1, source_target_pairs={{0,8},{4,12},{8,0},{12,4},{16,24},{20,28},{24,16},{28,20},{1,9},{5... | collective-permute-start | bytes 208904 | tf_op jit(solution)/shard_map/ppermute | solution.py:188
  29.1 5.3 %collective-permute-start.5 = (bf16[272,128]{1,0:T(8,128)(2,1)S(1)}, bf16[272,128]{1,0:T(8,128)(2,1)S(1)}, u32[]{:S(2)}, u32[]{:S(2)}) collective-permute-start(bf16[272,128]{1,0:T(8,128)(2,1)S(1)} %get-tuple-element.59), channel_id=1, source_target_pairs={{0,12},{4,8},{8,4},{12,0},{16,28},{20,24},{24,20},{28,16},{1,13},{... | collective-permute-start | bytes 208904 | tf_op jit(solution)/shard_map/ppermute | solution.py:188
  34.5 6.2 %collective-permute-start.6 = (bf16[272,128]{1,0:T(8,128)(2,1)S(1)}, bf16[272,128]{1,0:T(8,128)(2,1)S(1)}, u32[]{:S(2)}, u32[]{:S(2)}) collective-permute-start(bf16[272,128]{1,0:T(8,128)(2,1)S(1)} %get-tuple-element.60), channel_id=1, source_target_pairs={{0,16},{4,20},{8,24},{12,28},{16,0},{20,4},{24,8},{28,12},{1,17},{... | collective-permute-start | bytes 208904 | tf_op jit(solution)/shard_map/ppermute | solution.py:207
  38.9 9.2 %collective-permute-start.17 = (bf16[128,768]{1,0:T(8,128)(2,1)S(1)}, bf16[128,768]{1,0:T(8,128)(2,1)S(1)}, u32[]{:S(2)}, u32[]{:S(2)}) collective-permute-start(bf16[128,768]{1,0:T(8,128)(2,1)S(1)} %get-tuple-element.84), channel_id=1, source_target_pairs={{0,1},{1,0},{2,3},{3,2},{4,5},{5,4},{6,7},{7,6},{8,9},{9,8},{10,11... | collective-permute-start | bytes 589832 | tf_op jit(solution)/shard_map/ppermute | solution.py:188
  38.9 5.4 %collective-permute-start.18 = (bf16[128,768]{1,0:T(8,128)(2,1)S(1)}, bf16[128,768]{1,0:T(8,128)(2,1)S(1)}, u32[]{:S(2)}, u32[]{:S(2)}) collective-permute-start(bf16[128,768]{1,0:T(8,128)(2,1)S(1)} %get-tuple-element.85), channel_id=1, source_target_pairs={{0,1},{1,0},{2,3},{3,2},{4,5},{5,4},{6,7},{7,6},{8,9},{9,8},{10,11... | collective-permute-start | bytes 589832 | tf_op jit(solution)/shard_map/ppermute | solution.py:188
  40.8 7.3 %collective-permute-start.7 = (bf16[256,128]{1,0:T(8,128)(2,1)S(1)}, bf16[256,128]{1,0:T(8,128)(2,1)S(1)}, u32[]{:S(2)}, u32[]{:S(2)}) collective-permute-start(bf16[256,128]{1,0:T(8,128)(2,1)S(1)} %get-tuple-element.62), channel_id=1, source_target_pairs={{0,4},{4,0},{8,12},{12,8},{16,20},{20,16},{24,28},{28,24},{1,5},{5... | collective-permute-start | bytes 196616 | tf_op jit(solution)/shard_map/ppermute | solution.py:188
  40.9 7.2 %collective-permute-start.8 = (bf16[256,128]{1,0:T(8,128)(2,1)S(1)}, bf16[256,128]{1,0:T(8,128)(2,1)S(1)}, u32[]{:S(2)}, u32[]{:S(2)}) collective-permute-start(bf16[256,128]{1,0:T(8,128)(2,1)S(1)} %get-tuple-element.63), channel_id=1, source_target_pairs={{0,8},{4,12},{8,0},{12,4},{16,24},{20,28},{24,16},{28,20},{1,9},{5... | collective-permute-start | bytes 196616 | tf_op jit(solution)/shard_map/ppermute | solution.py:188
  42.6 5.2 %collective-permute-start.9 = (bf16[256,128]{1,0:T(8,128)(2,1)S(1)}, bf16[256,128]{1,0:T(8,128)(2,1)S(1)}, u32[]{:S(2)}, u32[]{:S(2)}) collective-permute-start(bf16[256,128]{1,0:T(8,128)(2,1)S(1)} %get-tuple-element.65), channel_id=1, source_target_pairs={{0,12},{4,8},{8,4},{12,0},{16,28},{20,24},{24,20},{28,16},{1,13},{... | collective-permute-start | bytes 196616 | tf_op jit(solution)/shard_map/ppermute | solution.py:188
  44.4 5.7 %collective-permute-start.19 = (bf16[128,768]{1,0:T(8,128)(2,1)S(1)}, bf16[128,768]{1,0:T(8,128)(2,1)S(1)}, u32[]{:S(2)}, u32[]{:S(2)}) collective-permute-start(bf16[128,768]{1,0:T(8,128)(2,1)S(1)} %add_convert_fusion), channel_id=1, source_target_pairs={{0,2},{1,3},{2,0},{3,1},{4,6},{5,7},{6,4},{7,5},{8,10},{9,11},{10,... | collective-permute-start | bytes 589832 | tf_op jit(solution)/shard_map/ppermute | solution.py:188

commit v6 on v5

--- a/solution.py
+++ b/solution.py
@@ -282,24 +282,33 @@
     put_summaries(plan, rank, left, lambda h: grad_ref[:, cols(h)], cum_ref[...], outs, scratch)
 
 
-def local_kernel(plan, cum_ref, cum_t_ref, rise_ref, fall_ref, q_ref, k_ref, v_ref, grad_ref, *outs):
-    out_ref, lq_ref, lk_ref, lv_ref, g_rise_ref, v_fall_ref = outs
+def local_kernel(plan, cum_ref, cum_t_ref, q_ref, k_ref, v_ref, grad_ref, attn_ref, pmat_ref, out_ref):
     scale = 1.0 / plan.width
     size = (plan.tok, plan.tok)
     lower = lax.broadcasted_iota(jnp.int32, size, 0) >= lax.broadcasted_iota(jnp.int32, size, 1)
     for h in range(plan.heads):
         at = slice(h * plan.width, (h + 1) * plan.width)
+        rows = slice(h * plan.tok, (h + 1) * plan.tok)
         gap = cum_ref[:, h : h + 1] - cum_t_ref[h : h + 1, :]
         mask = jnp.where(lower, jnp.exp(jnp.where(lower, gap, 0.0)), 0.0)
-        q, k, v, grad = q_ref[:, at], k_ref[:, at], v_ref[:, at], grad_ref[:, at]
-        attn = (scale * dot(q, k, 1, 1) * mask).astype(BF16)
-        pmat = (scale * dot(grad, v, 1, 1) * mask).astype(BF16)
+        v = v_ref[:, at]
+        attn = (scale * dot(q_ref[:, at], k_ref[:, at], 1, 1) * mask).astype(BF16)
+        attn_ref[rows, :] = attn
+        pmat_ref[rows, :] = (scale * dot(grad_ref[:, at], v, 1, 1) * mask).astype(BF16)
         out_ref[:, at] = dot(attn, v, 1, 0)
-        lq_ref[:, at] = dot(pmat, k, 1, 0)
-        lk_ref[:, at] = dot(pmat, q, 0, 0)
+
+
+def local_grad_kernel(plan, rise_ref, fall_ref, q_ref, k_ref, v_ref, grad_ref, attn_ref, pmat_ref, *outs):
+    lq_ref, lk_ref, lv_ref, g_rise_ref, v_fall_ref = outs
+    for h in range(plan.heads):
+        at = slice(h * plan.width, (h + 1) * plan.width)
+        rows = slice(h * plan.tok, (h + 1) * plan.tok)
+        attn, pmat, grad = attn_ref[rows, :], pmat_ref[rows, :], grad_ref[:, at]
+        lq_ref[:, at] = dot(pmat, k_ref[:, at], 1, 0)
+        lk_ref[:, at] = dot(pmat, q_ref[:, at], 0, 0)
         lv_ref[:, at] = dot(attn, grad, 0, 0)
         g_rise_ref[:, at] = (rise_ref[:, h : h + 1] * grad.astype(F32)).astype(BF16)
-        v_fall_ref[:, at] = (fall_ref[:, h : h + 1] * v.astype(F32)).astype(BF16)
+        v_fall_ref[:, at] = (fall_ref[:, h : h + 1] * v_ref[:, at].astype(F32)).astype(BF16)
 
 
 def mix(offsets, weight_ref, flat_ref, outs):
@@ -438,11 +447,18 @@
     )
     carries = scan_states(plan, summaries_back, -1)
 
-    local_out, local_q, local_k, local_v, g_rise, v_fall = call(
+    scores = shape((heads * tok, tok), BF16)
+    attn, pmat, local_out = call(
         functools.partial(local_kernel, plan),
-        [shape(wide, F32)] * 4 + [wide_bf] * 2,
+        [scores, scores, shape(wide, F32)],
+        [VMEM] * 6,
+        [cum, cum_t, queries, keys, values, grad],
+    )
+    local_q, local_k, local_v, g_rise, v_fall = call(
+        functools.partial(local_grad_kernel, plan),
+        [shape(wide, F32)] * 3 + [wide_bf] * 2,
         [VMEM] * 8,
-        [cum, cum_t, rise, fall, queries, keys, values, grad],
+        [rise, fall, queries, keys, values, grad, attn, pmat],
     )
 
     held = pltpu.VMEM((flat, plan.width), BF16)
@@ -492,7 +508,7 @@
         hop *= 2
     last_parts = [near_parts[0], move(near_parts, half // 2)[half // 2], move(far_parts, half)[half]]
 
-    early = sorted({0, plan.group - 1})
+    early = [j for j in range(plan.group) if j != 1]
     late = [j for j in range(plan.group) if j not in early]
     piece = plan.quarter * plan.width
     falls = [k_fall, v_fall, local_k, local_v]

time: 51.5 us -> 50.3 us (0.977)
  Pallas kernels: 9.26 us -> 8.71 us
    ppermute x18, waiting for transfers between devices: 11.5 us -> 10.8 us  [swap(): return lax.ppermute(value, axis, [(i, i ^ offset) for i in range(count)])]
    pallas_call x17 -> x18, Pallas kernels: 9.26 us -> 8.71 us  [call(): pl.pallas_call(kernel, out_shape=outs, in_specs=specs, out_specs=out_spec...]
  transfers between devices with their start and end apart: 20 -> 20, of which waited for: 8 -> 8; matrix products, arithmetic and copies ran while one was open for 0% -> 0% of each run, Pallas kernels for 16% -> 15%
where the time goes in v6:
time: 50.3 us; the launch traced here: 50.1 us
  starting transfers between devices  24.2 us (48%)
  waiting for transfers between devices  16 us (32%)
  Pallas kernels  8.71 us (17%)
  between operations  0.92 us (2%)
    ppermute x18, starting transfers between devices, swap(): return lax.ppermute(value, axis, [(i, i ^ offset) for i in range(count)])  18.3 us
    ppermute x18, waiting for transfers between devices, swap(): return lax.ppermute(value, axis, [(i, i ^ offset) for i in range(count)])  10.8 us
    pallas_call x18, Pallas kernels, call(): pl.pallas_call(kernel, out_shape=outs, in_specs=specs, out_specs=out_spec...  8.71 us
    ppermute x2, starting transfers between devices, shift(): lax.ppermute(value, 'seq', [(i, (i + hop) % count) for i in range(count)])  5.98 us
    ppermute x2, waiting for transfers between devices, shift(): lax.ppermute(value, 'seq', [(i, (i + hop) % count) for i in range(count)])  5.13 us
  transfers between devices with their start and end apart: 20, of which 8 were waited for; matrix products, arithmetic and copies ran while one was open for 0% of the time, Pallas kernels for 15%

profile of v6, /device:TPU:0, one launch (start us, length us, event | category | flops | bytes accessed | tf_op | source)
XLA Modules:
  0.0 50.1 jit_solution(1531978681633249007)
XLA Ops:
  0.7 3.1 %collective-permute-start = (bf16[128,768]{1,0:T(8,128)(2,1)}, bf16[128,768]{1,0:T(8,128)(2,1)S(1)}, u32[]{:S(2)}, u32[]{:S(2)}) collective-permute-start(bf16[128,768]{1,0:T(8,128)(2,1)} %rest_0_.1), channel_id=1, source_target_pairs={{0,2},{1,3},{2,0},{3,1},{4,6},{5,7},{6,4},{7,5},{8,10},{9,11},{10,... | collective-permute-start | bytes 589832 | tf_op jit(solution)/shard_map/ppermute | solution.py:188
  3.8 0.7 %shard_map.94 = (f32[272,128]{1,0:T(8,128)S(1)}, bf16[272,128]{1,0:T(8,128)(2,1)S(1)}, bf16[272,128]{1,0:T(8,128)(2,1)S(1)}, bf16[272,128]{1,0:T(8,128)(2,1)S(1)...) custom-call(bf16[128,128]{1,0:T(8,128)(2,1)S(1)} %shard_map.93.lower, ...), custom_call_target="tpu_custom_call" | custom-call | flops 2400000000 | bytes 8000000 | tf_op jit(solution)/shard_map/pallas_call | solution.py:27
  4.5 1.6 %collective-permute-start.10 = (bf16[272,128]{1,0:T(8,128)(2,1)S(1)}, bf16[272,128]{1,0:T(8,128)(2,1)S(1)}, u32[]{:S(2)}, u32[]{:S(2)}) collective-permute-start(bf16[272,128]{1,0:T(8,128)(2,1)S(1)} %get-tuple-element.75), channel_id=1, source_target_pairs={{0,4},{4,0},{8,12},{12,8},{16,20},{20,16},{24,28},{28,24},{1,5},{5... | collective-permute-start | bytes 208904 | tf_op jit(solution)/shard_map/ppermute | solution.py:188
  6.0 1.6 %collective-permute-start.11 = (bf16[272,128]{1,0:T(8,128)(2,1)S(1)}, bf16[272,128]{1,0:T(8,128)(2,1)S(1)}, u32[]{:S(2)}, u32[]{:S(2)}) collective-permute-start(bf16[272,128]{1,0:T(8,128)(2,1)S(1)} %get-tuple-element.76), channel_id=1, source_target_pairs={{0,8},{4,12},{8,0},{12,4},{16,24},{20,28},{24,16},{28,20},{1,9},{5... | collective-permute-start | bytes 208904 | tf_op jit(solution)/shard_map/ppermute | solution.py:188
  7.6 0.4 collective-permute-start.12
  8.0 1.1 %collective-permute-done.10.rest_1_ = bf16[272,128]{1,0:T(8,128)(2,1)S(1)} collective-permute-done((bf16[272,128]{1,0:T(8,128)(2,1)S(1)}, bf16[272,128]{1,0:T(8,128)(2,1)S(1)}, u32[]{:S(2)}, u32[]{:S(2)}) %collective-permute-start.10) | collective-permute-done | bytes 69664 | tf_op jit(solution)/shard_map/ppermute | solution.py:188
  9.1 1.4 %collective-permute-done.11.rest_2_ = bf16[272,128]{1,0:T(8,128)(2,1)S(1)} collective-permute-done((bf16[272,128]{1,0:T(8,128)(2,1)S(1)}, bf16[272,128]{1,0:T(8,128)(2,1)S(1)}, u32[]{:S(2)}, u32[]{:S(2)}) %collective-permute-start.11) | collective-permute-done | bytes 69664 | tf_op jit(solution)/shard_map/ppermute | solution.py:188
  10.6 2.3 %collective-permute-done.12.rest_3_ = bf16[272,128]{1,0:T(8,128)(2,1)S(1)} collective-permute-done((bf16[272,128]{1,0:T(8,128)(2,1)S(1)}, bf16[272,128]{1,0:T(8,128)(2,1)S(1)}, u32[]{:S(2)}, u32[]{:S(2)}) %collective-permute-start.12) | collective-permute-done | bytes 69664 | tf_op jit(solution)/shard_map/ppermute | solution.py:188
  12.9 2.7 %collective-permute-start.13 = (bf16[272,128]{1,0:T(8,128)(2,1)S(1)}, bf16[272,128]{1,0:T(8,128)(2,1)S(1)}, u32[]{:S(2)}, u32[]{:S(2)}) collective-permute-start(bf16[272,128]{1,0:T(8,128)(2,1)S(1)} %get-tuple-element.78), channel_id=1, source_target_pairs={{0,16},{4,20},{8,24},{12,28},{16,0},{20,4},{24,8},{28,12},{1,17},{... | collective-permute-start | bytes 208904 | tf_op jit(solution)/shard_map/ppermute | solution.py:207
  15.6 3.3 %collective-permute-done.13.entry_ref = bf16[272,128]{1,0:T(8,128)(2,1)S(1)} collective-permute-done((bf16[272,128]{1,0:T(8,128)(2,1)S(1)}, bf16[272,128]{1,0:T(8,128)(2,1)S(1)}, u32[]{:S(2)}, u32[]{:S(2)}) %collective-permute-start.13) | collective-permute-done | bytes 69664 | tf_op jit(solution)/shard_map/ppermute | solution.py:207
  19.1 1.3 %collective-permute-start.15 = (bf16[256,128]{1,0:T(8,128)(2,1)S(1)}, bf16[256,128]{1,0:T(8,128)(2,1)S(1)}, u32[]{:S(2)}, u32[]{:S(2)}) collective-permute-start(bf16[256,128]{1,0:T(8,128)(2,1)S(1)} %get-tuple-element.82), channel_id=1, source_target_pairs={{0,8},{4,12},{8,0},{12,4},{16,24},{20,28},{24,16},{28,20},{1,9},{5... | collective-permute-start | bytes 196616 | tf_op jit(solution)/shard_map/ppermute | solution.py:188
  20.4 2.2 %collective-permute-start.16 = (bf16[256,128]{1,0:T(8,128)(2,1)S(1)}, bf16[256,128]{1,0:T(8,128)(2,1)S(1)}, u32[]{:S(2)}, u32[]{:S(2)}) collective-permute-start(bf16[256,128]{1,0:T(8,128)(2,1)S(1)} %get-tuple-element.83), channel_id=1, source_target_pairs={{0,12},{4,8},{8,4},{12,0},{16,28},{20,24},{24,20},{28,16},{1,13},{... | collective-permute-start | bytes 196616 | tf_op jit(solution)/shard_map/ppermute | solution.py:188
  22.6 1.2 %shard_map.95.rest_1_ = f32[128,1024]{1,0:T(8,128)S(1)} custom-call(bf16[1024,3072]{1,0:T(8,128)(2,1)S(1)} %bitcast.2, bf16[128,768]{1,0:T(8,128)(2,1)S(1)} %copy-done.3, bf16[128,768]{1,0:T(8,128)(2,1)S(1)} %collective-permute-done.2.rest_1_), custom_call_target="tpu_custom_call" | custom-call | flops 2400000000 | bytes 8000000 | tf_op jit(solution)/shard_map/pallas_call | solution.py:27
  23.8 0.7 %shard_map.96.rest_1_ = f32[128,1024]{1,0:T(8,128)S(1)} custom-call(bf16[1024,3072]{1,0:T(8,128)(2,1)S(1)} %bitcast.2, bf16[128,768]{1,0:T(8,128)(2,1)S(1)} %collective-permute-done.rest_0_, f32[128,1024]{1,0:T(8,128)S(1)} %shard_map.95.rest_1_), custom_call_target="tpu_custom_call" | custom-call | flops 2400000000 | bytes 8000000 | tf_op jit(solution)/shard_map/pallas_call | solution.py:27
  24.8 0.9 %shard_map.97 = (bf16[128,1024]{1,0:T(8,128)(2,1)S(1)}, bf16[128,1024]{1,0:T(8,128)(2,1)S(1)}, f32[272,128]{1,0:T(8,128)S(1)}, bf16[272,128]{1,0:T(8,128)(2,1)S(...) custom-call(bf16[1024,3072]{1,0:T(8,128)(2,1)S(1)} %bitcast.2, ...), custom_call_target="tpu_custom_call" | custom-call | flops 2400000000 | bytes 8000000 | tf_op jit(solution)/shard_map/pallas_call | solution.py:27
  25.8 1.2 %collective-permute-start.4 = (bf16[272,128]{1,0:T(8,128)(2,1)S(1)}, bf16[272,128]{1,0:T(8,128)(2,1)S(1)}, u32[]{:S(2)}, u32[]{:S(2)}) collective-permute-start(bf16[272,128]{1,0:T(8,128)(2,1)S(1)} %get-tuple-element.62), channel_id=1, source_target_pairs={{0,8},{4,12},{8,0},{12,4},{16,24},{20,28},{24,16},{28,20},{1,9},{5... | collective-permute-start | bytes 208904 | tf_op jit(solution)/shard_map/ppermute | solution.py:188
  27.1 1.0 %shard_map.98 = (bf16[1024,128]{1,0:T(8,128)(2,1)S(1)}, bf16[1024,128]{1,0:T(8,128)(2,1)S(1)}, f32[128,1024]{1,0:T(8,128)S(1)}) custom-call(f32[128,8]{1,0:T(8,128)S(1)} %get-tuple-element.52.rest_2_.cum_ref, f32[8,128]{1,0:T(8,128)S(1)} %get-tuple-element.54.cum_t_ref, bf16[128,1024]{1,0:T(8,128)(2,1)S(1)} %copy-done.2, bf16[128,1024]{1,0:T(8,128)(2,1)S(1)} %copy-done, ...), custom_call_target="tpu_custom_call" | custom-call | flops 2400000000 | bytes 8000000 | tf_op jit(solution)/shard_map/pallas_call | solution.py:27
  28.0 2.2 %collective-permute-start.5 = (bf16[272,128]{1,0:T(8,128)(2,1)S(1)}, bf16[272,128]{1,0:T(8,128)(2,1)S(1)}, u32[]{:S(2)}, u32[]{:S(2)}) collective-permute-start(bf16[272,128]{1,0:T(8,128)(2,1)S(1)} %get-tuple-element.63), channel_id=1, source_target_pairs={{0,12},{4,8},{8,4},{12,0},{16,28},{20,24},{24,20},{28,16},{1,13},{... | collective-permute-start | bytes 208904 | tf_op jit(solution)/shard_map/ppermute | solution.py:188
  30.3 0.6 %shard_map.107 = (bf16[128,1024]{1,0:T(8,128)(2,1)S(1)}, bf16[128,768]{1,0:T(8,128)(2,1)S(1)}) custom-call(bf16[1024,3072]{1,0:T(8,128)(2,1)S(1)} %bitcast.2, f32[128,1024]{1,0:T(8,128)S(1)} %get-tuple-element.72.local_ref, bf16[128,1024]{1,0:T(8,128)(2,1)S(1)} %get-tuple-element.73.rise_ref, bf16[256,128]{1,0:T(8,128)(2,1)S(1)} %get-tuple-element.80.rest_0_, ...), custom_call_target="tpu_custom_call" | custom-call | flops 2400000000 | bytes 8000000 | tf_op jit(solution)/shard_map/pallas_call | solution.py:27
  30.8 0.4 shard_map.109
  31.3 0.6 %shard_map.99 = (f32[128,1024]{1,0:T(8,128)S(1)}, f32[128,1024]{1,0:T(8,128)S(1)}, f32[128,1024]{1,0:T(8,128)S(1)}, bf16[128,1024]{1,0:T(8,128)(2,1)S(1)}, bf16[128,1024]{1,0:T(8,128)(2,1)S(1)}) custom-call(f32[128,8]{1,0:T(8,128)S(1)} %get-tuple-element.50.rest_3_.rise_ref, f32[128,8]{1,0:T(8,128)S(1)} %get-tuple-element.51.fall_ref, ...), custom_call_target="tpu_custom_call" | custom-call | flops 2400000000 | bytes 8000000 | tf_op jit(solution)/shard_map/pallas_call | solution.py:27
  31.9 1.4 %collective-permute-done.5.rest_3_ = bf16[272,128]{1,0:T(8,128)(2,1)S(1)} collective-permute-done((bf16[272,128]{1,0:T(8,128)(2,1)S(1)}, bf16[272,128]{1,0:T(8,128)(2,1)S(1)}, u32[]{:S(2)}, u32[]{:S(2)}) %collective-permute-start.5) | collective-permute-done | bytes 69664 | tf_op jit(solution)/shard_map/ppermute | solution.py:188
  33.4 3.3 %collective-permute-start.6 = (bf16[272,128]{1,0:T(8,128)(2,1)S(1)}, bf16[272,128]{1,0:T(8,128)(2,1)S(1)}, u32[]{:S(2)}, u32[]{:S(2)}) collective-permute-start(bf16[272,128]{1,0:T(8,128)(2,1)S(1)} %get-tuple-element.64), channel_id=1, source_target_pairs={{0,16},{4,20},{8,24},{12,28},{16,0},{20,4},{24,8},{28,12},{1,17},{... | collective-permute-start | bytes 208904 | tf_op jit(solution)/shard_map/ppermute | solution.py:207
  36.7 1.0 %shard_map.108 = (bf16[128,1024]{1,0:T(8,128)(2,1)}, bf16[128,768]{1,0:T(8,128)(2,1)S(1)}, f32[128,768]{1,0:T(8,128)S(1)}) custom-call(bf16[1024,3072]{1,0:T(8,128)(2,1)S(1)} %bitcast.2, bf16[128,1024]{1,0:T(8,128)(2,1)S(1)} %get-tuple-element.84.flat_ref, f32[128,1024]{1,0:T(8,128)S(1)} %get-tuple-element.85.lq_ref, ...), custom_call_target="tpu_custom_call" | custom-call | flops 2400000000 | bytes 8000000 | tf_op jit(solution)/shard_map/pallas_call | solution.py:27
  37.9 1.8 %collective-permute-done.6.entry_ref = bf16[272,128]{1,0:T(8,128)(2,1)S(1)} collective-permute-done((bf16[272,128]{1,0:T(8,128)(2,1)S(1)}, bf16[272,128]{1,0:T(8,128)(2,1)S(1)}, u32[]{:S(2)}, u32[]{:S(2)}) %collective-permute-start.6) | collective-permute-done | bytes 69664 | tf_op jit(solution)/shard_map/ppermute | solution.py:207
  39.8 1.7 %collective-permute-start.8 = (bf16[256,128]{1,0:T(8,128)(2,1)S(1)}, bf16[256,128]{1,0:T(8,128)(2,1)S(1)}, u32[]{:S(2)}, u32[]{:S(2)}) collective-permute-start(bf16[256,128]{1,0:T(8,128)(2,1)S(1)} %get-tuple-element.68), channel_id=1, source_target_pairs={{0,8},{4,12},{8,0},{12,4},{16,24},{20,28},{24,16},{28,20},{1,9},{5... | collective-permute-start | bytes 196616 | tf_op jit(solution)/shard_map/ppermute | solution.py:188
  41.6 1.7 %collective-permute-start.9 = (bf16[256,128]{1,0:T(8,128)(2,1)S(1)}, bf16[256,128]{1,0:T(8,128)(2,1)S(1)}, u32[]{:S(2)}, u32[]{:S(2)}) collective-permute-start(bf16[256,128]{1,0:T(8,128)(2,1)S(1)} %get-tuple-element.69), channel_id=1, source_target_pairs={{0,12},{4,8},{8,4},{12,0},{16,28},{20,24},{24,20},{28,16},{1,13},{... | collective-permute-start | bytes 196616 | tf_op jit(solution)/shard_map/ppermute | solution.py:188
  43.4 0.8 %collective-permute-start.19 = (bf16[128,768]{1,0:T(8,128)(2,1)S(1)}, bf16[128,768]{1,0:T(8,128)(2,1)S(1)}, u32[]{:S(2)}, u32[]{:S(2)}) collective-permute-start(bf16[128,768]{1,0:T(8,128)(2,1)S(1)} %add_convert_fusion), channel_id=1, source_target_pairs={{0,2},{1,3},{2,0},{3,1},{4,6},{5,7},{6,4},{7,5},{8,10},{9,11},{10,... | collective-permute-start | bytes 589832 | tf_op jit(solution)/shard_map/ppermute | solution.py:188
  44.2 2.6 %collective-permute-done.9.refs_6_ = bf16[256,128]{1,0:T(8,128)(2,1)S(1)} collective-permute-done((bf16[256,128]{1,0:T(8,128)(2,1)S(1)}, bf16[256,128]{1,0:T(8,128)(2,1)S(1)}, u32[]{:S(2)}, u32[]{:S(2)}) %collective-permute-start.9) | collective-permute-done | bytes 65568 | tf_op jit(solution)/shard_map/ppermute | solution.py:188
  46.7 0.3 shard_map.103
  47.1 2.0 %collective-permute-done.19.refs_5_ = bf16[128,768]{1,0:T(8,128)(2,1)S(1)} collective-permute-done((bf16[128,768]{1,0:T(8,128)(2,1)S(1)}, bf16[128,768]{1,0:T(8,128)(2,1)S(1)}, u32[]{:S(2)}, u32[]{:S(2)}) %collective-permute-start.19) | collective-permute-done | bytes 196640 | tf_op jit(solution)/shard_map/ppermute | solution.py:188
  49.1 1.0 %shard_map.110 = (bf16[128,768]{1,0:T(8,128)(2,1)}, bf16[128,1024]{1,0:T(8,128)(2,1)}, bf16[128,1024]{1,0:T(8,128)(2,1)}) custom-call(bf16[128,1024]{1,0:T(8,128)(2,1)S(1)} %get-tuple-element.49.refs_0_.k_fall_ref, bf16[128,1024]{1,0:T(8,128)(2,1)S(1)} %get-tuple-element.57.refs_1_.v_fall_ref, f32[128,1024]{1,0:T(8,128)S(1)} %get-tuple-element.58.refs_2_.lk_ref, ...), custom_call_target="tpu_custom_call" | custom-call | flops 2400000000 | bytes 8000000 | tf_op jit(solution)/shard_map/pallas_call | solution.py:27
  (42 shorter events, 1.2 us)
Async XLA Ops:
  0.6 3.1 %copy-start.1 = (bf16[128,1024]{1,0:T(8,128)(2,1)S(1)}, bf16[128,1024]{1,0:T(8,128)(2,1)}, u32[]{:S(2)}) copy-start(bf16[128,1024]{1,0:T(8,128)(2,1)} %v_ref.5) | copy-start | bytes 786436
  0.6 3.1 %copy-start = (bf16[128,1024]{1,0:T(8,128)(2,1)S(1)}, bf16[128,1024]{1,0:T(8,128)(2,1)}, u32[]{:S(2)}) copy-start(bf16[128,1024]{1,0:T(8,128)(2,1)} %k_ref.5) | copy-start | bytes 786436
  0.7 3.1 %copy-start.4 = (s32[128,8]{0,1:T(8,128)S(1)}, s32[128,8]{0,1:T(8,128)}, u32[]{:S(2)}) copy-start(s32[128,8]{0,1:T(8,128)} %param.9) | copy-start | bytes 12292
  0.7 21.9 %collective-permute-start = (bf16[128,768]{1,0:T(8,128)(2,1)}, bf16[128,768]{1,0:T(8,128)(2,1)S(1)}, u32[]{:S(2)}, u32[]{:S(2)}) collective-permute-start(bf16[128,768]{1,0:T(8,128)(2,1)} %rest_0_.1), channel_id=1, source_target_pairs={{0,2},{1,3},{2,0},{3,1},{4,6},{5,7},{6,4},{7,5},{8,10},{9,11},{10,... | collective-permute-start | bytes 589832 | tf_op jit(solution)/shard_map/ppermute | solution.py:188
  3.7 18.9 %collective-permute-start.2 = (bf16[128,768]{1,0:T(8,128)(2,1)}, bf16[128,768]{1,0:T(8,128)(2,1)S(1)}, u32[]{:S(2)}, u32[]{:S(2)}) collective-permute-start(bf16[128,768]{1,0:T(8,128)(2,1)} %rest_0_.1), channel_id=1, source_target_pairs={{0,1},{1,0},{2,3},{3,2},{4,5},{5,4},{6,7},{7,6},{8,9},{9,8},{10,11... | collective-permute-start | bytes 589832 | tf_op jit(solution)/shard_map/ppermute | solution.py:188
  4.5 4.7 %collective-permute-start.10 = (bf16[272,128]{1,0:T(8,128)(2,1)S(1)}, bf16[272,128]{1,0:T(8,128)(2,1)S(1)}, u32[]{:S(2)}, u32[]{:S(2)}) collective-permute-start(bf16[272,128]{1,0:T(8,128)(2,1)S(1)} %get-tuple-element.75), channel_id=1, source_target_pairs={{0,4},{4,0},{8,12},{12,8},{16,20},{20,16},{24,28},{28,24},{1,5},{5... | collective-permute-start | bytes 208904 | tf_op jit(solution)/shard_map/ppermute | solution.py:188
  6.0 4.5 %collective-permute-start.11 = (bf16[272,128]{1,0:T(8,128)(2,1)S(1)}, bf16[272,128]{1,0:T(8,128)(2,1)S(1)}, u32[]{:S(2)}, u32[]{:S(2)}) collective-permute-start(bf16[272,128]{1,0:T(8,128)(2,1)S(1)} %get-tuple-element.76), channel_id=1, source_target_pairs={{0,8},{4,12},{8,0},{12,4},{16,24},{20,28},{24,16},{28,20},{1,9},{5... | collective-permute-start | bytes 208904 | tf_op jit(solution)/shard_map/ppermute | solution.py:188
  7.6 5.2 %collective-permute-start.12 = (bf16[272,128]{1,0:T(8,128)(2,1)S(1)}, bf16[272,128]{1,0:T(8,128)(2,1)S(1)}, u32[]{:S(2)}, u32[]{:S(2)}) collective-permute-start(bf16[272,128]{1,0:T(8,128)(2,1)S(1)} %get-tuple-element.77), channel_id=1, source_target_pairs={{0,12},{4,8},{8,4},{12,0},{16,28},{20,24},{24,20},{28,16},{1,13},{... | collective-permute-start | bytes 208904 | tf_op jit(solution)/shard_map/ppermute | solution.py:188
  12.9 6.0 %collective-permute-start.13 = (bf16[272,128]{1,0:T(8,128)(2,1)S(1)}, bf16[272,128]{1,0:T(8,128)(2,1)S(1)}, u32[]{:S(2)}, u32[]{:S(2)}) collective-permute-start(bf16[272,128]{1,0:T(8,128)(2,1)S(1)} %get-tuple-element.78), channel_id=1, source_target_pairs={{0,16},{4,20},{8,24},{12,28},{16,0},{20,4},{24,8},{28,12},{1,17},{... | collective-permute-start | bytes 208904 | tf_op jit(solution)/shard_map/ppermute | solution.py:207
  15.6 7.0 %slice-start = ((s8[6291456]{0:T(1024)(128)(4,1)}), s8[4194304]{0:T(1024)(128)(4,1)S(1)}, s32[]{:S(2)}) async-start(s8[6291456]{0:T(1024)(128)(4,1)} %bitcast.1), calls=%async_computation | async-start | bytes 8388608
  15.6 7.0 %copy-start.3 = (bf16[128,768]{1,0:T(8,128)(2,1)S(1)}, bf16[128,768]{1,0:T(8,128)(2,1)}, u32[]{:S(2)}) copy-start(bf16[128,768]{1,0:T(8,128)(2,1)} %rest_0_.1) | copy-start | bytes 589828
  18.9 3.7 %slice-start.1 = ((s8[6291456]{0:T(1024)(128)(4,1)}), s8[2097152]{0:T(1024)(128)(4,1)S(1)}, s32[]{:S(2)}) async-start(s8[6291456]{0:T(1024)(128)(4,1)} %bitcast.1), calls=%async_computation.1 | async-start | bytes 4194304
  19.0 9.0 %collective-permute-start.14 = (bf16[256,128]{1,0:T(8,128)(2,1)S(1)}, bf16[256,128]{1,0:T(8,128)(2,1)S(1)}, u32[]{:S(2)}, u32[]{:S(2)}) collective-permute-start(bf16[256,128]{1,0:T(8,128)(2,1)S(1)} %get-tuple-element.81), channel_id=1, source_target_pairs={{0,4},{4,0},{8,12},{12,8},{16,20},{20,16},{24,28},{28,24},{1,5},{5... | collective-permute-start | bytes 196616 | tf_op jit(solution)/shard_map/ppermute | solution.py:188
  19.1 11.1 %collective-permute-start.15 = (bf16[256,128]{1,0:T(8,128)(2,1)S(1)}, bf16[256,128]{1,0:T(8,128)(2,1)S(1)}, u32[]{:S(2)}, u32[]{:S(2)}) collective-permute-start(bf16[256,128]{1,0:T(8,128)(2,1)S(1)} %get-tuple-element.82), channel_id=1, source_target_pairs={{0,8},{4,12},{8,0},{12,4},{16,24},{20,28},{24,16},{28,20},{1,9},{5... | collective-permute-start | bytes 196616 | tf_op jit(solution)/shard_map/ppermute | solution.py:188
  20.4 9.8 %collective-permute-start.16 = (bf16[256,128]{1,0:T(8,128)(2,1)S(1)}, bf16[256,128]{1,0:T(8,128)(2,1)S(1)}, u32[]{:S(2)}, u32[]{:S(2)}) collective-permute-start(bf16[256,128]{1,0:T(8,128)(2,1)S(1)} %get-tuple-element.83), channel_id=1, source_target_pairs={{0,12},{4,8},{8,4},{12,0},{16,28},{20,24},{24,20},{28,16},{1,13},{... | collective-permute-start | bytes 196616 | tf_op jit(solution)/shard_map/ppermute | solution.py:188
  22.6 1.9 %collective-permute-start.1 = (bf16[128,768]{1,0:T(8,128)(2,1)S(1)}, bf16[128,768]{1,0:T(8,128)(2,1)S(1)}, u32[]{:S(2)}, u32[]{:S(2)}) collective-permute-start(bf16[128,768]{1,0:T(8,128)(2,1)S(1)} %collective-permute-done.rest_0_), channel_id=1, source_target_pairs={{0,1},{1,0},{2,3},{3,2},{4,5},{5,4},{6,7},{7,6},{8,9},{9,8},{10,11... | collective-permute-start | bytes 589832 | tf_op jit(solution)/shard_map/ppermute | solution.py:188
  23.8 1.0 %copy-start.2 = (bf16[128,1024]{1,0:T(8,128)(2,1)S(1)}, bf16[128,1024]{1,0:T(8,128)(2,1)}, u32[]{:S(2)}) copy-start(bf16[128,1024]{1,0:T(8,128)(2,1)} %q_ref.3) | copy-start | bytes 786436
  25.7 6.3 %collective-permute-start.3 = (bf16[272,128]{1,0:T(8,128)(2,1)S(1)}, bf16[272,128]{1,0:T(8,128)(2,1)S(1)}, u32[]{:S(2)}, u32[]{:S(2)}) collective-permute-start(bf16[272,128]{1,0:T(8,128)(2,1)S(1)} %get-tuple-element.61), channel_id=1, source_target_pairs={{0,4},{4,0},{8,12},{12,8},{16,20},{20,16},{24,28},{28,24},{1,5},{5... | collective-permute-start | bytes 208904 | tf_op jit(solution)/shard_map/ppermute | solution.py:188
  25.8 6.1 %collective-permute-start.4 = (bf16[272,128]{1,0:T(8,128)(2,1)S(1)}, bf16[272,128]{1,0:T(8,128)(2,1)S(1)}, u32[]{:S(2)}, u32[]{:S(2)}) collective-permute-start(bf16[272,128]{1,0:T(8,128)(2,1)S(1)} %get-tuple-element.62), channel_id=1, source_target_pairs={{0,8},{4,12},{8,0},{12,4},{16,24},{20,28},{24,16},{28,20},{1,9},{5... | collective-permute-start | bytes 208904 | tf_op jit(solution)/shard_map/ppermute | solution.py:188
  28.0 5.3 %collective-permute-start.5 = (bf16[272,128]{1,0:T(8,128)(2,1)S(1)}, bf16[272,128]{1,0:T(8,128)(2,1)S(1)}, u32[]{:S(2)}, u32[]{:S(2)}) collective-permute-start(bf16[272,128]{1,0:T(8,128)(2,1)S(1)} %get-tuple-element.63), channel_id=1, source_target_pairs={{0,12},{4,8},{8,4},{12,0},{16,28},{20,24},{24,20},{28,16},{1,13},{... | collective-permute-start | bytes 208904 | tf_op jit(solution)/shard_map/ppermute | solution.py:188
  31.2 12.1 %collective-permute-start.18 = (bf16[128,768]{1,0:T(8,128)(2,1)S(1)}, bf16[128,768]{1,0:T(8,128)(2,1)S(1)}, u32[]{:S(2)}, u32[]{:S(2)}) collective-permute-start(bf16[128,768]{1,0:T(8,128)(2,1)S(1)} %get-tuple-element.89), channel_id=1, source_target_pairs={{0,1},{1,0},{2,3},{3,2},{4,5},{5,4},{6,7},{7,6},{8,9},{9,8},{10,11... | collective-permute-start | bytes 589832 | tf_op jit(solution)/shard_map/ppermute | solution.py:188
  33.4 6.2 %collective-permute-start.6 = (bf16[272,128]{1,0:T(8,128)(2,1)S(1)}, bf16[272,128]{1,0:T(8,128)(2,1)S(1)}, u32[]{:S(2)}, u32[]{:S(2)}) collective-permute-start(bf16[272,128]{1,0:T(8,128)(2,1)S(1)} %get-tuple-element.64), channel_id=1, source_target_pairs={{0,16},{4,20},{8,24},{12,28},{16,0},{20,4},{24,8},{28,12},{1,17},{... | collective-permute-start | bytes 208904 | tf_op jit(solution)/shard_map/ppermute | solution.py:207
  37.8 9.2 %collective-permute-start.17 = (bf16[128,768]{1,0:T(8,128)(2,1)S(1)}, bf16[128,768]{1,0:T(8,128)(2,1)S(1)}, u32[]{:S(2)}, u32[]{:S(2)}) collective-permute-start(bf16[128,768]{1,0:T(8,128)(2,1)S(1)} %get-tuple-element.88), channel_id=1, source_target_pairs={{0,1},{1,0},{2,3},{3,2},{4,5},{5,4},{6,7},{7,6},{8,9},{9,8},{10,11... | collective-permute-start | bytes 589832 | tf_op jit(solution)/shard_map/ppermute | solution.py:188
  39.8 7.3 %collective-permute-start.7 = (bf16[256,128]{1,0:T(8,128)(2,1)S(1)}, bf16[256,128]{1,0:T(8,128)(2,1)S(1)}, u32[]{:S(2)}, u32[]{:S(2)}) collective-permute-start(bf16[256,128]{1,0:T(8,128)(2,1)S(1)} %get-tuple-element.66), channel_id=1, source_target_pairs={{0,4},{4,0},{8,12},{12,8},{16,20},{20,16},{24,28},{28,24},{1,5},{5... | collective-permute-start | bytes 196616 | tf_op jit(solution)/shard_map/ppermute | solution.py:188
  39.8 4.3 %collective-permute-start.8 = (bf16[256,128]{1,0:T(8,128)(2,1)S(1)}, bf16[256,128]{1,0:T(8,128)(2,1)S(1)}, u32[]{:S(2)}, u32[]{:S(2)}) collective-permute-start(bf16[256,128]{1,0:T(8,128)(2,1)S(1)} %get-tuple-element.68), channel_id=1, source_target_pairs={{0,8},{4,12},{8,0},{12,4},{16,24},{20,28},{24,16},{28,20},{1,9},{5... | collective-permute-start | bytes 196616 | tf_op jit(solution)/shard_map/ppermute | solution.py:188
  41.6 5.2 %collective-permute-start.9 = (bf16[256,128]{1,0:T(8,128)(2,1)S(1)}, bf16[256,128]{1,0:T(8,128)(2,1)S(1)}, u32[]{:S(2)}, u32[]{:S(2)}) collective-permute-start(bf16[256,128]{1,0:T(8,128)(2,1)S(1)} %get-tuple-element.69), channel_id=1, source_target_pairs={{0,12},{4,8},{8,4},{12,0},{16,28},{20,24},{24,20},{28,16},{1,13},{... | collective-permute-start | bytes 196616 | tf_op jit(solution)/shard_map/ppermute | solution.py:188
  43.4 5.7 %collective-permute-start.19 = (bf16[128,768]{1,0:T(8,128)(2,1)S(1)}, bf16[128,768]{1,0:T(8,128)(2,1)S(1)}, u32[]{:S(2)}, u32[]{:S(2)}) collective-permute-start(bf16[128,768]{1,0:T(8,128)(2,1)S(1)} %add_convert_fusion), channel_id=1, source_target_pairs={{0,2},{1,3},{2,0},{3,1},{4,6},{5,7},{6,4},{7,5},{8,10},{9,11},{10,... | collective-permute-start | bytes 589832 | tf_op jit(solution)/shard_map/ppermute | solution.py:188
